TPU v7x, 32 devices: a whole 2x2x4 slice. The times are simulated.
32 devices in a mesh: dp: 8 (over z, x), tensor: 4 (over y, core).
Axes of the slice: x: 2, y: 2, z: 4, core: 2. Of those that a mesh axis runs over, the one named last changes fastest.
Arguments:
- inputs: bfloat16 [8, 64, 64, 1280], P('dp', 'tensor'), may hold values from -6 to 6
- cotangent: bfloat16 [8, 64, 64, 1280], P('dp', 'tensor'), may hold values from -6 to 6
- teacher: bfloat16 [8, 64, 64, 1280], P('dp', 'tensor'), may hold values from -6 to 6
- qkv_weight: bfloat16 [3, 1280, 1280], P(None, 'dp', 'tensor'), may hold values from -0.15625 to 0.15625
- proj_weight: bfloat16 [1280, 1280], P('tensor', 'dp'), may hold values from -1 to 1
- up_weight: bfloat16 [1280, 5120], P('dp', 'tensor'), may hold values from -0.15625 to 0.15625
- down_weight: bfloat16 [5120, 1280], P('tensor', 'dp'), may hold values from -0.078125 to 0.078125
- qv_bias: bfloat16 [2, 1280], P(None, 'tensor'), may hold values from -3 to 3
- up_bias: bfloat16 [5120], P('tensor'), may hold values from -3 to 3
- norm_gains: bfloat16 [2, 1280], replicated, may hold values from 0.5 to 1.5
- norm_shifts: bfloat16 [2, 1280], replicated, may hold values from -3 to 3
- out_biases: bfloat16 [2, 1280], replicated, may hold values from -3 to 3
- rel_tables: bfloat16 [2, 27, 80], replicated, may hold values from -0.625 to 0.625
Outputs:
- output: bfloat16 [8, 64, 64, 1280], P('dp', 'tensor')
- input_grad: float32 [8, 64, 64, 1280], P('dp', 'tensor')
- loss: float32 [], replicated
- qkv_weight_grad: float32 [3, 1280, 1280], P(None, 'dp', 'tensor')
- proj_weight_grad: float32 [1280, 1280], P('tensor', 'dp')
- up_weight_grad: float32 [1280, 5120], P('dp', 'tensor')
- down_weight_grad: float32 [5120, 1280], P('tensor', 'dp')
- qv_bias_grad: float32 [2, 1280], P(None, 'tensor')
- up_bias_grad: float32 [5120], P('tensor')
- norm_gains_grad: float32 [2, 1280], replicated
- norm_shifts_grad: float32 [2, 1280], replicated
- out_biases_grad: float32 [2, 1280], replicated
- rel_tables_grad: float32 [2, 27, 80], replicated
All inputs are finite; a program needn't handle non-finite values.
Results may differ from a plain program's by a relative error of at most 0.013.
Values may be sent and summed in bfloat16 or wider, within the bound.
A program may use at most 256 MiB of HBM per device.

v0:
```python
from functools import partial

import jax
import jax.numpy as jnp
from jax import lax
from jax.sharding import PartitionSpec as P

D = 1280
HEAD_DIM = 80
GRID = 64
WIN = 14
PGRID = 70
NWIN = 5


highest = lax.Precision.HIGHEST


def layer_norm(values, gain_vector, shift_vector):
    average = jnp.mean(values, axis=-1, keepdims=True)
    centred = values - average
    variance = jnp.mean(centred * centred, axis=-1, keepdims=True)
    return centred * lax.rsqrt(variance + 1e-06) * gain_vector + shift_vector


def exact_gelu(values):
    return jax.nn.gelu(values, approximate=False)


def offset_tables(window):
    position = jnp.arange(window * window)
    across = jnp.arange(window)
    ranks = jnp.arange(2 * window - 1)
    high_sel = (
        position[:, None, None] // window - across[None, :, None] + window - 1
        == ranks[None, None, :]
    ).astype(jnp.float32)
    wide_sel = (
        position[:, None, None] % window - across[None, :, None] + window - 1
        == ranks[None, None, :]
    ).astype(jnp.float32)
    return (high_sel, wide_sel)


def to_windows(grid_values):
    extra = PGRID - GRID
    padded = jnp.pad(grid_values, ((0, extra), (0, extra), (0, 0)))
    channels = grid_values.shape[-1]
    shaped = padded.reshape(NWIN, WIN, NWIN, WIN, channels).transpose(0, 2, 1, 3, 4)
    return shaped.reshape(NWIN, NWIN, WIN * WIN, channels)


def from_windows(windowed):
    channels = windowed.shape[-1]
    shaped = windowed.reshape(NWIN, NWIN, WIN, WIN, channels).transpose(0, 2, 1, 3, 4)
    return shaped.reshape(PGRID, PGRID, channels)[:GRID, :GRID]


def score_block(queries, key_rows, tables, selectors):
    table_high, table_wide = tables
    high_sel, wide_sel = selectors
    raw = jnp.einsum(
        "wqhc,wkhc->whqk", queries, key_rows, preferred_element_type=jnp.float32
    ) * HEAD_DIM ** (-0.5)
    along_high = jnp.einsum(
        "wqhc,rc->wqhr", queries, table_high, preferred_element_type=jnp.float32
    )
    along_wide = jnp.einsum(
        "wqhc,rc->wqhr", queries, table_wide, preferred_element_type=jnp.float32
    )
    bias_high = jnp.einsum("wqhr,qkr->whqk", along_high, high_sel, precision=highest)
    bias_wide = jnp.einsum("wqhr,qkr->whqk", along_wide, wide_sel, precision=highest)
    shaped = (
        raw.reshape(raw.shape[:3] + (WIN, WIN)) + bias_high[..., :, None] + bias_wide[..., None, :]
    )
    return shaped.reshape(raw.shape)


def attend_row(block_parts, tables, selectors):
    queries, key_rows, value_rows = block_parts
    scores = score_block(queries, key_rows, tables, selectors)
    row_max = jnp.max(scores, axis=-1, keepdims=True)
    shifted = jnp.exp(scores - row_max)
    row_total = jnp.sum(shifted, axis=-1, keepdims=True)
    probs_low = (shifted / row_total).astype(jnp.bfloat16)
    attended = jnp.einsum(
        "whqk,wkhc->wqhc", probs_low, value_rows, preferred_element_type=jnp.float32
    )
    return (attended.astype(jnp.bfloat16), (row_max + jnp.log(row_total))[..., 0])


def attend_back(block_parts, tables, selectors):
    queries, key_rows, value_rows, attended_grad, log_total = block_parts
    high_sel, wide_sel = selectors
    scores = score_block(queries, key_rows, tables, selectors)
    probs = jnp.exp(scores - log_total[..., None])
    probs_grad = jnp.einsum(
        "wqhc,wkhc->whqk", attended_grad, value_rows, preferred_element_type=jnp.float32
    )
    value_grad = jnp.einsum(
        "whqk,wqhc->wkhc",
        probs.astype(jnp.bfloat16),
        attended_grad,
        preferred_element_type=jnp.float32,
    )
    scores_grad = probs * (probs_grad - jnp.sum(probs * probs_grad, axis=-1, keepdims=True))
    scores_low = scores_grad.astype(jnp.bfloat16)
    query_grad = jnp.einsum(
        "whqk,wkhc->wqhc", scores_low, key_rows, preferred_element_type=jnp.float32
    ) * HEAD_DIM ** (-0.5)
    key_grad = jnp.einsum(
        "whqk,wqhc->wkhc", scores_low, queries, preferred_element_type=jnp.float32
    ) * HEAD_DIM ** (-0.5)
    shaped = scores_grad.reshape(scores_grad.shape[:3] + (WIN, WIN))
    rank_high = jnp.einsum("whqa,qar->wqhr", jnp.sum(shaped, axis=-1), high_sel, precision=highest)
    rank_wide = jnp.einsum("whqb,qbr->wqhr", jnp.sum(shaped, axis=-2), wide_sel, precision=highest)
    table_high = tables[0].astype(jnp.float32)
    table_wide = tables[1].astype(jnp.float32)
    query_grad = query_grad + jnp.einsum("wqhr,rc->wqhc", rank_high, table_high, precision=highest)
    query_grad = query_grad + jnp.einsum("wqhr,rc->wqhc", rank_wide, table_wide, precision=highest)
    query_wide = queries.astype(jnp.float32)
    table_grad = jnp.stack(
        [
            jnp.einsum("wqhr,wqhc->rc", rank_high, query_wide, precision=highest),
            jnp.einsum("wqhr,wqhc->rc", rank_wide, query_wide, precision=highest),
        ]
    )
    return (query_grad, key_grad, value_grad, table_grad)


def shards(
    inputs,
    cotangent,
    teacher,
    qkv_weight,
    proj_weight,
    up_weight,
    down_weight,
    qv_bias,
    up_bias,
    norm_gains,
    norm_shifts,
    out_biases,
    rel_tables,
):
    qkv_full, proj_full, up_full, down_full = (
        lax.all_gather(qkv_weight, "dp", axis=1, tiled=True),
        lax.all_gather(proj_weight, "dp", axis=1, tiled=True),
        lax.all_gather(up_weight, "dp", axis=0, tiled=True),
        lax.all_gather(down_weight, "dp", axis=1, tiled=True),
    )
    up_matrix, down_matrix, up_bias_all = (up_full, down_full, up_bias)
    images, row_count = (inputs.shape[0], inputs.shape[1])
    local_width = qkv_full.shape[2]
    head_count = local_width // HEAD_DIM
    head_shape = (NWIN, NWIN, WIN * WIN, head_count, HEAD_DIM)
    selectors = offset_tables(WIN)
    tables = (rel_tables[0], rel_tables[1])
    gains_wide = norm_gains.astype(jnp.float32)
    shifts_wide = norm_shifts.astype(jnp.float32)
    source = inputs[0].astype(jnp.float32)
    normed = layer_norm(source, gains_wide[0], shifts_wide[0]).astype(jnp.bfloat16)
    gathered = lax.all_gather(normed, "tensor", axis=0, tiled=True)
    windows = to_windows(gathered)
    projected = jnp.einsum("abpd,sdc->sabpc", windows, qkv_full, preferred_element_type=jnp.float32)
    queries = (projected[0] + qv_bias[0]).astype(jnp.bfloat16).reshape(head_shape)
    key_rows = projected[1].astype(jnp.bfloat16).reshape(head_shape)
    value_rows = (projected[2] + qv_bias[1]).astype(jnp.bfloat16).reshape(head_shape)
    attended, log_totals = lax.map(
        partial(attend_row, tables=tables, selectors=selectors), (queries, key_rows, value_rows)
    )
    grid_out = from_windows(attended.reshape(NWIN, NWIN, WIN * WIN, local_width))
    row_piece = grid_out
    attn_branch = lax.psum_scatter(
        jnp.einsum("xyc,cd->xyd", row_piece, proj_full, preferred_element_type=jnp.float32).astype(
            jnp.bfloat16
        ),
        "tensor",
        scatter_dimension=0,
        tiled=True,
    ).astype(jnp.float32)
    middle = source + attn_branch + out_biases[0].astype(jnp.float32)
    normed_two = layer_norm(middle, gains_wide[1], shifts_wide[1]).astype(jnp.bfloat16)
    mlp_input = lax.all_gather(normed_two, "tensor", axis=0, tiled=True)
    hidden = (
        jnp.einsum("xyd,dm->xym", mlp_input, up_matrix, preferred_element_type=jnp.float32)
        + up_bias_all
    )
    active = exact_gelu(hidden).astype(jnp.bfloat16)
    row_piece = active
    mlp_branch = lax.psum_scatter(
        jnp.einsum(
            "xym,md->xyd", row_piece, down_matrix, preferred_element_type=jnp.float32
        ).astype(jnp.bfloat16),
        "tensor",
        scatter_dimension=0,
        tiled=True,
    ).astype(jnp.float32)
    result = middle + mlp_branch + out_biases[1].astype(jnp.float32)
    mismatch = result - teacher[0].astype(jnp.float32)
    loss_total = jnp.sum(mismatch * mismatch)
    outputs = [result.astype(jnp.bfloat16)]
    result_grad = cotangent[0].astype(jnp.float32) + mismatch
    result_low = result_grad.astype(jnp.bfloat16)
    grad_rows = lax.all_gather(result_low, "tensor", axis=0, tiled=True)
    down_acc = jnp.einsum("xym,xyd->md", active, grad_rows, preferred_element_type=jnp.float32)
    active_grad = jnp.einsum(
        "xyd,md->xym", grad_rows, down_matrix, preferred_element_type=jnp.float32
    )
    gelu_value, gelu_back = jax.vjp(exact_gelu, hidden)
    hidden_grad = gelu_back(active_grad)[0]
    up_bias_acc = jnp.sum(hidden_grad, axis=(0, 1))
    hidden_low = hidden_grad.astype(jnp.bfloat16)
    up_acc = jnp.einsum("xyd,xym->dm", mlp_input, hidden_low, preferred_element_type=jnp.float32)
    row_piece = hidden_low
    second_grad = lax.psum_scatter(
        jnp.einsum("xym,dm->xyd", row_piece, up_matrix, preferred_element_type=jnp.float32).astype(
            jnp.bfloat16
        ),
        "tensor",
        scatter_dimension=0,
        tiled=True,
    ).astype(jnp.float32)
    second_value, second_back = jax.vjp(layer_norm, middle, gains_wide[1], shifts_wide[1])
    middle_part, second_gain, second_shift = second_back(second_grad)
    middle_grad = result_grad + middle_part
    out_bias_acc = jnp.stack([jnp.sum(middle_grad, axis=(0, 1)), jnp.sum(result_grad, axis=(0, 1))])
    middle_low = middle_grad.astype(jnp.bfloat16)
    gathered_grad = lax.all_gather(middle_low, "tensor", axis=0, tiled=True)
    proj_acc = jnp.einsum(
        "xyc,xyd->cd", grid_out, gathered_grad, preferred_element_type=jnp.float32
    )
    attended_grad = jnp.einsum(
        "xyd,cd->xyc", gathered_grad, proj_full, preferred_element_type=jnp.float32
    ).astype(jnp.bfloat16)
    grad_windows = to_windows(attended_grad).reshape(head_shape)
    query_grad, key_grad, value_grad, table_parts = lax.map(
        partial(attend_back, tables=tables, selectors=selectors),
        (queries, key_rows, value_rows, grad_windows, log_totals),
    )
    table_acc = jnp.sum(table_parts, axis=0)
    query_flat = query_grad.reshape(NWIN, NWIN, WIN * WIN, local_width)
    key_flat = key_grad.reshape(NWIN, NWIN, WIN * WIN, local_width)
    value_flat = value_grad.reshape(NWIN, NWIN, WIN * WIN, local_width)
    qv_acc = jnp.stack([jnp.sum(query_flat, axis=(0, 1, 2)), jnp.sum(value_flat, axis=(0, 1, 2))])
    stacked = jnp.stack([query_flat, key_flat, value_flat]).astype(jnp.bfloat16)
    qkv_acc = jnp.einsum("abpd,sabpc->sdc", windows, stacked, preferred_element_type=jnp.float32)
    normed_back = jnp.einsum(
        "sabpc,sdc->abpd", stacked, qkv_full, preferred_element_type=jnp.float32
    )
    first_grad = lax.psum_scatter(
        from_windows(normed_back).astype(jnp.bfloat16), "tensor", scatter_dimension=0, tiled=True
    ).astype(jnp.float32)
    first_value, first_back = jax.vjp(layer_norm, source, gains_wide[0], shifts_wide[0])
    source_part, first_gain, first_shift = first_back(first_grad)
    gain_acc = jnp.stack([first_gain, second_gain])
    shift_acc = jnp.stack([first_shift, second_shift])
    input_grads = [middle_grad + source_part]
    qkv_grad, proj_grad, up_grad, down_grad = (
        lax.psum_scatter(
            qkv_acc.astype(jnp.bfloat16), "dp", scatter_dimension=1, tiled=True
        ).astype(jnp.float32),
        lax.psum_scatter(
            proj_acc.astype(jnp.bfloat16), "dp", scatter_dimension=1, tiled=True
        ).astype(jnp.float32),
        lax.psum_scatter(up_acc.astype(jnp.bfloat16), "dp", scatter_dimension=0, tiled=True).astype(
            jnp.float32
        ),
        lax.psum_scatter(
            down_acc.astype(jnp.bfloat16), "dp", scatter_dimension=1, tiled=True
        ).astype(jnp.float32),
    )
    qv_grad, up_bias_grad = lax.psum((qv_acc, up_bias_acc), "dp")
    gains_grad, shifts_grad, out_grad, table_grad, loss_sum = lax.psum(
        (gain_acc, shift_acc, out_bias_acc, table_acc, loss_total), ("dp", "tensor")
    )
    element_count = images * row_count * GRID * D * lax.axis_size("dp") * lax.axis_size("tensor")
    loss = loss_sum / element_count
    return (
        jnp.stack(outputs),
        jnp.stack(input_grads),
        loss,
        qkv_grad,
        proj_grad,
        up_grad,
        down_grad,
        qv_grad,
        up_bias_grad,
        gains_grad,
        shifts_grad,
        out_grad,
        table_grad,
    )


def solution(mesh):
    in_specs = (
        P("dp", "tensor", None, None),
        P("dp", "tensor", None, None),
        P("dp", "tensor", None, None),
        P(None, "dp", "tensor"),
        P("tensor", "dp"),
        P("dp", "tensor"),
        P("tensor", "dp"),
        P(None, "tensor"),
        P("tensor"),
        P(),
        P(),
        P(),
        P(),
    )
    out_specs = (
        P("dp", "tensor", None, None),
        P("dp", "tensor", None, None),
        P(),
        P(None, "dp", "tensor"),
        P("tensor", "dp"),
        P("dp", "tensor"),
        P("tensor", "dp"),
        P(None, "tensor"),
        P("tensor"),
        P(),
        P(),
        P(),
        P(),
    )
    return jax.shard_map(shards, mesh=mesh, in_specs=in_specs, out_specs=out_specs, check_vma=False)
```

profile of v0, /device:TPU:0, one launch (start us, length us, event | category | flops | bytes accessed | tf_op | source)
XLA Modules:
  0.0 2018.4 jit_solution(13288147670114072156)
XLA Ops:
  18.5 36.7 %all_gather.26 = bf16[320,1280]{0,1:T(8,128)(2,1)} all-gather(bf16[320,160]{0,1:T(8,128)(2,1)S(1)} %copy-done.44), channel_id=1, replica_groups=mesh['dp'=8,'tensor'=4] {'dp'}, dimensions={1}, use_global_device_ids=true | all-gather | bytes 921600 | tf_op jit(solution)/shard_map/all_gather | solution.py:148
  55.2 34.5 %all-gather.8.cloned.1.call-done = bf16[64,64,1280]{2,1,0:T(8,128)(2,1)} async-done(((bf16[16,64,1280]{2,1,0:T(8,128)(2,1)}), bf16[64,64,1280]{2,1,0:T(8,128)(2,1)}) %all-gather.8.cloned.1.call-update) | async-done | bytes 10485776 | tf_op jit(solution)/shard_map/all_gather | solution.py:163
  89.7 10.2 pad.8
  99.9 18.6 reshape.295
  118.5 13.4 copy.189
  131.9 19.4 reshape.319
  151.3 24.5 %fusion.109 = f32[3,5,5,196,320]{4,3,0,2,1:T(8,128)} fusion(bf16[5,5,196,1280,1]{3,2,1,0,4:T(8,128)(2,1)} %reshape.319, bf16[3,1280,320]{2,1,0:T(8,128)(2,1)} %all-gather.10.cloned.1.call-done), kind=kOutput, calls=%fused_computation.142 | convolution fusion | flops 12042240000 | bytes 33817600 | tf_op jit(solution)/shard_map/abpd,sdc->sabpc/dot_general | solution.py:165
  175.8 11.8 fusion.165
  193.1 10.5 copy.116
  203.6 10.4 copy.117
  222.0 9.1 add_convert_fusion
  231.1 193.3 %while.31 = (s32[]{:T(128)}, bf16[5,5,196,4,80]{2,4,3,1,0:T(8,128)(2,1)}, f32[5,5,4,196]{3,2,1,0:T(4,128)}, bf16[5,5,196,4,80]{2,4,3,1,0:T(8,128)(2,1)}, bf16[5,...) while((s32[]{:T(128)}, ...), condition=%wide.region_5.6_spmd.clone, body=%wide.region_2.5_spmd.clone.sunk | while | flops 322814336 | bytes 44160668 | solution.py:169
  424.5 11.4 copy.121
  435.9 10.0 reshape_reshape.6
  458.1 10.6 convolution_convert_fusion.2
  470.1 84.2 %reduce-scatter.11.cloned.1.call-done = bf16[16,64,1280]{2,1,0:T(8,128)(2,1)} async-done(((bf16[64,64,1280]{2,1,0:T(8,128)(2,1)}), bf16[16,64,1280]{2,1,0:T(8,128)(2,1)}) %reduce-scatter.11.cloned.1.call-update) | async-done | bytes 2621456 | tf_op jit(solution)/shard_map/reduce_scatter | solution.py:174
  562.9 55.4 %all-gather.14.cloned.1.call-done = bf16[1280,1280]{1,0:T(8,128)(2,1)} async-done(((bf16[160,1280]{1,0:T(8,128)(2,1)}), bf16[1280,1280]{1,0:T(8,128)(2,1)}) %all-gather.14.cloned.1.call-update) | async-done | bytes 3276816 | tf_op jit(solution)/shard_map/all_gather | solution.py:149
  618.3 70.8 %all-gather.12.cloned.1.call-done = bf16[64,64,1280]{2,1,0:T(8,128)(2,1)} async-done(((bf16[16,64,1280]{2,1,0:T(8,128)(2,1)}), bf16[64,64,1280]{2,1,0:T(8,128)(2,1)}) %all-gather.12.cloned.1.call-update) | async-done | bytes 10485776 | tf_op jit(solution)/shard_map/all_gather | solution.py:184
  689.1 60.9 %multiply_convert_fusion = (bf16[64,64,1280]{2,1,0:T(8,128)(2,1)}, f32[64,64,1280]{2,1,0:T(8,128)}, f32[64,64,1280]{2,1,0:T(8,128)}) fusion(f32[1280]{0:T(1024)S(1)} %convert_element_type.209, bf16[64,64,1280]{2,1,0:T(8,128)(2,1)} %all-gather.12.cloned.1.call-done, bf16[1280,1280]{1,0:T(8,128)(2,1)} %all-gather.14.cloned.1.call-done), kind=kOutput, calls=%fused_computation.117 | convolution fusion | flops 13767802880 | bytes 66196480 | tf_op jit(solution)/shard_map/xyd,dm->xym/dot_general | solution.py:186
  753.2 20.1 convolution_convert_fusion.1
  773.4 84.0 %reduce-scatter.13.cloned.1.call-done = bf16[16,64,1280]{2,1,0:T(8,128)(2,1)} async-done(((bf16[64,64,1280]{2,1,0:T(8,128)(2,1)}), bf16[16,64,1280]{2,1,0:T(8,128)(2,1)}) %reduce-scatter.13.cloned.1.call-update) | async-done | bytes 2621456 | tf_op jit(solution)/shard_map/reduce_scatter | solution.py:191
  868.4 70.3 %all-gather.18.cloned.1.call-done = bf16[64,64,1280]{2,1,0:T(8,128)(2,1)} async-done(((bf16[16,64,1280]{2,1,0:T(8,128)(2,1)}), bf16[64,64,1280]{2,1,0:T(8,128)(2,1)}) %all-gather.18.cloned.1.call-update) | async-done | bytes 10485776 | tf_op jit(solution)/shard_map/all_gather | solution.py:205
  938.7 30.7 %fusion.169 = (f32[1280]{0:T(1024)}, bf16[64,64,1280]{2,1,0:T(8,128)(2,1)}) fusion(f32[64,64,1280]{2,1,0:T(8,128)} %get-tuple-element.416, f32[64,64,1280]{2,1,0:T(8,128)} %get-tuple-element.430, bf16[64,64,1280]{2,1,0:T(8,128)(2,1)} %all-gather.18.cloned.1.call-done, bf16[1280,1280]{0,1:T(8,128)(2,1)} %all-gather.16.cloned.1.call-done), kind=kOutput, calls=%fused_computation.252 | convolution fusion | flops 13500414976 | bytes 66196480 | tf_op jit(solution)/shard_map/xyd,md->xym/dot_general | solution.py:207
  969.4 19.9 convolution_convert_fusion
  989.4 85.4 %reduce-scatter.15.cloned.1.call-done = bf16[16,64,1280]{2,1,0:T(8,128)(2,1)} async-done(((bf16[64,64,1280]{2,1,0:T(8,128)(2,1)}), bf16[16,64,1280]{2,1,0:T(8,128)(2,1)}) %reduce-scatter.15.cloned.1.call-update) | async-done | bytes 2621456 | tf_op jit(solution)/shard_map/reduce_scatter | solution.py:216
  1096.3 20.8 %fusion.112 = bf16[1280,1280]{0,1:T(8,128)(2,1)} fusion(bf16[64,64,1280]{2,1,0:T(8,128)(2,1)} %get-tuple-element.415, bf16[64,64,1280]{2,1,0:T(8,128)(2,1)} %all-gather.18.cloned.1.call-done), kind=kOutput, calls=%fused_computation.156 | convolution fusion | flops 13423411200 | bytes 24248320 | tf_op jit(solution)/shard_map/xym,xyd->md/dot_general | solution.py:206
  1117.2 21.1 %fusion.113 = bf16[1280,1280]{1,0:T(8,128)(2,1)} fusion(bf16[64,64,1280]{2,1,0:T(8,128)(2,1)} %all-gather.12.cloned.1.call-done, bf16[64,64,1280]{2,1,0:T(8,128)(2,1)} %get-tuple-element.432), kind=kOutput, calls=%fused_computation.157 | convolution fusion | flops 13423411200 | bytes 24248320 | tf_op jit(solution)/shard_map/xyd,xym->dm/dot_general | solution.py:214
  1138.4 28.2 %all-gather.20.cloned.1.call-done = bf16[64,64,1280]{2,1,0:T(8,128)(2,1)} async-done(((bf16[16,64,1280]{2,1,0:T(8,128)(2,1)}), bf16[64,64,1280]{2,1,0:T(8,128)(2,1)}) %all-gather.20.cloned.1.call-update) | async-done | bytes 10485776 | tf_op jit(solution)/shard_map/all_gather | solution.py:229
  1189.2 10.6 reshape_reshape.7
  1199.8 11.4 copy.124
  1211.2 468.2 %while.32 = (s32[]{:T(128)}, f32[5,5,196,4,80]{2,4,3,1,0:T(8,128)}, bf16[5,5,196,4,80]{2,4,3,1,0:T(8,128)(2,1)}, f32[5,5,196,4,80]{2,4,3,1,0:T(8,128)}, f32[5,2,...) while((s32[]{:T(128)}, f32[5,5,196,4,80]{2,4,3,1,0:T(8,128)}, ...), condition=%wide.region_17.18_spmd.clone.clone, body=%wide.region_13.17_spmd.clone.clone.sunk | while | flops 1137800704 | bytes 142737584 | solution.py:237
  1216.2 8.9 convolution_bitcast_fusion.17
  1308.3 8.8 convolution_bitcast_fusion.17
  1400.6 8.8 convolution_bitcast_fusion.17
  1492.8 8.8 convolution_bitcast_fusion.17
  1584.9 8.8 convolution_bitcast_fusion.17
  1679.5 9.0 fusion.166
  1696.4 9.1 fusion.167
  1721.2 10.1 fusion.148
  1731.4 17.5 fusion.143
  1763.5 25.8 %bitcast_convert_fusion = bf16[5,5,196,1280]{3,2,1,0:T(8,128)(2,1)} fusion(bf16[1,5,5,196,320]{4,3,0,2,1:T(8,128)(2,1)} %copy.127, bf16[1,5,5,196,320]{4,3,0,2,1:T(8,128)(2,1)} %copy.126, bf16[1,5,5,196,320]{4,3,0,2,1:T(8,128)(2,1)} %copy.125, bf16[3,1280,320]{2,1,0:T(8,128)(2,1)} %all-gather.10.cloned.1.call-done), kind=kOutput, calls=%fused_computation.114 | convolution fusion | flops 12057920512 | bytes 24409600 | tf_op jit(solution)/shard_map/sabpc,sdc->abpd/dot_general | solution.py:248
  1789.3 19.4 reshape.299
  1808.7 13.0 copy.188
  1821.7 18.7 reshape.300
  1840.4 9.2 slice.72
  1854.8 37.5 %all-reduce.3 = (f32[2,320]{1,0:T(2,128)}, f32[1280]{0:T(1024)}) all-reduce(f32[2,320]{1,0:T(2,128)S(1)} %pad_maximum_fusion.10, f32[1280]{0:T(1024)S(1)} %copy-done.57), channel_id=1, replica_groups=mesh['dp'=8,'tensor'=4] {'dp'}, use_global_device_ids=true, to_apply=%region_29.30 | all-reduce | flops 1920 | bytes 15360 | tf_op jit(solution)/shard_map/psum | solution.py:273
  1898.7 56.9 %reduce-scatter.17.cloned.1.call-done = bf16[16,64,1280]{2,1,0:T(8,128)(2,1)} async-done(((bf16[64,64,1280]{2,1,0:T(8,128)(2,1)}), bf16[16,64,1280]{2,1,0:T(8,128)(2,1)}) %reduce-scatter.17.cloned.1.call-update) | async-done | bytes 2621456 | tf_op jit(solution)/shard_map/reduce_scatter | solution.py:251
  1962.5 41.0 %all-reduce.2 = (f32[]{:T(128)}, f32[2,1280]{1,0:T(2,128)}, f32[2,1280]{1,0:T(2,128)}, f32[2,1280]{1,0:T(2,128)}, f32[2,27,80]{2,1,0:T(8,128)S(1)}) all-reduce(f32[]{:T(128)} %get-tuple-element.343, f32[2,1280]{1,0:T(2,128)S(1)} %pad_maximum_fusion.7, ...), channel_id=1, replica_groups=mesh['dp'=8,'tensor'=4] {'dp','tensor'}, use_global_device_ids=true, to_apply=%region_22.23 | all-reduce | flops 12001 | bytes 96008 | tf_op jit(solution)/shard_map/psum | solution.py:274
  (539 shorter events, 775.2 us)
Async XLA Ops:
  7.2 82.5 %all-gather.8.cloned.1.call-start = ((), (), s32[]{:S(2)}) async-start(), calls=%async_computation.8 | async-start | bytes 13107200 | tf_op jit(solution)/shard_map/all_gather | solution.py:163
  16.7 134.6 %all-gather.10.cloned.1.call-start = ((), (), s32[]{:S(2)}) async-start(), calls=%async_computation.9 | async-start | bytes 3317760 | tf_op jit(solution)/shard_map/all_gather | solution.py:147
  17.4 536.9 %reduce-scatter.11.cloned.1.call-start = ((), (), s32[]{:S(2)}) async-start(), calls=%async_computation.10 | async-start | bytes 13107200 | tf_op jit(solution)/shard_map/reduce_scatter | solution.py:174
  424.5 21.5 %copy-start.18 = (s32[196,14]{1,0:T(8,128)}, s32[196,14]{1,0:T(8,128)S(1)}, u32[]{:S(2)}) copy-start(s32[196,14]{1,0:T(8,128)S(1)} %get-tuple-element.697) | copy-start | bytes 32932
  424.5 21.5 %copy-start.24 = (bf16[27,80]{1,0:T(8,128)(2,1)}, bf16[27,80]{1,0:T(8,128)(2,1)S(1)}, u32[]{:S(2)}) copy-start(bf16[27,80]{1,0:T(8,128)(2,1)S(1)} %get-tuple-element.724) | copy-start | bytes 12964
  424.5 21.5 %copy-start.26 = (bf16[27,80]{1,0:T(8,128)(2,1)}, bf16[27,80]{1,0:T(8,128)(2,1)S(1)}, u32[]{:S(2)}) copy-start(bf16[27,80]{1,0:T(8,128)(2,1)S(1)} %get-tuple-element.725) | copy-start | bytes 12964
  468.8 85.6 %copy-start.5 = (bf16[1,16,64,1280]{3,2,1,0:T(8,128)(2,1)S(1)}, bf16[1,16,64,1280]{3,2,1,0:T(8,128)(2,1)}, u32[]{:S(2)}) copy-start(bf16[1,16,64,1280]{3,2,1,0:T(8,128)(2,1)} %param.17) | copy-start | bytes 7864324
  468.8 149.6 %all-gather.14.cloned.1.call-start = ((), (), s32[]{:S(2)}) async-start(), calls=%async_computation.12 | async-start | bytes 3686400 | tf_op jit(solution)/shard_map/all_gather | solution.py:149
  469.4 219.8 %all-gather.12.cloned.1.call-start = ((), (), s32[]{:S(2)}) async-start(), calls=%async_computation.11 | async-start | bytes 13107200 | tf_op jit(solution)/shard_map/all_gather | solution.py:184
  470.1 89.0 %copy-start.30 = (f32[1280]{0:T(1024)}, f32[1280]{0:T(1024)S(1)}, u32[]{:S(2)}) copy-start(f32[1280]{0:T(1024)S(1)} %get-tuple-element.352) | copy-start | bytes 15364
  562.3 190.9 %all-gather.16.cloned.1.call-start = ((), (), s32[]{:S(2)}) async-start(), calls=%async_computation.13 | async-start | bytes 3686400 | tf_op jit(solution)/shard_map/all_gather | solution.py:150
  562.9 294.5 %reduce-scatter.13.cloned.1.call-start = ((), (), s32[]{:S(2)}) async-start(), calls=%async_computation.14 | async-start | bytes 13107200 | tf_op jit(solution)/shard_map/reduce_scatter | solution.py:191
  773.3 84.1 %copy-start.6 = (bf16[1,16,64,1280]{3,2,1,0:T(8,128)(2,1)S(1)}, bf16[1,16,64,1280]{3,2,1,0:T(8,128)(2,1)}, u32[]{:S(2)}) copy-start(bf16[1,16,64,1280]{3,2,1,0:T(8,128)(2,1)} %param.17) | copy-start | bytes 7864324
  773.3 84.1 %copy-start.31 = (f32[1280]{0:T(1024)S(1)}, f32[1280]{0:T(1024)}, u32[]{:S(2)}) copy-start(f32[1280]{0:T(1024)} %copy-done.30) | copy-start | bytes 15364
  773.3 84.1 %copy-start.45 = (f32[1280]{0:T(1024)S(1)}, f32[1280]{0:T(1024)}, u32[]{:S(2)}) copy-start(f32[1280]{0:T(1024)} %get-tuple-element.353) | copy-start | bytes 15364
  773.3 165.4 %all-gather.18.cloned.1.call-start = ((), (), s32[]{:S(2)}) async-start(), calls=%async_computation.15 | async-start | bytes 13107200 | tf_op jit(solution)/shard_map/all_gather | solution.py:205
  868.3 206.5 %reduce-scatter.15.cloned.1.call-start = ((), (), s32[]{:S(2)}) async-start(), calls=%async_computation.16 | async-start | bytes 13107200 | tf_op jit(solution)/shard_map/reduce_scatter | solution.py:216
  989.3 85.5 %copy-start.35 = (f32[16,64]{1,0:T(8,128)S(1)}, f32[16,64]{1,0:T(8,128)}, u32[]{:S(2)}) copy-start(f32[16,64]{1,0:T(8,128)} %copy-done.34) | copy-start | bytes 12292
  989.3 85.5 %copy-start.39 = (f32[1280]{0:T(1024)S(1)}, f32[1280]{0:T(1024)}, u32[]{:S(2)}) copy-start(f32[1280]{0:T(1024)} %get-tuple-element.349) | copy-start | bytes 15364
  989.3 90.7 %copy-start.49 = (f32[16,64]{1,0:T(8,128)S(1)}, f32[16,64]{1,0:T(8,128)}, u32[]{:S(2)}) copy-start(f32[16,64]{1,0:T(8,128)} %copy-done.48) | copy-start | bytes 12292
  989.4 90.7 %copy-start.43 = (f32[16,64]{1,0:T(8,128)S(1)}, f32[16,64]{1,0:T(8,128)}, u32[]{:S(2)}) copy-start(f32[16,64]{1,0:T(8,128)} %copy-done.42) | copy-start | bytes 12292
  989.4 177.2 %all-gather.20.cloned.1.call-start = ((), (), s32[]{:S(2)}) async-start(), calls=%async_computation.17 | async-start | bytes 13107200 | tf_op jit(solution)/shard_map/all_gather | solution.py:229
  1074.8 13.8 slice-start
  1096.2 754.0 %reduce-scatter.23.cloned.1.call-start = ((), (), s32[]{:S(2)}) async-start(), calls=%async_computation.21 | async-start | bytes 3686400 | tf_op jit(solution)/shard_map/reduce_scatter | solution.py:269
  1117.1 735.3 %reduce-scatter.21.cloned.1.call-start = ((), (), s32[]{:S(2)}) async-start(), calls=%async_computation.20 | async-start | bytes 3686400 | tf_op jit(solution)/shard_map/reduce_scatter | solution.py:266
  1117.2 49.4 %copy-start.29 = (bf16[320,1280]{0,1:T(8,128)(2,1)S(1)}, bf16[320,1280]{0,1:T(8,128)(2,1)}, u32[]{:S(2)}) copy-start(bf16[320,1280]{0,1:T(8,128)(2,1)} %all_gather.26) | copy-start | bytes 2457604
  1138.4 753.9 %reduce-scatter.19.cloned.1.call-start = ((), (), s32[]{:S(2)}) async-start(), calls=%async_computation.19 | async-start | bytes 1105920 | tf_op jit(solution)/shard_map/reduce_scatter | solution.py:263
  1199.8 11.4 copy-start.19
  1199.8 11.4 copy-start.21
  1199.8 11.4 copy-start.25
  1199.8 11.4 copy-start.27
  1279.1 10.3 copy-start.9
  1279.1 13.4 copy-start.1
  1371.2 10.3 copy-start.9
  1371.2 13.4 copy-start.1
  1463.4 10.3 copy-start.9
  1463.4 13.4 copy-start.1
  1555.6 10.3 copy-start.9
  1555.6 13.4 copy-start.1
  1647.6 10.3 copy-start.9
  1647.6 13.4 copy-start.1
  1731.3 162.5 %reduce-scatter.25.cloned.1.call-start = ((), (), s32[]{:S(2)}) async-start(), calls=%async_computation.22 | async-start | bytes 2949120
  1763.4 192.2 %reduce-scatter.17.cloned.1.call-start = ((), (), s32[]{:S(2)}) async-start(), calls=%async_computation.18 | async-start | bytes 13107200 | tf_op jit(solution)/shard_map/reduce_scatter | solution.py:251
  1849.6 106.0 %copy-start.7 = (bf16[1,16,64,1280]{3,2,1,0:T(8,128)(2,1)S(1)}, bf16[1,16,64,1280]{3,2,1,0:T(8,128)(2,1)}, u32[]{:S(2)}) copy-start(bf16[1,16,64,1280]{3,2,1,0:T(8,128)(2,1)} %param.17) | copy-start | bytes 7864324
  1849.6 106.0 %copy-start.33 = (f32[16,64]{1,0:T(8,128)S(1)}, f32[16,64]{1,0:T(8,128)}, u32[]{:S(2)}) copy-start(f32[16,64]{1,0:T(8,128)} %copy-done.32) | copy-start | bytes 12292
  1849.6 106.0 %copy-start.37 = (f32[1280]{0:T(1024)S(1)}, f32[1280]{0:T(1024)}, u32[]{:S(2)}) copy-start(f32[1280]{0:T(1024)} %copy-done.36) | copy-start | bytes 15364
  1852.4 107.0 %copy-start.47 = (f32[16,64]{1,0:T(8,128)S(1)}, f32[16,64]{1,0:T(8,128)}, u32[]{:S(2)}) copy-start(f32[16,64]{1,0:T(8,128)} %copy-done.46) | copy-start | bytes 12292
  1852.4 107.1 %copy-start.41 = (f32[16,64]{1,0:T(8,128)S(1)}, f32[16,64]{1,0:T(8,128)}, u32[]{:S(2)}) copy-start(f32[16,64]{1,0:T(8,128)} %copy-done.40) | copy-start | bytes 12292
  (75 other events, 284.7 us)
Sparse Core Ops, SparseCore 0:
  16.8 72.8 all-gather.7
  91.9 58.3 all-gather.9
  468.9 85.3 reduce-scatter.10
  556.3 61.9 all-gather.13
  620.3 68.7 all-gather.11
  691.2 61.9 all-gather.15
  773.4 83.8 reduce-scatter.12
  868.5 70.1 all-gather.17
  989.5 85.2 reduce-scatter.14
  1096.4 70.1 all-gather.19
  1170.2 76.0 reduce-scatter.22
  1250.2 74.9 reduce-scatter.20
  1731.5 63.6 reduce-scatter.18
  1798.9 69.6 reduce-scatter.24
  1871.2 84.3 reduce-scatter.16
where the time goes:
time: 2030 us; the launch traced here: 2020 us
  matrix products  677 us (33%)
  waiting for transfers between devices  575 us (28%)
  local copies, waits for them, and re-layouts  520 us (26%)
  blocking collectives  115 us (6%)
  other arithmetic  105 us (5%)
    reduce_scatter x1, waiting for transfers between devices, shards(): lax.psum_scatter(jnp.einsum('xym,dm->xyd', row_piece, up_matrix, preferre...  85.4 us
    reduce_scatter x1, waiting for transfers between devices, shards(): lax.psum_scatter(jnp.einsum('xyc,cd->xyd', row_piece, proj_full, preferre...  84.2 us
    reduce_scatter x1, waiting for transfers between devices, shards(): lax.psum_scatter(jnp.einsum('xym,md->xyd', row_piece, down_matrix, prefer...  84 us
    dot_general x10, matrix products, score_block(): jnp.einsum('wqhr,qkr->whqk', along_wide, wide_sel, precision=highest)  78 us
    dot_general x10, matrix products, score_block(): jnp.einsum('wqhr,qkr->whqk', along_high, high_sel, precision=highest)  77.8 us
    all_gather x1, waiting for transfers between devices, shards(): mlp_input = lax.all_gather(normed_two, 'tensor', axis=0, tiled=True)  70.8 us
    all_gather x1, waiting for transfers between devices, shards(): grad_rows = lax.all_gather(result_low, 'tensor', axis=0, tiled=True)  70.3 us
    dot_general x1, matrix products, shards(): jnp.einsum('xyd,dm->xym', mlp_input, up_matrix, preferred_element_type=jn...  60.9 us
  transfers between devices with their start and end apart: 15, of which 10 were waited for; matrix products, arithmetic and copies ran while one was open for 42% of the time, Pallas kernels for 0%

commit v1 on v0

--- a/solution.py
+++ b/solution.py
@@ -2,7 +2,10 @@
 
 import jax
 import jax.numpy as jnp
+import numpy as np
 from jax import lax
+from jax.experimental import pallas as pl
+from jax.experimental.pallas import tpu as pltpu
 from jax.sharding import PartitionSpec as P
 
 D = 1280
@@ -128,7 +131,7 @@
     return (query_grad, key_grad, value_grad, table_grad)
 
 
-def shards(
+def general_shards(
     inputs,
     cotangent,
     teacher,
@@ -293,6 +296,576 @@
     )
 
 
+SIDE = 16
+GROUP = 4
+KEYS = WIN * SIDE
+SLABS = ((0, 128), (0, 256), (128, 256), (128, 384))
+SCALE = HEAD_DIM ** (-0.5)
+LOG2E = 1.4426950408889634
+NT = (((1,), (1,)), ((), ()))
+TN = (((0,), (0,)), ((), ()))
+NN = (((1,), (0,)), ((), ()))
+
+
+def dot(a, b, dims):
+    return lax.dot_general(a, b, dims, preferred_element_type=jnp.float32)
+
+
+def bias_tables(rel_tables):
+    tables = rel_tables.astype(jnp.bfloat16)
+
+    def place(rows):
+        padded = jnp.pad(rows, ((0, 5), (0, 0)))
+        eye = jnp.eye(GROUP, dtype=jnp.bfloat16)
+        spread = eye[:, None, :, None] * padded[None, :, None, :]
+        return spread.reshape(GROUP * 32, GROUP * HEAD_DIM)
+
+    forward = jnp.concatenate([place(tables[0][::-1]), place(tables[1][::-1])])
+    backward = jnp.concatenate([place(tables[0][::-1]), place(tables[1])])
+    lanes = ((0, 0), (0, 64))
+    return jnp.pad(forward, lanes), jnp.pad(backward, lanes)
+
+
+def selectors():
+    key = np.arange(KEYS)
+    high, wide = key // SIDE, key % SIDE
+    fwd = np.zeros((GROUP, KEYS, 128), np.float32)
+    bwd = np.zeros((GROUP, KEYS, 128), np.float32)
+    real = wide < WIN
+    for head in range(GROUP):
+        for j in range(KEYS):
+            if real[j]:
+                fwd[head, j, 32 * head + high[j]] = 1.0
+                fwd[head, j, 32 * head + 16 + wide[j]] = 1.0
+                bwd[head, j, 32 * head + high[j]] = 1.0
+                bwd[head, j, 32 * head + 16 + 13 - wide[j]] = 1.0
+            else:
+                fwd[head, j, 32 * head + 14] = -1e30
+    fwd = np.concatenate([fwd, fwd], axis=-1)
+    return jnp.asarray(fwd, jnp.bfloat16), jnp.asarray(bwd, jnp.bfloat16)
+
+
+def lane_iota(shape):
+    return lax.broadcasted_iota(jnp.int32, shape, 1)
+
+
+def head_mask(values, head, low):
+    lane = lane_iota(values.shape) + low
+    inside = (lane >= HEAD_DIM * head) & (lane < HEAD_DIM * head + HEAD_DIM)
+    return jnp.where(inside, values, jnp.zeros_like(values))
+
+
+def shift_lanes(values, amount):
+    wide = values.astype(jnp.float32)
+    return pltpu.roll(wide, amount % wide.shape[1], 1)
+
+
+def load_group(qkv_ref, part, first):
+    rows = qkv_ref.shape[1]
+    q = qkv_ref[part, first:first + 16, :, 0:384].reshape(16 * SIDE, 384)
+    k = qkv_ref[part, :, :, 256:640].reshape(rows * SIDE, 384)
+    k = shift_lanes(k, -64).astype(jnp.bfloat16)
+    v = qkv_ref[part, :, :, 640:960].reshape(rows * SIDE, 320)
+    return q, k, v
+
+
+def bias_rows(q, tables, first):
+    along = dot(q, tables, NT) * (HEAD_DIM ** 0.5)
+    high, wide = along[:, :128], along[:, 128:]
+    pieces = []
+    lane = lane_iota((SIDE, 128)) % 32
+    for row in range(16):
+        ih = (first + row) % WIN
+        rows = slice(row * SIDE, (row + 1) * SIDE)
+        up = pltpu.roll(high[rows], (ih - 13) % 128, 1)
+        across = pltpu.roll(wide[rows], 3, 1, stride=1, stride_axis=0)
+        both = jnp.where(lane < 16, up, across)
+        pieces.append(jnp.where(lane == 14, 1.0, both))
+    both = jnp.concatenate(pieces)
+    upper = both.astype(jnp.bfloat16)
+    lower = (both - upper.astype(jnp.float32)).astype(jnp.bfloat16)
+    return jnp.concatenate([upper, lower], axis=1)
+
+
+def softmax_rows(q, k, bias, select, head, split):
+    low, high = SLABS[head]
+    left = jnp.concatenate([q[:, low:high], bias], axis=1)
+    sides = []
+    for side, rows in ((0, slice(0, split)), (1, slice(split, 16 * SIDE))):
+        keys = head_mask(k[side * KEYS:(side + 1) * KEYS, low:high], head, low)
+        sides.append(dot(left[rows], jnp.concatenate([keys, select], axis=1), NT))
+    scores = jnp.concatenate(sides)
+    top = jnp.max(scores, axis=1, keepdims=True)
+    raised = jnp.exp2((scores - top) * (SCALE * LOG2E))
+    total = jnp.sum(raised, axis=1, keepdims=True)
+    return raised * (1.0 / total)
+
+
+def forward_body(first, qkv_ref, table_ref, select_ref, out_ref, acc):
+    split = (WIN - first) * SIDE
+    for part in range(2):
+        q, k, v = load_group(qkv_ref, part, first)
+        bias = bias_rows(q, table_ref[...], first)
+        for head in range(GROUP):
+            low, high = SLABS[head]
+            high = min(high, 320)
+            probs = softmax_rows(q, k, bias, select_ref[head], head, split).astype(jnp.bfloat16)
+            sides = []
+            for side, rows in ((0, slice(0, split)), (1, slice(split, 16 * SIDE))):
+                values = head_mask(v[side * KEYS:(side + 1) * KEYS, low:high], head, low)
+                sides.append(dot(probs[rows], values, NN))
+            piece = jnp.concatenate(sides)
+            if head == 0:
+                acc[part, :, 0:128] = piece
+                acc[part, :, 128:384] = jnp.zeros((16 * SIDE, 256), jnp.float32)
+            else:
+                acc[part, :, low:high] += piece
+    second = pltpu.roll(acc[1], 64, 1)
+    middle = acc[0, :, 256:384] + second[:, 0:128]
+    whole = jnp.concatenate([acc[0, :, 0:256], middle, second[:, 128:384]], axis=1)
+    out_ref[...] = whole.astype(jnp.bfloat16).reshape(16, SIDE, 640)
+
+
+def by_shard(shard_ref, body):
+    for shard in range(4):
+        @pl.when(shard_ref[0] == shard)
+        def _():
+            body(2 * shard)
+
+
+def forward_kernel(shard_ref, qkv_ref, table_ref, select_ref, out_ref, acc):
+    by_shard(shard_ref, lambda first: forward_body(first, qkv_ref, table_ref, select_ref, out_ref, acc))
+
+
+def window_attend(shard, qkv, tables, select):
+    spec = pltpu.PrefetchScalarGridSpec(
+        num_scalar_prefetch=1,
+        grid=(5, 2),
+        in_specs=[
+            pl.BlockSpec((2, 28, SIDE, 960), lambda w, p, s: (p, 0, w, 0)),
+            pl.BlockSpec((256, 384), lambda w, p, s: (0, 0)),
+            pl.BlockSpec((GROUP, KEYS, 256), lambda w, p, s: (0, 0, 0)),
+        ],
+        out_specs=pl.BlockSpec((16, SIDE, 640), lambda w, p, s: (0, w, p)),
+        scratch_shapes=[pltpu.VMEM((2, 16 * SIDE, 384), jnp.float32)],
+    )
+    return pl.pallas_call(
+        forward_kernel,
+        grid_spec=spec,
+        out_shape=jax.ShapeDtypeStruct((16, 5 * SIDE, 1280), jnp.bfloat16),
+        compiler_params=pltpu.CompilerParams(vmem_limit_bytes=48 << 20),
+        cost_estimate=pl.CostEstimate(flops=1_000_000, bytes_accessed=1_000_000, transcendentals=0),
+        name="attend",
+    )(shard, qkv, tables, select)
+
+
+def backward_body(first, qkv_ref, grad_ref, table_ref, back_ref, select_ref, spread_ref, out_ref, sums_ref, dq, dk, dv):
+    split = (WIN - first) * SIDE
+    queries = 16 * SIDE
+    ranges = ((0, slice(0, split)), (1, slice(split, queries)))
+    zero = jnp.zeros((queries, 128), jnp.float32)
+    lane = lane_iota((SIDE, 128)) % 32
+    for part in range(2):
+        q, k, v = load_group(qkv_ref, part, first)
+        if part == 0:
+            go = grad_ref[:, :, 0:384].reshape(queries, 384)
+        else:
+            go = shift_lanes(grad_ref[:, :, 256:640].reshape(queries, 384), -64).astype(jnp.bfloat16)
+        bias = bias_rows(q, table_ref[...], first)
+        dq[...] = jnp.zeros_like(dq)
+        dk[...] = jnp.zeros_like(dk)
+        dv[...] = jnp.zeros_like(dv)
+        marks = zero
+        for head in range(GROUP):
+            low, high = SLABS[head]
+            vhigh = min(high, 320)
+            probs = softmax_rows(q, k, bias, select_ref[head], head, split)
+            probs_low = probs.astype(jnp.bfloat16)
+            sides = []
+            for side, rows in ranges:
+                values = head_mask(v[side * KEYS:(side + 1) * KEYS, low:vhigh], head, low)
+                sides.append(dot(go[rows, low:vhigh], values, NT))
+            probs_grad = jnp.concatenate(sides)
+            weighted = probs * probs_grad
+            scores_grad = weighted - probs * jnp.sum(weighted, axis=1, keepdims=True)
+            scores_low = scores_grad.astype(jnp.bfloat16)
+            go_head = head_mask(go[:, low:high], head, low)
+            q_head = head_mask(q[:, low:high], head, low)
+            for side, rows in ranges:
+                span = slice(side * KEYS, (side + 1) * KEYS)
+                dv[span, low:high] += dot(probs_low[rows], go_head[rows], TN)
+                dk[span, low:high] += dot(scores_low[rows], q_head[rows], TN)
+                keys = head_mask(k[span, low:high], head, low)
+                dq[rows, low:high] += dot(scores_low[rows], keys, NN)
+            marks = marks + dot(scores_low, spread_ref[head], NN)
+        highs, wides = [], []
+        for row in range(16):
+            ih = (first + row) % WIN
+            piece = marks[row * SIDE:(row + 1) * SIDE]
+            highs.append(pltpu.roll(jnp.where(lane < 14, piece, 0.0), (13 - ih) % 128, 1))
+            across = jnp.where((lane >= 16) & (lane < 30), piece, 0.0)
+            wides.append(pltpu.roll(across, 112, 1, stride=1, stride_axis=0))
+        ranks = jnp.concatenate([jnp.concatenate(highs), jnp.concatenate(wides)], axis=1).astype(jnp.bfloat16)
+        dq_full = dq[...] * SCALE + dot(ranks, back_ref[...], NN)
+        sums_ref[...] += dot(ranks, q, TN)
+        before, after = first * SIDE, (28 - 16 - first) * SIDE
+        pieces = [dq_full]
+        if before:
+            pieces = [jnp.zeros((before, 384), jnp.float32)] + pieces
+        if after:
+            pieces = pieces + [jnp.zeros((after, 384), jnp.float32)]
+        dq_all = jnp.concatenate(pieces) if len(pieces) > 1 else dq_full
+        dk_all = pltpu.roll(dk[...] * SCALE, 64, 1)
+        joint = lane_iota((28 * SIDE, 128))
+        middle = jnp.where(joint < 64, dq_all[:, 256:384], dk_all[:, 0:128])
+        left = jnp.concatenate([dq_all[:, 0:256], middle, dk_all[:, 128:384]], axis=1)
+        out_ref[part, :, :, 0:640] = left.astype(jnp.bfloat16).reshape(28, SIDE, 640)
+        out_ref[part, :, :, 640:960] = dv[:, 0:320].astype(jnp.bfloat16).reshape(28, SIDE, 320)
+
+
+def backward_kernel(shard_ref, qkv_ref, grad_ref, table_ref, back_ref, select_ref, spread_ref, out_ref, sums_ref, dq, dk, dv):
+    @pl.when(pl.program_id(0) == 0)
+    def _():
+        sums_ref[...] = jnp.zeros_like(sums_ref)
+
+    by_shard(shard_ref, lambda first: backward_body(first, qkv_ref, grad_ref, table_ref, back_ref, select_ref, spread_ref, out_ref, sums_ref, dq, dk, dv))
+
+
+def window_attend_back(pair, shard, qkv, grad, tables, back, select, spread):
+    spec = pltpu.PrefetchScalarGridSpec(
+        num_scalar_prefetch=1,
+        grid=(5,),
+        in_specs=[
+            pl.BlockSpec((2, 28, SIDE, 960), lambda w, s: (pair, 0, w, 0)),
+            pl.BlockSpec((16, SIDE, 640), lambda w, s: (0, w, pair)),
+            pl.BlockSpec((256, 384), lambda w, s: (0, 0)),
+            pl.BlockSpec((256, 384), lambda w, s: (0, 0)),
+            pl.BlockSpec((GROUP, KEYS, 256), lambda w, s: (0, 0, 0)),
+            pl.BlockSpec((GROUP, KEYS, 128), lambda w, s: (0, 0, 0)),
+        ],
+        out_specs=[
+            pl.BlockSpec((2, 28, SIDE, 960), lambda w, s: (0, 0, w, 0)),
+            pl.BlockSpec((256, 384), lambda w, s: (0, 0)),
+        ],
+        scratch_shapes=[
+            pltpu.VMEM((16 * SIDE, 384), jnp.float32),
+            pltpu.VMEM((2 * KEYS, 384), jnp.float32),
+            pltpu.VMEM((2 * KEYS, 384), jnp.float32),
+        ],
+    )
+    return pl.pallas_call(
+        backward_kernel,
+        grid_spec=spec,
+        out_shape=[
+            jax.ShapeDtypeStruct((2, 28, 5 * SIDE, 960), jnp.bfloat16),
+            jax.ShapeDtypeStruct((256, 384), jnp.float32),
+        ],
+        compiler_params=pltpu.CompilerParams(vmem_limit_bytes=48 << 20),
+        cost_estimate=pl.CostEstimate(flops=1_000_000, bytes_accessed=1_000_000, transcendentals=0),
+        name="attend_back",
+    )(shard, qkv, grad, tables, back, select, spread)
+
+
+def project_kernel(shard_ref, x_ref, w_ref, bias_ref, out_ref):
+    weights = w_ref[0][:, :960]
+    for start in range(0, x_ref.shape[0], 448):
+        rows = slice(start, start + 448)
+        out_ref[0, rows, :] = (dot(x_ref[rows, :], weights, NN) + bias_ref[0]).astype(jnp.bfloat16)
+
+
+def project(shard, x, weights, bias):
+    tokens = x.shape[0]
+    spec = pltpu.PrefetchScalarGridSpec(
+        num_scalar_prefetch=1,
+        grid=(4,),
+        in_specs=[
+            pl.BlockSpec((tokens, x.shape[1]), lambda p, s: (0, 0)),
+            pl.BlockSpec((1,) + weights.shape[1:], lambda p, s: (p ^ s[0], 0, 0)),
+            pl.BlockSpec((1, 1, 960), lambda p, s: (p ^ s[0], 0, 0)),
+        ],
+        out_specs=pl.BlockSpec((1, tokens, 960), lambda p, s: (p, 0, 0)),
+    )
+    return pl.pallas_call(
+        project_kernel,
+        grid_spec=spec,
+        out_shape=jax.ShapeDtypeStruct((4, tokens, 960), jnp.bfloat16),
+        compiler_params=pltpu.CompilerParams(vmem_limit_bytes=48 << 20),
+        cost_estimate=pl.CostEstimate(flops=1_000_000, bytes_accessed=1_000_000, transcendentals=0),
+        name="project",
+    )(shard, x, weights, bias)
+
+
+ROWS = 16
+FRAME = 28
+EARLY, LATE = 6, 12
+EPSILON = 1e-06
+
+
+def swap(values, shifts):
+    return lax.ppermute(values, "tensor", shifts)
+
+
+def own(values, index, axis=0):
+    return lax.dynamic_index_in_dim(values, index, axis, keepdims=False)
+
+
+def gather_small(values, shard):
+    parts = [values]
+    for step in (1, 2, 3):
+        parts.append(swap(values, [(i, (i + step) % 4) for i in range(4)]))
+    stack = jnp.stack(parts)
+    return jnp.stack([own(stack, (shard - i) % 4) for i in range(4)])
+
+
+CORES = [(0, 1), (1, 0), (2, 3), (3, 2)]
+SIDES = [(0, 2), (2, 0), (1, 3), (3, 1)]
+
+
+def add_low(left, right):
+    return (left.astype(jnp.float32) + right.astype(jnp.float32)).astype(jnp.bfloat16)
+
+
+def scatter_dp(quarter):
+    return lax.psum_scatter(quarter, "dp", scatter_dimension=0, tiled=True)
+
+
+def after(first, *values):
+    return lax.optimization_barrier((first,) + values)[1:]
+
+
+def sum_everywhere(values):
+    values = values + swap(values, CORES)
+    values = values + swap(values, SIDES)
+    count = lax.axis_size("dp")
+    step = 1
+    while step < count:
+        values = values + lax.ppermute(values, "dp", [(i, i ^ step) for i in range(count)])
+        step *= 2
+    return values
+
+
+def statistics(values):
+    average = jnp.mean(values, axis=-1, keepdims=True)
+    centred = values - average
+    rstd = lax.rsqrt(jnp.mean(centred * centred, axis=-1, keepdims=True) + EPSILON)
+    return centred * rstd, rstd
+
+
+def norm_back(grad, gain, hat, rstd):
+    scaled = grad * gain
+    mean_one = jnp.mean(scaled, axis=-1, keepdims=True)
+    mean_two = jnp.mean(scaled * hat, axis=-1, keepdims=True)
+    return rstd * (scaled - mean_one - hat * mean_two)
+
+
+def column_selector():
+    column = np.arange(GRID)
+    place = SIDE * (column // WIN) + column % WIN
+    select = np.zeros((NWIN * SIDE, GRID), np.float32)
+    select[place, column] = 1.0
+    return jnp.asarray(select, jnp.bfloat16)
+
+
+def fast_shards(
+    inputs,
+    cotangent,
+    teacher,
+    qkv_weight,
+    proj_weight,
+    up_weight,
+    down_weight,
+    qv_bias,
+    up_bias,
+    norm_gains,
+    norm_shifts,
+    out_biases,
+    rel_tables,
+):
+    f32, bf16 = jnp.float32, jnp.bfloat16
+    shard = lax.axis_index("tensor")
+    both = ("tensor", "dp")
+    tokens = ROWS * GRID
+    inner = qkv_weight.shape[1]
+    joint = jnp.concatenate([qkv_weight.transpose(1, 0, 2).reshape(inner, 960), proj_weight.T], axis=1)
+    joint_all = lax.all_gather(joint, both, axis=0, tiled=True)
+    joint_all = joint_all.reshape(4, D, 1280)
+    biases = gather_small(jnp.concatenate([qv_bias.reshape(-1), up_bias]), shard)
+    qkv_bias = jnp.concatenate(
+        [biases[:, :320], jnp.zeros((4, 320), bf16), biases[:, 320:640]], axis=1
+    ).astype(f32)
+    up_bias_all = biases[:, 640:].astype(f32)
+
+    gains = norm_gains.astype(f32)
+    shifts = norm_shifts.astype(f32)
+    image = inputs[0]
+    above = swap(image[ROWS - EARLY:], [(i, i + 1) for i in range(3)])
+    below = swap(image[:LATE], [(i + 1, i) for i in range(3)])
+    framed = lax.dynamic_slice_in_dim(
+        jnp.concatenate([above, image, below]), EARLY - 2 * shard, FRAME, 0
+    )
+    frame_hat, _ = statistics(framed.astype(f32))
+    inside = (WIN * shard + jnp.arange(FRAME) < GRID)[:, None, None]
+    normed = jnp.where(inside, frame_hat * gains[0] + shifts[0], 0.0).astype(bf16)
+    select = column_selector()
+    windows = jnp.einsum("pc,rcd->rpd", select, normed, preferred_element_type=f32).astype(bf16)
+    flat = windows.reshape(FRAME * NWIN * SIDE, D)
+    where = shard[None].astype(jnp.int32)
+    qkv = project(where, flat, joint_all, qkv_bias[:, None, :])
+    qkv = qkv.reshape(4, FRAME, NWIN * SIDE, 960)
+    tables, back_tables = bias_tables(rel_tables)
+    select_keys, spread_keys = selectors()
+    (up_shard,) = after((joint_all, flat), up_weight)
+    up_all = lax.all_gather(up_shard, both, axis=0, tiled=True).reshape(4, D, 1280)
+    joint_own = [own(joint_all, shard ^ p) for p in range(4)]
+    proj_full = jnp.concatenate([part[:, 960:] for part in joint_own], axis=1)
+    attended = window_attend(where, qkv, tables, select_keys)
+    attended = jnp.einsum("pc,rpd->rcd", select, attended, preferred_element_type=f32)
+    attended = attended.astype(bf16).reshape(tokens, D)
+
+    (down_shard,) = after(attended, down_weight.T)
+    down_all = lax.all_gather(down_shard, both, axis=0, tiled=True).reshape(4, D, 1280)
+    source = image.astype(f32).reshape(tokens, D)
+    branch = jnp.einsum("nk,ck->nc", attended, proj_full, preferred_element_type=f32)
+    middle = source + branch + out_biases[0].astype(f32)
+    second_hat, second_rstd = statistics(middle)
+    normed_two = (second_hat * gains[1] + shifts[1]).astype(bf16)
+    hidden = jnp.einsum("nd,tdm->tnm", normed_two, up_all, preferred_element_type=f32)
+    hidden = hidden + up_bias_all[:, None, :]
+    cdf = 0.5 + 0.5 * lax.erf(hidden * (0.5 ** 0.5))
+    active = (hidden * cdf).astype(bf16)
+    slope = (cdf + hidden * (jnp.exp(-0.5 * hidden * hidden) * (0.5 / np.pi) ** 0.5)).astype(bf16)
+    result = jnp.einsum("tnm,tcm->nc", active, down_all, preferred_element_type=f32)
+    result = middle + result + out_biases[1].astype(f32)
+    mismatch = result - teacher[0].astype(f32).reshape(tokens, D)
+    loss_total = jnp.sum(mismatch * mismatch)
+    output = result.astype(bf16)
+
+    result_grad = cotangent[0].astype(f32).reshape(tokens, D) + mismatch
+    result_low = result_grad.astype(bf16)
+    def down_block(p):
+        return jnp.einsum("nc,nm->cm", result_low, own(active, shard ^ p), preferred_element_type=f32)
+
+    sends = [down_block(3).astype(bf16), down_block(1).astype(bf16)]
+    down_three, down_one = swap(sends[0], CORES), swap(sends[1], CORES)
+    (result_next,) = after(tuple(sends), result_low)
+    active_grad = jnp.einsum("nc,tcm->tnm", result_next, down_all, preferred_element_type=f32)
+    hidden_grad = active_grad * slope.astype(f32)
+    up_bias_acc = jnp.sum(hidden_grad, axis=1)
+    hidden_low = hidden_grad.astype(bf16)
+    down_far = (down_block(2) + down_three.astype(f32)).astype(bf16)
+    down_near = (down_block(0) + down_one.astype(f32)).astype(bf16)
+    down_side = swap(down_far, SIDES)
+    hidden_low, normed_two = after((down_far, down_near), hidden_low, normed_two)
+
+    def up_block(p):
+        return jnp.einsum("nd,nm->dm", normed_two, own(hidden_low, shard ^ p), preferred_element_type=f32)
+
+    sends = [up_block(3).astype(bf16), up_block(1).astype(bf16)]
+    up_three, up_one = swap(sends[0], CORES), swap(sends[1], CORES)
+    (hidden_next,) = after(tuple(sends), hidden_low)
+    second_grad = jnp.einsum("tnm,tdm->nd", hidden_next, up_all, preferred_element_type=f32)
+    middle_grad = result_grad + norm_back(second_grad, gains[1], second_hat, second_rstd)
+    second_gain = jnp.sum(second_grad * second_hat, axis=0)
+    second_shift = jnp.sum(second_grad, axis=0)
+    middle_low = middle_grad.astype(bf16)
+    attended_grad = jnp.einsum("nc,ck->nk", middle_low, proj_full, preferred_element_type=f32)
+    attended_grad = attended_grad.astype(bf16).reshape(ROWS, GRID, D)
+    attended_grad = jnp.einsum("pc,rcd->rpd", select, attended_grad, preferred_element_type=f32)
+    attended_grad = attended_grad.astype(bf16)
+    up_far = (up_block(2) + up_three.astype(f32)).astype(bf16)
+    up_near = (up_block(0) + up_one.astype(f32)).astype(bf16)
+    up_side = swap(up_far, SIDES)
+
+    def proj_block(p):
+        part = attended[:, 320 * p:320 * p + 320]
+        return jnp.einsum("nc,nk->ck", middle_low, part, preferred_element_type=f32)
+
+    proj_three = swap(proj_block(3).astype(bf16), CORES)
+    proj_one = swap(proj_block(1).astype(bf16), CORES)
+    down_quarter = add_low(down_near, down_side)
+    down_grad = scatter_dp(down_quarter)
+    (grad_far,) = after((up_far, up_near, down_quarter), attended_grad)
+    far_back, far_sums = window_attend_back(
+        1, where, qkv, grad_far, tables, back_tables, select_keys, spread_keys
+    )
+    proj_far = (proj_block(2) + proj_three.astype(f32)).astype(bf16)
+    proj_near = (proj_block(0) + proj_one.astype(f32)).astype(bf16)
+    far_back = far_back.reshape(2, FRAME * NWIN * SIDE, 960)
+
+    def qkv_block(back):
+        return jnp.einsum("nd,nc->dc", flat, back, preferred_element_type=f32)
+
+    qkv_three = swap(qkv_block(far_back[1]).astype(bf16), CORES)
+    qkv_far = (qkv_block(far_back[0]) + qkv_three.astype(f32)).astype(bf16)
+    far_side = swap(jnp.concatenate([qkv_far, proj_far], axis=1), SIDES)
+    (grad_near,) = after((qkv_far, proj_far), attended_grad)
+    near_back, near_sums = window_attend_back(
+        0, where, qkv, grad_near, tables, back_tables, select_keys, spread_keys
+    )
+    near_back = near_back.reshape(2, FRAME * NWIN * SIDE, 960)
+    up_quarter = add_low(up_near, up_side)
+    up_grad = scatter_dp(up_quarter)
+    near_back, flat = after(up_quarter, near_back, flat)
+    qkv_one = swap(qkv_block(near_back[1]).astype(bf16), CORES)
+    qkv_near = qkv_block(near_back[0]) + qkv_one.astype(f32)
+    near = jnp.concatenate([qkv_near.astype(bf16), proj_near], axis=1)
+    joint_quarter = add_low(near, far_side)
+    joint_grad = scatter_dp(joint_quarter)
+    near_next, far_next = after(joint_quarter, near_back, far_back)
+    table_sums = far_sums + near_sums
+    bias_sums = jnp.concatenate([jnp.sum(near_next.astype(f32), axis=1), jnp.sum(far_next.astype(f32), axis=1)])
+    qv_acc = jnp.stack([bias_sums[:, :320], bias_sums[:, 640:]], axis=1)
+    qv_acc = jnp.stack([own(qv_acc, shard ^ t) for t in range(4)])
+    table_sums = table_sums[:, :320].reshape(2, GROUP, 32, GROUP, HEAD_DIM)
+    table_acc = jnp.einsum("phrhd->prd", table_sums)
+    table_acc = jnp.stack([table_acc[0, :27][::-1], table_acc[1, :27]])
+    weights = [part[:, :960] for part in joint_own]
+    frame_grad = jnp.einsum("tnc,tdc->nd", far_next, jnp.stack(weights[2:]), preferred_element_type=f32)
+    frame_grad = frame_grad + jnp.einsum("tnc,tdc->nd", near_next, jnp.stack(weights[:2]), preferred_element_type=f32)
+    frame_grad = frame_grad.astype(bf16).reshape(FRAME, NWIN * SIDE, D)
+    frame_grad = jnp.einsum("pc,rpd->rcd", select, frame_grad, preferred_element_type=f32).astype(bf16)
+    spread = jnp.zeros((EARLY + ROWS + LATE, GRID, D), bf16)
+    spread = lax.dynamic_update_slice_in_dim(spread, frame_grad, EARLY - 2 * shard, 0)
+    from_next = swap(spread[:EARLY], [(i + 1, i) for i in range(3)])
+    from_before = swap(spread[EARLY + ROWS:], [(i, i + 1) for i in range(3)])
+    first_grad = spread[EARLY:EARLY + ROWS].astype(f32)
+    first_grad = first_grad + jnp.pad(from_next.astype(f32), ((ROWS - EARLY, 0), (0, 0), (0, 0)))
+    first_grad = first_grad + jnp.pad(from_before.astype(f32), ((0, ROWS - LATE), (0, 0), (0, 0)))
+    first_grad = first_grad.reshape(tokens, D)
+    first_hat, first_rstd = statistics(source)
+    first_gain = jnp.sum(first_grad * first_hat, axis=0)
+    first_shift = jnp.sum(first_grad, axis=0)
+    input_grad = middle_grad + norm_back(first_grad, gains[0], first_hat, first_rstd)
+
+    small = [
+        qv_acc, up_bias_acc, first_gain, second_gain, first_shift, second_shift,
+        jnp.sum(middle_grad, axis=0), jnp.sum(result_grad, axis=0), table_acc, loss_total,
+    ]
+    sums = sum_everywhere(jnp.concatenate([part.reshape(-1) for part in small]))
+    parts = []
+    place = 0
+    for part in small:
+        parts.append(sums[place:place + part.size].reshape(part.shape))
+        place += part.size
+    qv_sum, up_sum, gain_one, gain_two, shift_one, shift_two, bias_one, bias_two, table_grad, loss_sum = parts
+    loss = loss_sum / (tokens * D * lax.axis_size("dp") * lax.axis_size("tensor"))
+    return (
+        output.reshape(1, ROWS, GRID, D),
+        input_grad.reshape(1, ROWS, GRID, D),
+        loss,
+        joint_grad[:, :960].reshape(inner, 3, 320).transpose(1, 0, 2).astype(f32),
+        joint_grad[:, 960:].T.astype(f32),
+        up_grad.astype(f32),
+        down_grad.T.astype(f32),
+        own(qv_sum, shard),
+        own(up_sum, shard),
+        jnp.stack([gain_one, gain_two]),
+        jnp.stack([shift_one, shift_two]),
+        jnp.stack([bias_one, bias_two]),
+        table_grad,
+    )
+
+
 def solution(mesh):
     in_specs = (
         P("dp", "tensor", None, None),
@@ -324,4 +897,6 @@
         P(),
         P(),
     )
+    fits = mesh.shape["tensor"] == 4 and GRID // mesh.shape["tensor"] == 16
+    shards = fast_shards if fits else general_shards
     return jax.shard_map(shards, mesh=mesh, in_specs=in_specs, out_specs=out_specs, check_vma=False)

time: 2030 us -> 865 us (0.43)
  local copies, waits for them, and re-layouts: 520 us -> 86.3 us
  matrix products: 677 us -> 255 us
  waiting for transfers between devices: 575 us -> 240 us
  Pallas kernels: 0 us -> 161 us
  blocking collectives: 115 us -> 0 us
  other arithmetic: 105 us -> 66.7 us
  starting transfers between devices: 0.61 us -> 29.6 us
    dot_general x117 -> x28, matrix products: 677 us -> 255 us  [the longest x4 36.7 us: qkv_block(): return jnp.einsum('nd,nc->dc', flat, back, preferred_element_type=f32)]
    reduce_scatter x7 -> x2, waiting for transfers between devices: 311 us -> 0.01 us  [scatter_dp(): return lax.psum_scatter(quarter, 'dp', scatter_dimension=0, tiled=True)]
    pallas_call x0 -> x4, Pallas kernels: none -> 161 us  [the longest x2 85.8 us: window_attend_back(): pl.pallas_call(backward_kernel, grid_spec=spec, out_shape=[jax.ShapeDtype...]
    reshape x9, local copies, waits for them, and re-layouts: 122 us -> 1.83 us  [the longest x1 1.07 us: fast_shards(): qkv_weight.transpose(1, 0, 2).reshape(inner, 960)]
    all_gather x7 -> x3, waiting for transfers between devices: 262 us -> 143 us  [the longest x1 82 us: fast_shards(): joint_all = lax.all_gather(joint, both, axis=0, tiled=True)]
    ppermute x0 -> x23, waiting for transfers between devices: none -> 96.7 us  [the longest x20 89.4 us: swap(): return lax.ppermute(values, 'tensor', shifts)]
    psum x2 -> x0, blocking collectives: 78.5 us -> none  [the longest x1 41 us: shards(): lax.psum((gain_acc, shift_acc, out_bias_acc, table_acc, loss_total), ('dp...]
    dot_general x20 -> x0, local copies, waits for them, and re-layouts: 64.2 us -> none  [the longest x10 33 us: score_block(): jnp.einsum('wqhc,rc->wqhr', queries, table_high, preferred_element_type=j...]
  transfers between devices with their start and end apart: 15 -> 29, of which waited for: 10 -> 12; matrix products, arithmetic and copies ran while one was open for 42% -> 39% of each run, Pallas kernels for 0% -> 19%
where the time goes in v1:
time: 865 us; the launch traced here: 856 us
  matrix products  255 us (29%)
  waiting for transfers between devices  240 us (28%)
  Pallas kernels  161 us (19%)
  local copies, waits for them, and re-layouts  86.3 us (10%)
  other arithmetic  66.7 us (8%)
  starting transfers between devices  29.6 us (3%)
  between operations  17.5 us (2%)
    ppermute x20, waiting for transfers between devices, swap(): return lax.ppermute(values, 'tensor', shifts)  89.4 us
    pallas_call x2, Pallas kernels, window_attend_back(): pl.pallas_call(backward_kernel, grid_spec=spec, out_shape=[jax.ShapeDtype...  85.8 us
    all_gather x1, waiting for transfers between devices, fast_shards(): joint_all = lax.all_gather(joint, both, axis=0, tiled=True)  82 us
    all_gather x1, waiting for transfers between devices, fast_shards(): lax.all_gather(down_shard, both, axis=0, tiled=True).reshape(4, D, 1280)  60.9 us
    pallas_call x1, Pallas kernels, window_attend(): pl.pallas_call(forward_kernel, grid_spec=spec, out_shape=jax.ShapeDtypeSt...  46.5 us
    dot_general x4, matrix products, qkv_block(): return jnp.einsum('nd,nc->dc', flat, back, preferred_element_type=f32)  36.7 us
    unnamed x154, local copies, waits for them, and re-layouts  33.8 us
    dot_general x4, matrix products, down_block(): jnp.einsum('nc,nm->cm', result_low, own(active, shard ^ p), preferred_ele...  30 us
  transfers between devices with their start and end apart: 29, of which 12 were waited for; matrix products, arithmetic and copies ran while one was open for 39% of the time, Pallas kernels for 19%

profile of v1, /device:TPU:0, one launch (start us, length us, event | category | flops | bytes accessed | tf_op | source)
XLA Modules:
  0.0 855.5 jit_solution(4613107285801820648)
XLA Ops:
  17.0 4.0 collective-permute-start
  27.3 4.6 convolution_convert_fusion.4
  31.9 82.0 %all-gather.4.cloned.1.call-done = bf16[5120,1280]{1,0:T(8,128)(2,1)} async-done(((bf16[160,1280]{1,0:T(8,128)(2,1)}), bf16[5120,1280]{1,0:T(8,128)(2,1)}) %all-gather.4.cloned.1.call-update) | async-done | bytes 13107216 | tf_op jit(solution)/shard_map/all_gather | solution.py:690
  122.4 28.7 %project.1 = bf16[4,2240,960]{2,1,0:T(8,128)(2,1)} custom-call(s32[1]{0:T(128)} %bitcast.1.shard_ref, bf16[2240,1280]{1,0:T(8,128)(2,1)S(1)} %bitcast.248, bf16[4,1280,1280]{2,1,0:T(8,128)(2,1)} %bitcast.260, f32[4,1,960]{2,1,0:T(1,128)S(1)} %maximum_convert_fusion.bias_ref), custom_call_target="tpu_custom_call" | custom-call | flops 1000000 | bytes 1000000 | tf_op jit(solution)/shard_map/project/pallas_call | solution.py:588
  151.1 46.5 %attend.1 = bf16[16,80,1280]{2,1,0:T(8,128)(2,1)S(1)} custom-call(s32[1]{0:T(128)} %bitcast.1.shard_ref, bf16[4,28,80,960]{3,2,1,0:T(8,128)(2,1)} %bitcast.256, bf16[256,384]{1,0:T(8,128)(2,1)S(1)} %pad.34.table_ref, bf16[4,224,256]{2,1,0:T(8,128)(2,1)S(1)} %copy-done.1), custom_call_target="tpu_custom_call" | custom-call | flops 1000000 | bytes 1000000 | tf_op jit(solution)/shard_map/attend/pallas_call | solution.py:452
  200.1 5.3 dynamic-slice_bitcast_fusion
  213.6 6.7 concatenate.51
  220.4 6.6 fusion.124
  230.3 21.9 %fusion.8 = (bf16[4,1024,1280]{2,1,0:T(8,128)(2,1)}, f32[4,1280,1024]{1,2,0:T(8,128)}) fusion(f32[4,1280]{1,0:T(4,128)S(1)} %fusion.97, bf16[4,1280,1280]{2,1,0:T(8,128)(2,1)} %bitcast.293, bf16[1024,1280]{1,0:T(8,128)(2,1)S(1)} %add_convert_fusion.7), kind=kOutput, calls=%fused_computation.12 | convolution fusion | flops 13453230080 | bytes 47206400 | tf_op jit(solution)/shard_map/nd,tdm->tnm/dot_general | solution.py:732
  252.2 60.9 %all-gather.8.cloned.1.call-done = bf16[5120,1280]{1,0:T(8,128)(2,1)} async-done(((bf16[160,1280]{1,0:T(8,128)(2,1)}), bf16[5120,1280]{1,0:T(8,128)(2,1)}) %all-gather.8.cloned.1.call-update) | async-done | bytes 13107216 | tf_op jit(solution)/shard_map/all_gather | solution.py:726
  313.1 23.3 %fusion.117 = (bf16[1024,1280]{1,0:T(8,128)(2,1)}, f32[1024,1280]{1,0:T(8,128)}) fusion(bf16[1,16,64,1280]{3,2,1,0:T(8,128)(2,1)} %param.18, bf16[1,16,64,1280]{3,2,1,0:T(8,128)(2,1)} %param.17, f32[1280]{0:T(1024)S(1)} %get-tuple-element.111, f32[1024,1280]{1,0:T(8,128)} %copy-done.14, bf16[4,1024,1280]{2,1,0:T(8,128)(2,1)} %get-tuple-element.158, ...), kind=kOutput, calls=%fused_computation.227 | convolution fusion | flops 13430947840 | bytes 41948160 | tf_op jit(solution)/shard_map/tnm,tcm->nc/dot_general | solution.py:737
  336.4 8.0 convolution_convert_fusion.3
  344.7 6.9 convolution_convert_fusion.2
  351.9 26.0 %fusion.120 = (f32[4,1280]{1,0:T(4,128)}, bf16[4,1024,1280]{2,1,0:T(8,128)(2,1)}) fusion(f32[4,1280,1024]{1,2,0:T(8,128)} %get-tuple-element.159, bf16[4,1280,1280]{2,1,0:T(8,128)(2,1)S(1)} %bitcast.298, bf16[1024,1280]{1,0:T(8,128)(2,1)} %get-tuple-element.31), kind=kOutput, calls=%fused_computation.229 | convolution fusion | flops 13489925120 | bytes 47206400 | tf_op jit(solution)/shard_map/nc,tcm->tnm/dot_general | solution.py:751
  377.9 8.1 add_convert_fusion.6
  386.0 7.0 add_convert_fusion.5
  393.0 5.1 convolution_convert_fusion.1
  398.1 5.1 convolution_convert_fusion
  405.2 22.8 %fusion.22 = (f32[1280]{0:T(1024)}, f32[1024]{0:T(1024)S(1)}, f32[1024]{0:T(1024)S(1)}, f32[1280]{0:T(1024)}, f32[1024,1280,1]{1,0,2:T(8,128)}) fusion(f32[1024,1280]{1,0:T(8,128)} %copy-done.14, f32[1024]{0:T(1024)S(1)} %add_rsqrt_fusion.2, f32[1024]{0:T(1024)S(1)} %broadcast_multiply_fusion.9, f32[1280]{0:T(1024)S(1)} %get-tuple-element.165, ...), kind=kOutput, calls=%fused_computation.54 | convolution fusion | flops 13433565184 | bytes 34110464 | tf_op jit(solution)/shard_map/tnm,tdm->nd/dot_general | solution.py:766
  428.0 12.1 %multiply_reduce_fusion = (f32[]{:T(128)}, f32[1280]{0:T(1024)}, f32[1280]{0:T(1024)}, f32[1024,1280]{1,0:T(8,128)S(1)}, bf16[1024,1280]{1,0:T(8,128)(2,1)}) fusion(f32[1024,1280]{1,0:T(8,128)} %get-tuple-element.161, bf16[1,16,64,1280]{3,2,1,0:T(8,128)(2,1)S(1)} %copy-done.34, bf16[1,16,64,1280]{3,2,1,0:T(8,128)(2,1)} %param.17, ...), kind=kLoop, calls=%fused_computation.66 | loop fusion | flops 22279680 | bytes 28867588 | tf_op jit(solution)/shard_map/reduce_sum | solution.py:740
  444.3 3.8 convolution_convert_fusion.8
  449.2 27.9 %collective-permute-done.10 = bf16[1280,1280]{1,0:T(8,128)(2,1)} collective-permute-done((bf16[1280,1280]{1,0:T(8,128)(2,1)}, bf16[1280,1280]{1,0:T(8,128)(2,1)}, u32[]{:S(2)}, u32[]{:S(2)}) %collective-permute-start.10) | collective-permute-done | bytes 3276832 | tf_op jit(solution)/shard_map/ppermute | solution.py:605
  477.1 4.4 add_convert_fusion.1
  481.6 8.9 %add_convert_fusion.3 = bf16[1280,1280]{1,0:T(8,128)(2,1)} fusion(bf16[1280,1280]{1,0:T(8,128)(2,1)} %collective-permute-done.8, bf16[1024,1280]{1,0:T(8,128)(2,1)} %copy-done.29, bf16[4,1024,1280]{2,1,0:T(8,128)(2,1)} %get-tuple-element.34, s32[]{:T(128)S(6)} %select_n.85), kind=kOutput, calls=%fused_computation.36 | convolution fusion | flops 3360358400 | bytes 11796484 | tf_op jit(solution)/shard_map/nd,nm->dm/dot_general | solution.py:761
  490.5 7.5 add_convert_fusion.4
  498.0 42.9 %attend_back.2 = (bf16[2,28,80,960]{3,2,1,0:T(8,128)(2,1)}, f32[256,384]{1,0:T(8,128)S(1)}) custom-call(s32[1]{0:T(128)} %bitcast.1.shard_ref, bf16[4,28,80,960]{3,2,1,0:T(8,128)(2,1)} %bitcast.257, bf16[16,80,1280]{2,1,0:T(8,128)(2,1)S(1)} %fusion.54.grad_ref, bf16[256,384]{1,0:T(8,128)(2,1)S(1)} %copy-done.4, bf16[256,384]{1,0:T(8,128)(2,1)S(1)} %pad.36.back_ref, ...), custom_call_target="tpu_custom_call" | custom-call | flops 1000000 | bytes 1000000 | tf_op jit(solution)/shard_map/attend_back/pallas_call | solution.py:556
  541.0 9.4 %fusion.121 = (bf16[1,28,80,960]{3,2,1,0:T(8,128)(2,1)}, bf16[1,28,80,960]{3,2,1,0:T(8,128)(2,1)}) fusion(bf16[2,28,80,960]{3,2,1,0:T(8,128)(2,1)} %get-tuple-element.36), kind=kLoop, calls=%fused_computation.230 | loop fusion | bytes 17203200 | tf_op jit(solution)/shard_map/slice | solution.py:798
  550.4 8.7 %convolution_convert_fusion.9 = bf16[1280,960]{0,1:T(8,128)(2,1)S(1)} fusion(bf16[2240,1280]{1,0:T(8,128)(2,1)S(1)} %bitcast.251, bf16[2240,960]{1,0:T(8,128)(2,1)} %bitcast.275), kind=kOutput, calls=%fused_computation.105 | convolution fusion | flops 5506252800 | bytes 12492800 | tf_op jit(solution)/shard_map/nd,nc->dc/dot_general | solution.py:796
  567.2 8.1 add_convert_fusion.9
  575.4 42.9 %attend_back.3 = (bf16[2,28,80,960]{3,2,1,0:T(8,128)(2,1)}, f32[256,384]{1,0:T(8,128)S(1)}) custom-call(s32[1]{0:T(128)} %bitcast.1.shard_ref, bf16[4,28,80,960]{3,2,1,0:T(8,128)(2,1)} %bitcast.258, bf16[16,80,1280]{2,1,0:T(8,128)(2,1)S(1)} %fusion.54.grad_ref, bf16[256,384]{1,0:T(8,128)(2,1)S(1)} %copy-done.4, bf16[256,384]{1,0:T(8,128)(2,1)S(1)} %pad.36.back_ref, ...), custom_call_target="tpu_custom_call" | custom-call | flops 1000000 | bytes 1000000 | tf_op jit(solution)/shard_map/attend_back/pallas_call | solution.py:556
  619.0 15.7 %collective-permute-done.9 = bf16[1280,1280]{1,0:T(8,128)(2,1)} collective-permute-done((bf16[1280,1280]{1,0:T(8,128)(2,1)}, bf16[1280,1280]{1,0:T(8,128)(2,1)}, u32[]{:S(2)}, u32[]{:S(2)}) %collective-permute-start.9) | collective-permute-done | bytes 3276832 | tf_op jit(solution)/shard_map/ppermute | solution.py:605
  634.7 4.6 add_convert_fusion.2
  639.4 11.1 %fusion.51 = bf16[1280,960]{0,1:T(8,128)(2,1)} fusion(bf16[2240,1280]{1,0:T(8,128)(2,1)} %bitcast.247, bf16[2,2240,960]{2,1,0:T(8,128)(2,1)} %bitcast.264), kind=kOutput, calls=%fused_computation.106 | convolution fusion | flops 5506252800 | bytes 12779520 | tf_op jit(solution)/shard_map/nd,nc->dc/dot_general | solution.py:796
  651.0 3.7 convolution_convert_fusion.10
  668.0 4.5 copy.84
  675.1 4.5 copy.86
  683.2 8.8 %add_convert_fusion.8 = bf16[1280,960]{0,1:T(8,128)(2,1)S(1)} fusion(bf16[1280,960]{0,1:T(8,128)(2,1)} %collective-permute-done.13, bf16[2240,1280]{1,0:T(8,128)(2,1)S(1)} %bitcast.255, bf16[2,2240,960]{2,1,0:T(8,128)(2,1)} %bitcast.265), kind=kOutput, calls=%fused_computation.84 | convolution fusion | flops 5508710400 | bytes 15237120 | tf_op jit(solution)/shard_map/nd,nc->dc/dot_general | solution.py:796
  692.0 38.1 %collective-permute-done.15 = bf16[1280,1280]{0,1:T(8,128)(2,1)} collective-permute-done((bf16[1280,1280]{0,1:T(8,128)(2,1)}, bf16[1280,1280]{0,1:T(8,128)(2,1)}, u32[]{:S(2)}, u32[]{:S(2)}) %collective-permute-start.15) | collective-permute-done | bytes 3276832 | tf_op jit(solution)/shard_map/ppermute | solution.py:605
  736.4 17.9 %convolution_bitcast_fusion.1 = f32[2240,1280]{1,0:T(8,128)} fusion(bf16[2,2240,960]{2,1,0:T(8,128)(2,1)} %bitcast.262, bf16[1,1280,960]{1,2,0:T(8,128)(2,1)} %bitcast.283, bf16[1,1280,960]{1,2,0:T(8,128)(2,1)} %bitcast.284), kind=kOutput, calls=%fused_computation.18 | convolution fusion | flops 11012505600 | bytes 24985600 | tf_op jit(solution)/shard_map/tnc,tdc->nd/dot_general | solution.py:823
  754.3 16.6 %fusion.10 = bf16[2240,1280]{1,0:T(8,128)(2,1)} fusion(f32[2240,1280]{1,0:T(8,128)} %convolution_bitcast_fusion.1, bf16[2,2240,960]{2,1,0:T(8,128)(2,1)S(1)} %bitcast.269, bf16[1,1280,960]{1,2,0:T(8,128)(2,1)S(1)} %bitcast.285, bf16[1,1280,960]{1,2,0:T(8,128)(2,1)} %bitcast.286), kind=kOutput, calls=%fused_computation.21 | convolution fusion | flops 11018240000 | bytes 30720000 | tf_op jit(solution)/shard_map/tnc,tdc->nd/dot_general | solution.py:824
  771.6 4.1 bitcast_dynamic-update-slice_fusion
  786.6 5.5 convert_reduce_fusion
  792.1 5.9 convert_reduce_fusion.1
  798.3 6.9 multiply_reduce_fusion.1
  806.0 6.4 collective-permute-start.18
  819.6 3.8 collective-permute-done.20
  824.4 3.5 collective-permute-done.21
  829.4 6.4 fusion.21
  (339 shorter events, 113.8 us)
Async XLA Ops:
  7.2 106.7 %all-gather.4.cloned.1.call-start = ((), (), s32[]{:S(2)}) async-start(), calls=%async_computation.3 | async-start | bytes 13516800 | tf_op jit(solution)/shard_map/all_gather | solution.py:690
  11.6 218.7 %all-gather.6.cloned.1.call-start = ((), (), s32[]{:S(2)}) async-start(), calls=%async_computation.4 | async-start | bytes 13516800 | tf_op jit(solution)/shard_map/all_gather | solution.py:718
  14.7 7.9 collective-permute-start.1
  17.0 5.5 collective-permute-start
  27.2 86.8 %copy-start.53 = (bf16[2,320]{1,0:T(2,128)(2,1)S(1)}, bf16[2,320]{1,0:T(2,128)(2,1)}, u32[]{:S(2)}) copy-start(bf16[2,320]{1,0:T(2,128)(2,1)} %param.23) | copy-start | bytes 3844
  27.3 87.0 %copy-start.52 = (bf16[1280]{0:T(1024)(128)(2,1)S(1)}, bf16[1280]{0:T(1024)(128)(2,1)}, u32[]{:S(2)}) copy-start(bf16[1280]{0:T(1024)(128)(2,1)} %param.24) | copy-start | bytes 7684
  27.3 89.2 %copy-start.43 = (bf16[2,27,80]{2,0,1:T(2,128)(2,1)S(1)}, bf16[2,27,80]{2,0,1:T(2,128)(2,1)}, u32[]{:S(2)}) copy-start(bf16[2,27,80]{2,0,1:T(2,128)(2,1)} %param.28) | copy-start | bytes 25924
  114.0 199.2 %all-gather.8.cloned.1.call-start = ((), (), s32[]{:S(2)}) async-start(), calls=%async_computation.5 | async-start | bytes 13516800 | tf_op jit(solution)/shard_map/all_gather | solution.py:726
  114.5 3.0 collective-permute-start.4
  115.9 3.6 collective-permute-start.3
  116.4 3.1 collective-permute-start.2
  117.4 33.7 %copy-start.3 = (bf16[256,384]{1,0:T(8,128)(2,1)}, bf16[256,384]{1,0:T(8,128)(2,1)S(1)}, u32[]{:S(2)}) copy-start(bf16[256,384]{1,0:T(8,128)(2,1)S(1)} %pad.34.table_ref) | copy-start | bytes 589828
  122.4 28.7 %copy-start.1 = (bf16[4,224,256]{2,1,0:T(8,128)(2,1)S(1)}, bf16[4,224,256]{2,1,0:T(8,128)(2,1)}, u32[]{:S(2)}) copy-start(bf16[4,224,256]{2,1,0:T(8,128)(2,1)} %constant.148.clone.select_ref) | copy-start | bytes 1376260
  199.9 616.2 %reduce-scatter.8.cloned.1.call-start = ((), (), s32[]{:S(2)}) async-start(), calls=%async_computation.7 | async-start | bytes 3686400 | tf_op jit(solution)/shard_map/reduce_scatter | solution.py:629
  230.3 167.8 %copy-start.29 = (bf16[1024,1280]{1,0:T(8,128)(2,1)}, bf16[1024,1280]{1,0:T(8,128)(2,1)S(1)}, u32[]{:S(2)}) copy-start(bf16[1024,1280]{1,0:T(8,128)(2,1)S(1)} %add_convert_fusion.7) | copy-start | bytes 7864324
  336.4 15.5 %slice-start.9 = ((s8[13107200]{0:T(1024)(128)(4,1)}), s8[4194304]{0:T(1024)(128)(4,1)S(1)}, s32[]{:S(2)}) async-start(s8[13107200]{0:T(1024)(128)(4,1)} %bitcast.296), calls=%async_computation.18 | async-start | bytes 8388608
  336.4 15.5 %slice-start.10 = ((s8[13107200]{0:T(1024)(128)(4,1)}), s8[4194304]{0:T(1024)(128)(4,1)S(1)}, s32[]{:S(2)}) async-start(s8[13107200]{0:T(1024)(128)(4,1)} %bitcast.296), calls=%async_computation.19 | async-start | bytes 8388608
  344.4 33.5 %collective-permute-start.5 = (bf16[1280,1280]{1,0:T(8,128)(2,1)}, bf16[1280,1280]{1,0:T(8,128)(2,1)S(1)}, u32[]{:S(2)}, u32[]{:S(2)}) collective-permute-start(bf16[1280,1280]{1,0:T(8,128)(2,1)} %convolution_convert_fusion.3), channel_id=1, source_target_pairs={{0,1},{1,0},{2,3},{3,2},{4,5},{5,4},{6,7},{7,6},{8,9},{9,8},{10,11... | collective-permute-start | bytes 9830408 | tf_op jit(solution)/shard_map/ppermute | solution.py:605
  351.6 34.4 %collective-permute-start.6 = (bf16[1280,1280]{1,0:T(8,128)(2,1)}, bf16[1280,1280]{1,0:T(8,128)(2,1)S(1)}, u32[]{:S(2)}, u32[]{:S(2)}) collective-permute-start(bf16[1280,1280]{1,0:T(8,128)(2,1)} %convolution_convert_fusion.2), channel_id=1, source_target_pairs={{0,1},{1,0},{2,3},{3,2},{4,5},{5,4},{6,7},{7,6},{8,9},{9,8},{10,11... | collective-permute-start | bytes 9830408 | tf_op jit(solution)/shard_map/ppermute | solution.py:605
  377.9 15.1 %slice-start.13 = ((s8[10485760]{0:T(1024)(128)(4,1)}), s8[4194304]{0:T(1024)(128)(4,1)S(1)}, s32[]{:S(2)}) async-start(s8[10485760]{0:T(1024)(128)(4,1)} %bitcast.299), calls=%async_computation.22 | async-start | bytes 8388608
  377.9 15.1 %slice-start.14 = ((s8[10485760]{0:T(1024)(128)(4,1)}), s8[4194304]{0:T(1024)(128)(4,1)S(1)}, s32[]{:S(2)}) async-start(s8[10485760]{0:T(1024)(128)(4,1)} %bitcast.299), calls=%async_computation.23 | async-start | bytes 8388608
  403.2 24.8 %copy-start.34 = (bf16[1,16,64,1280]{3,2,1,0:T(8,128)(2,1)S(1)}, bf16[1,16,64,1280]{3,2,1,0:T(8,128)(2,1)}, u32[]{:S(2)}) copy-start(bf16[1,16,64,1280]{3,2,1,0:T(8,128)(2,1)} %param.18) | copy-start | bytes 7864324
  403.2 78.4 %collective-permute-start.8 = (bf16[1280,1280]{1,0:T(8,128)(2,1)}, bf16[1280,1280]{1,0:T(8,128)(2,1)}, u32[]{:S(2)}, u32[]{:S(2)}) collective-permute-start(bf16[1280,1280]{1,0:T(8,128)(2,1)} %convolution_convert_fusion.1), channel_id=1, source_target_pairs={{0,1},{1,0},{2,3},{3,2},{4,5},{5,4},{6,7},{7,6},{8,9},{9,8},{10,11... | collective-permute-start | bytes 9830408 | tf_op jit(solution)/shard_map/ppermute | solution.py:605
  403.5 87.1 %collective-permute-start.7 = (bf16[1280,1280]{1,0:T(8,128)(2,1)}, bf16[1280,1280]{1,0:T(8,128)(2,1)}, u32[]{:S(2)}, u32[]{:S(2)}) collective-permute-start(bf16[1280,1280]{1,0:T(8,128)(2,1)} %convolution_convert_fusion), channel_id=1, source_target_pairs={{0,1},{1,0},{2,3},{3,2},{4,5},{5,4},{6,7},{7,6},{8,9},{9,8},{10,11... | collective-permute-start | bytes 9830408 | tf_op jit(solution)/shard_map/ppermute | solution.py:605
  403.7 73.4 %collective-permute-start.10 = (bf16[1280,1280]{1,0:T(8,128)(2,1)}, bf16[1280,1280]{1,0:T(8,128)(2,1)}, u32[]{:S(2)}, u32[]{:S(2)}) collective-permute-start(bf16[1280,1280]{1,0:T(8,128)(2,1)} %add_convert_fusion.6), channel_id=1, source_target_pairs={{0,2},{2,0},{1,3},{3,1},{4,6},{6,4},{5,7},{7,5},{8,10},{10,8},{9,1... | collective-permute-start | bytes 9830408 | tf_op jit(solution)/shard_map/ppermute | solution.py:605
  448.1 29.0 %copy-start.26 = (bf16[1280,1280]{1,0:T(8,128)(2,1)S(1)}, bf16[1280,1280]{1,0:T(8,128)(2,1)}, u32[]{:S(2)}) copy-start(bf16[1280,1280]{1,0:T(8,128)(2,1)} %add_convert_fusion.5) | copy-start | bytes 9830404
  481.5 359.6 %reduce-scatter.6.cloned.1.call-start = ((), (), s32[]{:S(2)}) async-start(), calls=%async_computation.6 | async-start | bytes 3686400 | tf_op jit(solution)/shard_map/reduce_scatter | solution.py:629
  490.5 59.9 %slice-start = ((s8[5734400]{0:T(1024)(128)(4,1)}), s8[4194304]{0:T(1024)(128)(4,1)S(1)}, s32[]{:S(2)}) async-start(s8[5734400]{0:T(1024)(128)(4,1)} %bitcast.249), calls=%async_computation.9 | async-start | bytes 8388608
  498.0 52.4 %slice-start.1 = ((s8[5734400]{0:T(1024)(128)(4,1)}), s8[1540096]{0:T(1024)(128)(4,1)S(1)}, s32[]{:S(2)}) async-start(s8[5734400]{0:T(1024)(128)(4,1)} %bitcast.249), calls=%async_computation.10 | async-start | bytes 3080192
  559.2 8.0 collective-permute-start.11
  561.0 4.1 collective-permute-start.12
  561.2 73.6 %collective-permute-start.9 = (bf16[1280,1280]{1,0:T(8,128)(2,1)}, bf16[1280,1280]{1,0:T(8,128)(2,1)}, u32[]{:S(2)}, u32[]{:S(2)}) collective-permute-start(bf16[1280,1280]{1,0:T(8,128)(2,1)} %add_convert_fusion.3), channel_id=1, source_target_pairs={{0,2},{2,0},{1,3},{3,1},{4,6},{6,4},{5,7},{7,5},{8,10},{10,8},{9,1... | collective-permute-start | bytes 9830408 | tf_op jit(solution)/shard_map/ppermute | solution.py:605
  575.4 59.4 %copy-start.27 = (bf16[1280,1280]{1,0:T(8,128)(2,1)S(1)}, bf16[1280,1280]{1,0:T(8,128)(2,1)}, u32[]{:S(2)}) copy-start(bf16[1280,1280]{1,0:T(8,128)(2,1)} %add_convert_fusion.4) | copy-start | bytes 9830404
  639.4 203.6 %reduce-scatter.10.cloned.1.call-start = ((), (), s32[]{:S(2)}) async-start(), calls=%async_computation.8 | async-start | bytes 3686400
  650.5 32.6 %collective-permute-start.13 = (bf16[1280,960]{0,1:T(8,128)(2,1)}, bf16[1280,960]{0,1:T(8,128)(2,1)}, u32[]{:S(2)}, u32[]{:S(2)}) collective-permute-start(bf16[1280,960]{0,1:T(8,128)(2,1)} %fusion.51), channel_id=1, source_target_pairs={{0,1},{1,0},{2,3},{3,2},{4,5},{5,4},{6,7},{7,6},{8,9},{9,8},{10,11... | collective-permute-start | bytes 7372808 | tf_op jit(solution)/shard_map/ppermute | solution.py:605
  654.6 25.0 %collective-permute-start.14 = (bf16[1280,320]{0,1:T(8,128)(2,1)}, bf16[1280,320]{0,1:T(8,128)(2,1)}, u32[]{:S(2)}, u32[]{:S(2)}) collective-permute-start(bf16[1280,320]{0,1:T(8,128)(2,1)} %convolution_convert_fusion.10), channel_id=1, source_target_pairs={{0,1},{1,0},{2,3},{3,2},{4,5},{5,4},{6,7},{7,6},{8,9},{9,8},{10,11... | collective-permute-start | bytes 2457608 | tf_op jit(solution)/shard_map/ppermute | solution.py:605
  656.8 73.4 %collective-permute-start.15 = (bf16[1280,1280]{0,1:T(8,128)(2,1)}, bf16[1280,1280]{0,1:T(8,128)(2,1)}, u32[]{:S(2)}, u32[]{:S(2)}) collective-permute-start(bf16[1280,1280]{0,1:T(8,128)(2,1)} %pad_maximum_fusion), channel_id=1, source_target_pairs={{0,2},{2,0},{1,3},{3,1},{4,6},{6,4},{5,7},{7,5},{8,10},{10,8},{9,1... | collective-permute-start | bytes 9830408 | tf_op jit(solution)/shard_map/ppermute | solution.py:605
  736.3 18.0 %slice-start.4 = ((s8[9175040]{0:T(1024)(128)(4,1)}), s8[786432]{0:T(1024)(128)(4,1)S(1)}, s32[]{:S(2)}) async-start(s8[9175040]{0:T(1024)(128)(4,1)} %bitcast.267), calls=%async_computation.13 | async-start | bytes 1572864
  736.4 17.9 %slice-start.5 = ((s8[9175040]{0:T(1024)(128)(4,1)}), s8[4194304]{0:T(1024)(128)(4,1)S(1)}, s32[]{:S(2)}) async-start(s8[9175040]{0:T(1024)(128)(4,1)} %bitcast.267), calls=%async_computation.14 | async-start | bytes 8388608
  736.4 17.9 %slice-start.6 = ((s8[9175040]{0:T(1024)(128)(4,1)}), s8[4194304]{0:T(1024)(128)(4,1)S(1)}, s32[]{:S(2)}) async-start(s8[9175040]{0:T(1024)(128)(4,1)} %bitcast.267), calls=%async_computation.15 | async-start | bytes 8388608
  736.4 17.9 %copy-start.36 = (bf16[1280,960]{0,1:T(8,128)(2,1)S(1)}, bf16[1280,960]{0,1:T(8,128)(2,1)}, u32[]{:S(2)}) copy-start(bf16[1280,960]{0,1:T(8,128)(2,1)} %copy.87) | copy-start | bytes 7372804
  779.7 18.6 %collective-permute-start.17 = (bf16[12,64,1280]{2,1,0:T(8,128)(2,1)}, bf16[12,64,1280]{2,1,0:T(8,128)(2,1)}, u32[]{:S(2)}, u32[]{:S(2)}) collective-permute-start(bf16[12,64,1280]{2,1,0:T(8,128)(2,1)} %slice.228), channel_id=1, source_target_pairs={{0,1},{1,2},{2,3},{4,5},{5,6},{6,7},{8,9},{9,10},{10,11},{12,13},{... | collective-permute-start | bytes 5898248 | tf_op jit(solution)/shard_map/ppermute | solution.py:605
  785.3 12.9 %collective-permute-start.16 = (bf16[6,64,1280]{2,1,0:T(8,128)(2,1)}, bf16[6,64,1280]{2,1,0:T(8,128)(2,1)}, u32[]{:S(2)}, u32[]{:S(2)}) collective-permute-start(bf16[6,64,1280]{2,1,0:T(8,128)(2,1)} %slice.227), channel_id=1, source_target_pairs={{1,0},{2,1},{3,2},{5,4},{6,5},{7,6},{9,8},{10,9},{11,10},{13,12},{... | collective-permute-start | bytes 2949128 | tf_op jit(solution)/shard_map/ppermute | solution.py:605
  806.0 7.3 collective-permute-start.18
  813.3 5.5 collective-permute-start.19
  818.9 4.5 collective-permute-start.20
  823.4 4.5 collective-permute-start.21
  827.9 8.0 collective-permute-start.22
  (53 other events, 335.8 us)
Sparse Core Ops, SparseCore 0:
  11.8 102.1 all-gather.3
  116.8 96.7 all-gather.5
  216.4 96.6 all-gather.7
  481.6 74.3 reduce-scatter.7
  639.5 74.1 reduce-scatter.5
  736.5 74.2 reduce-scatter.9

commit v2 on v1

--- a/solution.py
+++ b/solution.py
@@ -350,9 +350,9 @@
 
 
 def head_mask(values, head, low):
-    lane = lane_iota(values.shape) + low
+    lane = lane_iota((1, values.shape[1])) + low
     inside = (lane >= HEAD_DIM * head) & (lane < HEAD_DIM * head + HEAD_DIM)
-    return jnp.where(inside, values, jnp.zeros_like(values))
+    return values * inside.astype(jnp.float32).astype(jnp.bfloat16)
 
 
 def shift_lanes(values, amount):
@@ -362,11 +362,17 @@
 
 def load_group(qkv_ref, part, first):
     rows = qkv_ref.shape[1]
-    q = qkv_ref[part, first:first + 16, :, 0:384].reshape(16 * SIDE, 384)
+    q = qkv_ref[part, pl.ds(first, 16), :, 0:384].reshape(16 * SIDE, 384)
     k = qkv_ref[part, :, :, 256:640].reshape(rows * SIDE, 384)
     k = shift_lanes(k, -64).astype(jnp.bfloat16)
     v = qkv_ref[part, :, :, 640:960].reshape(rows * SIDE, 320)
     return q, k, v
+
+
+def by_side(values, first):
+    row = lax.broadcasted_iota(jnp.int32, (16 * SIDE, 1), 0)
+    upper = (row < (WIN - first) * SIDE).astype(jnp.float32)
+    return values * upper.astype(jnp.bfloat16), values * (1.0 - upper).astype(jnp.bfloat16)
 
 
 def bias_rows(q, tables, first):
@@ -375,9 +381,9 @@
     pieces = []
     lane = lane_iota((SIDE, 128)) % 32
     for row in range(16):
-        ih = (first + row) % WIN
+        ih = lax.rem(first + row, WIN)
         rows = slice(row * SIDE, (row + 1) * SIDE)
-        up = pltpu.roll(high[rows], (ih - 13) % 128, 1)
+        up = pltpu.roll(high[rows], lax.rem(ih + 115, 128), 1)
         across = pltpu.roll(wide[rows], 3, 1, stride=1, stride_axis=0)
         both = jnp.where(lane < 16, up, across)
         pieces.append(jnp.where(lane == 14, 1.0, both))
@@ -387,34 +393,47 @@
     return jnp.concatenate([upper, lower], axis=1)
 
 
-def softmax_rows(q, k, bias, select, head, split):
+def beside(upper, lower):
+    return jnp.concatenate([upper, lower], axis=1)
+
+
+def softmax_rows(q_sides, keys, bias, select, head):
     low, high = SLABS[head]
-    left = jnp.concatenate([q[:, low:high], bias], axis=1)
-    sides = []
-    for side, rows in ((0, slice(0, split)), (1, slice(split, 16 * SIDE))):
-        keys = head_mask(k[side * KEYS:(side + 1) * KEYS, low:high], head, low)
-        sides.append(dot(left[rows], jnp.concatenate([keys, select], axis=1), NT))
-    scores = jnp.concatenate(sides)
+    left = jnp.concatenate([q_sides[0][:, low:high], q_sides[1][:, low:high], bias], axis=1)
+    right = jnp.concatenate([keys[:KEYS], keys[KEYS:], select], axis=1)
+    scores = dot(left, right, NT)
     top = jnp.max(scores, axis=1, keepdims=True)
     raised = jnp.exp2((scores - top) * (SCALE * LOG2E))
     total = jnp.sum(raised, axis=1, keepdims=True)
     return raised * (1.0 / total)
 
 
-def forward_body(first, qkv_ref, table_ref, select_ref, out_ref, acc):
-    split = (WIN - first) * SIDE
+def pick_side(both, first):
+    width = both.shape[1] // 2
+    row = lax.broadcasted_iota(jnp.int32, (16 * SIDE, 1), 0)
+    return jnp.where(row < (WIN - first) * SIDE, both[:, :width], both[:, width:])
+
+
+def pad_lanes(values, width):
+    missing = width - values.shape[1]
+    if missing == 0:
+        return values
+    return jnp.concatenate([values, jnp.zeros((values.shape[0], missing), values.dtype)], axis=1)
+
+
+def forward_kernel(shard_ref, qkv_ref, table_ref, select_ref, out_ref, acc):
+    first = 2 * shard_ref[0]
     for part in range(2):
         q, k, v = load_group(qkv_ref, part, first)
+        q_sides = by_side(q, first)
         bias = bias_rows(q, table_ref[...], first)
+        v = pad_lanes(v, 384)
         for head in range(GROUP):
             low, high = SLABS[head]
-            high = min(high, 320)
-            probs = softmax_rows(q, k, bias, select_ref[head], head, split).astype(jnp.bfloat16)
-            sides = []
-            for side, rows in ((0, slice(0, split)), (1, slice(split, 16 * SIDE))):
-                values = head_mask(v[side * KEYS:(side + 1) * KEYS, low:high], head, low)
-                sides.append(dot(probs[rows], values, NN))
-            piece = jnp.concatenate(sides)
+            keys = head_mask(k[:, low:high], head, low)
+            probs = softmax_rows(q_sides, keys, bias, select_ref[head], head).astype(jnp.bfloat16)
+            values = head_mask(v[:, low:high], head, low)
+            piece = pick_side(dot(probs, beside(values[:KEYS], values[KEYS:]), NN), first)
             if head == 0:
                 acc[part, :, 0:128] = piece
                 acc[part, :, 128:384] = jnp.zeros((16 * SIDE, 256), jnp.float32)
@@ -426,17 +445,6 @@
     out_ref[...] = whole.astype(jnp.bfloat16).reshape(16, SIDE, 640)
 
 
-def by_shard(shard_ref, body):
-    for shard in range(4):
-        @pl.when(shard_ref[0] == shard)
-        def _():
-            body(2 * shard)
-
-
-def forward_kernel(shard_ref, qkv_ref, table_ref, select_ref, out_ref, acc):
-    by_shard(shard_ref, lambda first: forward_body(first, qkv_ref, table_ref, select_ref, out_ref, acc))
-
-
 def window_attend(shard, qkv, tables, select):
     spec = pltpu.PrefetchScalarGridSpec(
         num_scalar_prefetch=1,
@@ -454,81 +462,82 @@
         grid_spec=spec,
         out_shape=jax.ShapeDtypeStruct((16, 5 * SIDE, 1280), jnp.bfloat16),
         compiler_params=pltpu.CompilerParams(vmem_limit_bytes=48 << 20),
-        cost_estimate=pl.CostEstimate(flops=1_000_000, bytes_accessed=1_000_000, transcendentals=0),
+        cost_estimate=pl.CostEstimate(flops=50_000_000_000, bytes_accessed=20_000_000, transcendentals=0),
         name="attend",
     )(shard, qkv, tables, select)
 
 
-def backward_body(first, qkv_ref, grad_ref, table_ref, back_ref, select_ref, spread_ref, out_ref, sums_ref, dq, dk, dv):
-    split = (WIN - first) * SIDE
+def backward_kernel(
+    shard_ref, qkv_ref, grad_ref, table_ref, back_ref, select_ref, spread_ref, own_ref, other_ref, sums_ref, dq, dk, dv
+):
+    first = 2 * shard_ref[0]
     queries = 16 * SIDE
-    ranges = ((0, slice(0, split)), (1, slice(split, queries)))
-    zero = jnp.zeros((queries, 128), jnp.float32)
+
+    @pl.when(pl.program_id(0) == 0)
+    def _():
+        sums_ref[...] = jnp.zeros_like(sums_ref)
+
     lane = lane_iota((SIDE, 128)) % 32
-    for part in range(2):
+    for part, out_ref in enumerate((own_ref, other_ref)):
         q, k, v = load_group(qkv_ref, part, first)
+        v = pad_lanes(v, 384)
         if part == 0:
             go = grad_ref[:, :, 0:384].reshape(queries, 384)
         else:
             go = shift_lanes(grad_ref[:, :, 256:640].reshape(queries, 384), -64).astype(jnp.bfloat16)
+        q_sides = by_side(q, first)
+        go_sides = by_side(go, first)
         bias = bias_rows(q, table_ref[...], first)
         dq[...] = jnp.zeros_like(dq)
         dk[...] = jnp.zeros_like(dk)
         dv[...] = jnp.zeros_like(dv)
-        marks = zero
+        marks = jnp.zeros((queries, 128), jnp.float32)
         for head in range(GROUP):
             low, high = SLABS[head]
-            vhigh = min(high, 320)
-            probs = softmax_rows(q, k, bias, select_ref[head], head, split)
+            keys = head_mask(k[:, low:high], head, low)
+            values = head_mask(v[:, low:high], head, low)
+            probs = softmax_rows(q_sides, keys, bias, select_ref[head], head)
             probs_low = probs.astype(jnp.bfloat16)
-            sides = []
-            for side, rows in ranges:
-                values = head_mask(v[side * KEYS:(side + 1) * KEYS, low:vhigh], head, low)
-                sides.append(dot(go[rows, low:vhigh], values, NT))
-            probs_grad = jnp.concatenate(sides)
+            go_both = beside(go_sides[0][:, low:high], go_sides[1][:, low:high])
+            probs_grad = dot(go_both, beside(values[:KEYS], values[KEYS:]), NT)
             weighted = probs * probs_grad
             scores_grad = weighted - probs * jnp.sum(weighted, axis=1, keepdims=True)
             scores_low = scores_grad.astype(jnp.bfloat16)
-            go_head = head_mask(go[:, low:high], head, low)
-            q_head = head_mask(q[:, low:high], head, low)
-            for side, rows in ranges:
+            width = high - low
+            go_head = beside(*(head_mask(side[:, low:high], head, low) for side in go_sides))
+            q_head = beside(*(head_mask(side[:, low:high], head, low) for side in q_sides))
+            value_grad = dot(probs_low, go_head, TN)
+            key_grad = dot(scores_low, q_head, TN)
+            for side in range(2):
                 span = slice(side * KEYS, (side + 1) * KEYS)
-                dv[span, low:high] += dot(probs_low[rows], go_head[rows], TN)
-                dk[span, low:high] += dot(scores_low[rows], q_head[rows], TN)
-                keys = head_mask(k[span, low:high], head, low)
-                dq[rows, low:high] += dot(scores_low[rows], keys, NN)
-            marks = marks + dot(scores_low, spread_ref[head], NN)
+                lanes = slice(side * width, (side + 1) * width)
+                dv[span, low:high] += value_grad[:, lanes]
+                dk[span, low:high] += key_grad[:, lanes]
+            back = jnp.concatenate([keys[:KEYS], keys[KEYS:], spread_ref[head]], axis=1)
+            joint = dot(scores_low, back, NN)
+            dq[:, low:high] += pick_side(joint[:, :2 * width], first)
+            marks = marks + joint[:, 2 * width:]
         highs, wides = [], []
         for row in range(16):
-            ih = (first + row) % WIN
+            ih = lax.rem(first + row, WIN)
             piece = marks[row * SIDE:(row + 1) * SIDE]
-            highs.append(pltpu.roll(jnp.where(lane < 14, piece, 0.0), (13 - ih) % 128, 1))
+            highs.append(pltpu.roll(jnp.where(lane < 14, piece, 0.0), 13 - ih, 1))
             across = jnp.where((lane >= 16) & (lane < 30), piece, 0.0)
             wides.append(pltpu.roll(across, 112, 1, stride=1, stride_axis=0))
         ranks = jnp.concatenate([jnp.concatenate(highs), jnp.concatenate(wides)], axis=1).astype(jnp.bfloat16)
-        dq_full = dq[...] * SCALE + dot(ranks, back_ref[...], NN)
+        dq_full = (dq[...] * SCALE + dot(ranks, back_ref[...], NN)).reshape(16, SIDE, 384)
         sums_ref[...] += dot(ranks, q, TN)
-        before, after = first * SIDE, (28 - 16 - first) * SIDE
-        pieces = [dq_full]
-        if before:
-            pieces = [jnp.zeros((before, 384), jnp.float32)] + pieces
-        if after:
-            pieces = pieces + [jnp.zeros((after, 384), jnp.float32)]
-        dq_all = jnp.concatenate(pieces) if len(pieces) > 1 else dq_full
         dk_all = pltpu.roll(dk[...] * SCALE, 64, 1)
         joint = lane_iota((28 * SIDE, 128))
-        middle = jnp.where(joint < 64, dq_all[:, 256:384], dk_all[:, 0:128])
-        left = jnp.concatenate([dq_all[:, 0:256], middle, dk_all[:, 128:384]], axis=1)
-        out_ref[part, :, :, 0:640] = left.astype(jnp.bfloat16).reshape(28, SIDE, 640)
-        out_ref[part, :, :, 640:960] = dv[:, 0:320].astype(jnp.bfloat16).reshape(28, SIDE, 320)
-
-
-def backward_kernel(shard_ref, qkv_ref, grad_ref, table_ref, back_ref, select_ref, spread_ref, out_ref, sums_ref, dq, dk, dv):
-    @pl.when(pl.program_id(0) == 0)
-    def _():
-        sums_ref[...] = jnp.zeros_like(sums_ref)
-
-    by_shard(shard_ref, lambda first: backward_body(first, qkv_ref, grad_ref, table_ref, back_ref, select_ref, spread_ref, out_ref, sums_ref, dq, dk, dv))
+        middle = jnp.where(joint < 64, 0.0, dk_all[:, 0:128])
+        right = jnp.concatenate([middle, dk_all[:, 128:384]], axis=1).reshape(28, SIDE, 384)
+        out_ref[:, :, 0:256] = jnp.zeros((28, SIDE, 256), jnp.bfloat16)
+        out_ref[:, :, 256:640] = right.astype(jnp.bfloat16)
+        own_rows = pl.ds(first, 16)
+        out_ref[own_rows, :, 0:256] = dq_full[:, :, 0:256].astype(jnp.bfloat16)
+        edge = out_ref[own_rows, :, 256:384].astype(jnp.float32) + dq_full[:, :, 256:384]
+        out_ref[own_rows, :, 256:384] = edge.astype(jnp.bfloat16)
+        out_ref[:, :, 640:960] = dv[:, 0:320].astype(jnp.bfloat16).reshape(28, SIDE, 320)
 
 
 def window_attend_back(pair, shard, qkv, grad, tables, back, select, spread):
@@ -544,7 +553,8 @@
             pl.BlockSpec((GROUP, KEYS, 128), lambda w, s: (0, 0, 0)),
         ],
         out_specs=[
-            pl.BlockSpec((2, 28, SIDE, 960), lambda w, s: (0, 0, w, 0)),
+            pl.BlockSpec((28, SIDE, 960), lambda w, s: (0, w, 0)),
+            pl.BlockSpec((28, SIDE, 960), lambda w, s: (0, w, 0)),
             pl.BlockSpec((256, 384), lambda w, s: (0, 0)),
         ],
         scratch_shapes=[
@@ -557,42 +567,126 @@
         backward_kernel,
         grid_spec=spec,
         out_shape=[
-            jax.ShapeDtypeStruct((2, 28, 5 * SIDE, 960), jnp.bfloat16),
+            jax.ShapeDtypeStruct((28, 5 * SIDE, 960), jnp.bfloat16),
+            jax.ShapeDtypeStruct((28, 5 * SIDE, 960), jnp.bfloat16),
             jax.ShapeDtypeStruct((256, 384), jnp.float32),
         ],
         compiler_params=pltpu.CompilerParams(vmem_limit_bytes=48 << 20),
-        cost_estimate=pl.CostEstimate(flops=1_000_000, bytes_accessed=1_000_000, transcendentals=0),
+        cost_estimate=pl.CostEstimate(flops=60_000_000_000, bytes_accessed=20_000_000, transcendentals=0),
         name="attend_back",
     )(shard, qkv, grad, tables, back, select, spread)
 
 
-def project_kernel(shard_ref, x_ref, w_ref, bias_ref, out_ref):
+def project_kernel(shard_ref, x_ref, w_ref, bias_ref, out_ref, proj_ref):
     weights = w_ref[0][:, :960]
     for start in range(0, x_ref.shape[0], 448):
         rows = slice(start, start + 448)
         out_ref[0, rows, :] = (dot(x_ref[rows, :], weights, NN) + bias_ref[0]).astype(jnp.bfloat16)
+    odd = pl.program_id(0) % 2
+
+    @pl.when(odd == 0)
+    def _():
+        proj_ref[:, 0:384] = shift_lanes(w_ref[0, :, 896:1280], -64).astype(jnp.bfloat16)
+
+    @pl.when(odd == 1)
+    def _():
+        lane = lane_iota((1, 128))
+        left = (lane < 64).astype(jnp.float32).astype(jnp.bfloat16)
+        right = (lane >= 64).astype(jnp.float32).astype(jnp.bfloat16)
+        proj_ref[:, 256:384] = proj_ref[:, 256:384] * left + w_ref[0, :, 896:1024] * right
+        proj_ref[:, 384:640] = w_ref[0, :, 1024:1280]
 
 
 def project(shard, x, weights, bias):
-    tokens = x.shape[0]
+    tokens, width = x.shape
     spec = pltpu.PrefetchScalarGridSpec(
         num_scalar_prefetch=1,
         grid=(4,),
         in_specs=[
-            pl.BlockSpec((tokens, x.shape[1]), lambda p, s: (0, 0)),
-            pl.BlockSpec((1,) + weights.shape[1:], lambda p, s: (p ^ s[0], 0, 0)),
+            pl.BlockSpec((tokens, width), lambda p, s: (0, 0)),
+            pl.BlockSpec((1, width, 1280), lambda p, s: (p ^ s[0], 0, 0)),
             pl.BlockSpec((1, 1, 960), lambda p, s: (p ^ s[0], 0, 0)),
         ],
-        out_specs=pl.BlockSpec((1, tokens, 960), lambda p, s: (p, 0, 0)),
+        out_specs=[
+            pl.BlockSpec((1, tokens, 960), lambda p, s: (p, 0, 0)),
+            pl.BlockSpec((width, 640), lambda p, s: (0, p // 2)),
+        ],
     )
     return pl.pallas_call(
         project_kernel,
         grid_spec=spec,
-        out_shape=jax.ShapeDtypeStruct((4, tokens, 960), jnp.bfloat16),
+        out_shape=[
+            jax.ShapeDtypeStruct((4, tokens, 960), jnp.bfloat16),
+            jax.ShapeDtypeStruct((width, 1280), jnp.bfloat16),
+        ],
         compiler_params=pltpu.CompilerParams(vmem_limit_bytes=48 << 20),
-        cost_estimate=pl.CostEstimate(flops=1_000_000, bytes_accessed=1_000_000, transcendentals=0),
+        cost_estimate=pl.CostEstimate(flops=24_000_000_000, bytes_accessed=35_000_000, transcendentals=0),
         name="project",
     )(shard, x, weights, bias)
+
+
+def frame_kernel(shard_ref, near_own, near_other, far_own, far_other, w_ref, fold_ref, out_ref, sums_ref):
+    total = None
+    for p, back_ref in enumerate((near_own, near_other, far_own, far_other)):
+        back = back_ref[...]
+        piece = dot(back, w_ref[p ^ shard_ref[0]][:, :960], NT)
+        total = piece if total is None else total + piece
+        column = jnp.sum(back.astype(jnp.float32), axis=0, keepdims=True)
+
+        @pl.when(pl.program_id(0) == 0)
+        def _():
+            sums_ref[p] = column
+
+        @pl.when(pl.program_id(0) > 0)
+        def _():
+            sums_ref[p] += column
+    total = total.astype(jnp.bfloat16)
+    for row in range(out_ref.shape[0]):
+        piece = total[row * 80:(row + 1) * 80, :]
+        out_ref[row] = dot(fold_ref[...], piece, NN).astype(jnp.bfloat16)
+
+
+def frame_back(shard, backs, weights, fold):
+    width = weights.shape[1]
+    chunk = 7
+    back_spec = pl.BlockSpec((chunk * 80, 960), lambda g, s: (g, 0))
+    spec = pltpu.PrefetchScalarGridSpec(
+        num_scalar_prefetch=1,
+        grid=(28 // chunk,),
+        in_specs=[back_spec] * 4 + [
+            pl.BlockSpec((4, width, 1280), lambda g, s: (0, 0, 0), pipeline_mode=pl.Buffered(1)),
+            pl.BlockSpec(fold.shape, lambda g, s: (0, 0)),
+        ],
+        out_specs=[
+            pl.BlockSpec((chunk, 64, width), lambda g, s: (g, 0, 0)),
+            pl.BlockSpec((4, 1, 960), lambda g, s: (0, 0, 0)),
+        ],
+    )
+    return pl.pallas_call(
+        frame_kernel,
+        grid_spec=spec,
+        out_shape=[
+            jax.ShapeDtypeStruct((28, 64, width), jnp.bfloat16),
+            jax.ShapeDtypeStruct((4, 1, 960), jnp.float32),
+        ],
+        compiler_params=pltpu.CompilerParams(vmem_limit_bytes=58 << 20),
+        cost_estimate=pl.CostEstimate(flops=1_000_000, bytes_accessed=1_000_000, transcendentals=0),
+        name="frame_back",
+    )(shard, *backs, weights, fold)
+
+
+def turn_kernel(x_ref, out_ref):
+    out_ref[...] = x_ref[...].T
+
+
+def turn(x):
+    return pl.pallas_call(
+        turn_kernel,
+        out_shape=jax.ShapeDtypeStruct(x.shape[::-1], x.dtype),
+        compiler_params=pltpu.CompilerParams(vmem_limit_bytes=48 << 20),
+        cost_estimate=pl.CostEstimate(flops=0, bytes_accessed=12_000_000, transcendentals=0),
+        name="turn",
+    )(x)
 
 
 ROWS = 16
@@ -687,8 +781,8 @@
     tokens = ROWS * GRID
     inner = qkv_weight.shape[1]
     joint = jnp.concatenate([qkv_weight.transpose(1, 0, 2).reshape(inner, 960), proj_weight.T], axis=1)
-    joint_all = lax.all_gather(joint, both, axis=0, tiled=True)
-    joint_all = joint_all.reshape(4, D, 1280)
+    joint = jnp.concatenate([joint, up_weight], axis=1)
+    joint_all = lax.all_gather(joint, both, axis=0, tiled=True).reshape(4, D, 2560)
     biases = gather_small(jnp.concatenate([qv_bias.reshape(-1), up_bias]), shard)
     qkv_bias = jnp.concatenate(
         [biases[:, :320], jnp.zeros((4, 320), bf16), biases[:, 320:640]], axis=1
@@ -710,20 +804,18 @@
     windows = jnp.einsum("pc,rcd->rpd", select, normed, preferred_element_type=f32).astype(bf16)
     flat = windows.reshape(FRAME * NWIN * SIDE, D)
     where = shard[None].astype(jnp.int32)
-    qkv = project(where, flat, joint_all, qkv_bias[:, None, :])
+    qkv, proj_full = project(where, flat, joint_all, qkv_bias[:, None, :])
     qkv = qkv.reshape(4, FRAME, NWIN * SIDE, 960)
     tables, back_tables = bias_tables(rel_tables)
     select_keys, spread_keys = selectors()
-    (up_shard,) = after((joint_all, flat), up_weight)
-    up_all = lax.all_gather(up_shard, both, axis=0, tiled=True).reshape(4, D, 1280)
-    joint_own = [own(joint_all, shard ^ p) for p in range(4)]
-    proj_full = jnp.concatenate([part[:, 960:] for part in joint_own], axis=1)
+    flat_turned = turn(flat)
+    (down_shard,) = after((joint_all, flat_turned), down_weight.T)
+    down_all = lax.all_gather(down_shard, both, axis=0, tiled=True).reshape(4, D, 1280)
+    up_all = joint_all[:, :, 1280:]
     attended = window_attend(where, qkv, tables, select_keys)
     attended = jnp.einsum("pc,rpd->rcd", select, attended, preferred_element_type=f32)
     attended = attended.astype(bf16).reshape(tokens, D)
 
-    (down_shard,) = after(attended, down_weight.T)
-    down_all = lax.all_gather(down_shard, both, axis=0, tiled=True).reshape(4, D, 1280)
     source = image.astype(f32).reshape(tokens, D)
     branch = jnp.einsum("nk,ck->nc", attended, proj_full, preferred_element_type=f32)
     middle = source + branch + out_biases[0].astype(f32)
@@ -780,50 +872,54 @@
         part = attended[:, 320 * p:320 * p + 320]
         return jnp.einsum("nc,nk->ck", middle_low, part, preferred_element_type=f32)
 
-    proj_three = swap(proj_block(3).astype(bf16), CORES)
-    proj_one = swap(proj_block(1).astype(bf16), CORES)
+    proj_sends = (proj_block(3).astype(bf16), proj_block(1).astype(bf16))
+    proj_three, proj_one = swap(proj_sends[0], CORES), swap(proj_sends[1], CORES)
+    (down_near,) = after((up_far, up_near, proj_sends), down_near)
     down_quarter = add_low(down_near, down_side)
-    down_grad = scatter_dp(down_quarter)
     (grad_far,) = after((up_far, up_near, down_quarter), attended_grad)
-    far_back, far_sums = window_attend_back(
+    far_own, far_other, far_sums = window_attend_back(
         1, where, qkv, grad_far, tables, back_tables, select_keys, spread_keys
     )
+
+    def flatten(back):
+        return back.reshape(FRAME * NWIN * SIDE, 960)
+
+    def qkv_block(tokens_in, back):
+        return jnp.einsum("dn,nc->dc", tokens_in, back, preferred_element_type=f32)
+
+    far_own, far_other = flatten(far_own), flatten(far_other)
+    qkv_send = qkv_block(flat_turned, far_other).astype(bf16)
+    qkv_three = swap(qkv_send, CORES)
+    flat_far, up_side, _ = lax.optimization_barrier((flat_turned, up_side, qkv_send))
+    up_quarter = add_low(up_near, up_side)
+    mlp_grad = scatter_dp(jnp.concatenate([up_quarter, down_quarter], axis=1))
     proj_far = (proj_block(2) + proj_three.astype(f32)).astype(bf16)
     proj_near = (proj_block(0) + proj_one.astype(f32)).astype(bf16)
-    far_back = far_back.reshape(2, FRAME * NWIN * SIDE, 960)
-
-    def qkv_block(back):
-        return jnp.einsum("nd,nc->dc", flat, back, preferred_element_type=f32)
-
-    qkv_three = swap(qkv_block(far_back[1]).astype(bf16), CORES)
-    qkv_far = (qkv_block(far_back[0]) + qkv_three.astype(f32)).astype(bf16)
+    qkv_far = (qkv_block(flat_far, far_own) + qkv_three.astype(f32)).astype(bf16)
     far_side = swap(jnp.concatenate([qkv_far, proj_far], axis=1), SIDES)
-    (grad_near,) = after((qkv_far, proj_far), attended_grad)
-    near_back, near_sums = window_attend_back(
+    (grad_near,) = after((qkv_far, proj_far, proj_near, up_quarter), attended_grad)
+    near_own, near_other, near_sums = window_attend_back(
         0, where, qkv, grad_near, tables, back_tables, select_keys, spread_keys
     )
-    near_back = near_back.reshape(2, FRAME * NWIN * SIDE, 960)
-    up_quarter = add_low(up_near, up_side)
-    up_grad = scatter_dp(up_quarter)
-    near_back, flat = after(up_quarter, near_back, flat)
-    qkv_one = swap(qkv_block(near_back[1]).astype(bf16), CORES)
-    qkv_near = qkv_block(near_back[0]) + qkv_one.astype(f32)
+    near_own, near_other = flatten(near_own), flatten(near_other)
+    qkv_send = qkv_block(flat_turned, near_other).astype(bf16)
+    qkv_one = swap(qkv_send, CORES)
+    backs = after(qkv_send, near_own, near_other, far_own, far_other)
+    frame_grad, bias_sums = frame_back(where, backs, joint_all, select.T)
+    flat_near, far_side, _ = lax.optimization_barrier((flat_turned, far_side, frame_grad))
+    qkv_near = qkv_block(flat_near, near_own) + qkv_one.astype(f32)
     near = jnp.concatenate([qkv_near.astype(bf16), proj_near], axis=1)
     joint_quarter = add_low(near, far_side)
-    joint_grad = scatter_dp(joint_quarter)
-    near_next, far_next = after(joint_quarter, near_back, far_back)
+    mlp_grad, joint_ready = lax.optimization_barrier((mlp_grad, joint_quarter))
+    joint_grad = scatter_dp(joint_ready)
     table_sums = far_sums + near_sums
-    bias_sums = jnp.concatenate([jnp.sum(near_next.astype(f32), axis=1), jnp.sum(far_next.astype(f32), axis=1)])
+    (frame_grad,) = after(joint_quarter, frame_grad)
+    bias_sums = bias_sums[:, 0]
     qv_acc = jnp.stack([bias_sums[:, :320], bias_sums[:, 640:]], axis=1)
     qv_acc = jnp.stack([own(qv_acc, shard ^ t) for t in range(4)])
     table_sums = table_sums[:, :320].reshape(2, GROUP, 32, GROUP, HEAD_DIM)
     table_acc = jnp.einsum("phrhd->prd", table_sums)
     table_acc = jnp.stack([table_acc[0, :27][::-1], table_acc[1, :27]])
-    weights = [part[:, :960] for part in joint_own]
-    frame_grad = jnp.einsum("tnc,tdc->nd", far_next, jnp.stack(weights[2:]), preferred_element_type=f32)
-    frame_grad = frame_grad + jnp.einsum("tnc,tdc->nd", near_next, jnp.stack(weights[:2]), preferred_element_type=f32)
-    frame_grad = frame_grad.astype(bf16).reshape(FRAME, NWIN * SIDE, D)
-    frame_grad = jnp.einsum("pc,rpd->rcd", select, frame_grad, preferred_element_type=f32).astype(bf16)
     spread = jnp.zeros((EARLY + ROWS + LATE, GRID, D), bf16)
     spread = lax.dynamic_update_slice_in_dim(spread, frame_grad, EARLY - 2 * shard, 0)
     from_next = swap(spread[:EARLY], [(i + 1, i) for i in range(3)])
@@ -855,8 +951,8 @@
         loss,
         joint_grad[:, :960].reshape(inner, 3, 320).transpose(1, 0, 2).astype(f32),
         joint_grad[:, 960:].T.astype(f32),
-        up_grad.astype(f32),
-        down_grad.T.astype(f32),
+        mlp_grad[:, :1280].astype(f32),
+        mlp_grad[:, 1280:].T.astype(f32),
         own(qv_sum, shard),
         own(up_sum, shard),
         jnp.stack([gain_one, gain_two]),

time: 865 us -> 766 us (0.89)
  waiting for transfers between devices: 240 us -> 189 us
  matrix products: 255 us -> 208 us
  Pallas kernels: 161 us -> 203 us
  local copies, waits for them, and re-layouts: 86.3 us -> 50 us
  other arithmetic: 66.7 us -> 54 us
  starting transfers between devices: 29.6 us -> 38.3 us
    ppermute x20, waiting for transfers between devices: 89.4 us -> 26.7 us  [swap(): return lax.ppermute(values, 'tensor', shifts)]
    all_gather x1, waiting for transfers between devices: 60.9 us -> 0.01 us  [fast_shards(): lax.all_gather(down_shard, both, axis=0, tiled=True).reshape(4, D, 1280)]
    all_gather x2 -> x1, waiting for transfers between devices: 82 us -> 140 us  [fast_shards(): lax.all_gather(joint, both, axis=0, tiled=True).reshape(4, D, 2560)]
    pallas_call x1 -> x3, Pallas kernels: 28.7 us -> 77.8 us  [the longest x1 42.1 us: frame_back(): pl.pallas_call(frame_kernel, grid_spec=spec, out_shape=[jax.ShapeDtypeStr...]
    dot_general x7 -> x4, matrix products: 75.3 us -> 39.7 us  [qkv_block(): return jnp.einsum('dn,nc->dc', tokens_in, back, preferred_element_type=f32)]
    slice x9 -> x0, local copies, waits for them, and re-layouts: 21.9 us -> none  [the longest x1 9.42 us: fast_shards(): qkv_three = swap(qkv_block(far_back[1]).astype(bf16), CORES)]
    reduce_sum x2 -> x0, other arithmetic: 11.4 us -> none  [the longest x1 5.92 us: fast_shards(): jnp.sum(near_next.astype(f32), axis=1)]
    unnamed x154 -> x139, local copies, waits for them, and re-layouts: 33.8 us -> 23.2 us
  transfers between devices with their start and end apart: 29 -> 27, of which waited for: 12 -> 13; matrix products, arithmetic and copies ran while one was open for 39% -> 30% of each run, Pallas kernels for 19% -> 27%
where the time goes in v2:
time: 766 us; the launch traced here: 760 us
  matrix products  208 us (27%)
  Pallas kernels  203 us (27%)
  waiting for transfers between devices  189 us (25%)
  other arithmetic  54 us (7%)
  local copies, waits for them, and re-layouts  50 us (7%)
  starting transfers between devices  38.3 us (5%)
  between operations  17 us (2%)
    all_gather x1, waiting for transfers between devices, fast_shards(): lax.all_gather(joint, both, axis=0, tiled=True).reshape(4, D, 2560)  140 us
    pallas_call x2, Pallas kernels, window_attend_back(): pl.pallas_call(backward_kernel, grid_spec=spec, out_shape=[jax.ShapeDtype...  80.7 us
    pallas_call x1, Pallas kernels, window_attend(): pl.pallas_call(forward_kernel, grid_spec=spec, out_shape=jax.ShapeDtypeSt...  44.9 us
    pallas_call x1, Pallas kernels, frame_back(): pl.pallas_call(frame_kernel, grid_spec=spec, out_shape=[jax.ShapeDtypeStr...  42.1 us
    dot_general x4, matrix products, qkv_block(): return jnp.einsum('dn,nc->dc', tokens_in, back, preferred_element_type=f32)  39.7 us
    ppermute x20, starting transfers between devices, swap(): return lax.ppermute(values, 'tensor', shifts)  34.3 us
    pallas_call x1, Pallas kernels, project(): pl.pallas_call(project_kernel, grid_spec=spec, out_shape=[jax.ShapeDtypeS...  31.6 us
    dot_general x4, matrix products, down_block(): jnp.einsum('nc,nm->cm', result_low, own(active, shard ^ p), preferred_ele...  30 us
  transfers between devices with their start and end apart: 27, of which 13 were waited for; matrix products, arithmetic and copies ran while one was open for 30% of the time, Pallas kernels for 27%

profile of v2, /device:TPU:0, one launch (start us, length us, event | category | flops | bytes accessed | tf_op | source)
XLA Modules:
  0.0 759.6 jit_solution(13744074982290302782)
XLA Ops:
  14.8 4.0 collective-permute-start
  20.3 3.2 convert_reduce_fusion
  25.0 2.8 convolution_convert_fusion.4
  27.8 4.1 turn.1
  34.4 139.8 %all-gather.3.cloned.1.call-done = bf16[5120,2560]{1,0:T(8,128)(2,1)} async-done(((bf16[160,2560]{1,0:T(8,128)(2,1)}), bf16[5120,2560]{1,0:T(8,128)(2,1)}) %all-gather.3.cloned.1.call-update) | async-done | bytes 26214416 | tf_op jit(solution)/shard_map/all_gather | solution.py:785
  184.7 31.6 %project.1 = (bf16[4,2240,960]{2,1,0:T(8,128)(2,1)}, bf16[1280,1280]{1,0:T(8,128)(2,1)S(1)}) custom-call(s32[1]{0:T(128)} %bitcast.1.shard_ref, bf16[2240,1280]{1,0:T(8,128)(2,1)} %bitcast.215, bf16[4,1280,2560]{2,1,0:T(8,128)(2,1)} %bitcast.217, f32[4,1,960]{2,1,0:T(1,128)S(1)} %maximum_convert_fusion.bias_ref), custom_call_target="tpu_custom_call" | custom-call | flops 24000000000 | bytes 35000000 | tf_op jit(solution)/shard_map/project/pallas_call | solution.py:615
  216.3 44.9 %attend.1 = bf16[16,80,1280]{2,1,0:T(8,128)(2,1)S(1)} custom-call(s32[1]{0:T(128)} %bitcast.1.shard_ref, bf16[4,28,80,960]{3,2,1,0:T(8,128)(2,1)} %bitcast.250, bf16[256,384]{1,0:T(8,128)(2,1)S(1)} %pad.34.table_ref, bf16[4,224,256]{2,1,0:T(8,128)(2,1)S(1)} %copy-done.9), custom_call_target="tpu_custom_call" | custom-call | flops 49999998976 | bytes 20000000 | tf_op jit(solution)/shard_map/attend/pallas_call | solution.py:460
  262.1 3.8 fusion.105
  268.3 22.5 %fusion.8 = (bf16[4,1024,1280]{2,1,0:T(8,128)(2,1)}, f32[4,1280,1024]{1,2,0:T(8,128)}) fusion(f32[4,1280]{1,0:T(4,128)S(1)} %fusion.81, bf16[4,1280,2560]{2,1,0:T(8,128)(2,1)} %bitcast.218, bf16[1024,1280]{1,0:T(8,128)(2,1)S(1)} %add_convert_fusion.7), kind=kOutput, calls=%fused_computation.12 | convolution fusion | flops 13453230080 | bytes 47206400 | tf_op jit(solution)/shard_map/nd,tdm->tnm/dot_general | solution.py:824
  290.8 23.1 %fusion.99 = (bf16[1024,1280]{1,0:T(8,128)(2,1)}, f32[1024,1280]{1,0:T(8,128)}) fusion(bf16[1,16,64,1280]{3,2,1,0:T(8,128)(2,1)} %param.18, bf16[1,16,64,1280]{3,2,1,0:T(8,128)(2,1)} %param.17, f32[1280]{0:T(1024)S(1)} %get-tuple-element.137, f32[1024,1280]{1,0:T(8,128)} %copy-done.19, bf16[4,1024,1280]{2,1,0:T(8,128)(2,1)} %get-tuple-element.180, ...), kind=kOutput, calls=%fused_computation.207 | convolution fusion | flops 13430947840 | bytes 41948160 | tf_op jit(solution)/shard_map/tnm,tcm->nc/dot_general | solution.py:829
  313.9 8.0 %convolution_convert_fusion.3 = bf16[1280,1280]{1,0:T(8,128)(2,1)} fusion(bf16[1024,1280]{1,0:T(8,128)(2,1)} %get-tuple-element.45, bf16[4,1024,1280]{2,1,0:T(8,128)(2,1)} %get-tuple-element.180, s32[]{:T(128)S(6)} %select_n.79), kind=kOutput, calls=%fused_computation.29 | convolution fusion | flops 3357081600 | bytes 8519684 | tf_op jit(solution)/shard_map/nc,nm->cm/dot_general | solution.py:838
  323.4 6.8 convolution_convert_fusion.2
  330.4 25.8 %fusion.102 = (f32[4,1280]{1,0:T(4,128)}, bf16[4,1024,1280]{2,1,0:T(8,128)(2,1)}) fusion(f32[4,1280,1024]{1,2,0:T(8,128)} %get-tuple-element.181, bf16[4,1280,1280]{2,1,0:T(8,128)(2,1)S(1)} %bitcast.249, bf16[1024,1280]{1,0:T(8,128)(2,1)} %get-tuple-element.45), kind=kOutput, calls=%fused_computation.209 | convolution fusion | flops 13489925120 | bytes 47206400 | tf_op jit(solution)/shard_map/nc,tcm->tnm/dot_general | solution.py:843
  356.2 8.1 %add_convert_fusion.6 = bf16[1280,1280]{1,0:T(8,128)(2,1)} fusion(bf16[1280,1280]{1,0:T(8,128)(2,1)S(1)} %collective-permute-done.5, bf16[1024,1280]{1,0:T(8,128)(2,1)} %get-tuple-element.45, bf16[4,1024,1280]{2,1,0:T(8,128)(2,1)} %get-tuple-element.180, s32[]{:T(128)S(6)} %select_n.78), kind=kOutput, calls=%fused_computation.37 | convolution fusion | flops 3360358400 | bytes 11796484 | tf_op jit(solution)/shard_map/nc,nm->cm/dot_general | solution.py:838
  364.3 7.1 add_convert_fusion.5
  371.5 5.1 convolution_convert_fusion.1
  376.6 5.1 convolution_convert_fusion
  383.1 23.9 %fusion.23 = (f32[1280]{0:T(1024)}, f32[1024]{0:T(1024)S(1)}, f32[1024]{0:T(1024)S(1)}, f32[1280]{0:T(1024)}, f32[1024,1280,1]{1,0,2:T(8,128)}) fusion(f32[1024,1280]{1,0:T(8,128)} %copy-done.19, f32[1024]{0:T(1024)S(1)} %add_rsqrt_fusion.2, f32[1024]{0:T(1024)S(1)} %broadcast_multiply_fusion.9, f32[1280]{0:T(1024)S(1)} %get-tuple-element.133, ...), kind=kOutput, calls=%fused_computation.52 | convolution fusion | flops 13433565184 | bytes 34110464 | tf_op jit(solution)/shard_map/tnm,tdm->nd/dot_general | solution.py:858
  407.0 12.1 %multiply_reduce_fusion = (f32[]{:T(128)}, f32[1280]{0:T(1024)}, f32[1280]{0:T(1024)}, f32[1024,1280]{1,0:T(8,128)S(1)}, bf16[1024,1280]{1,0:T(8,128)(2,1)}) fusion(f32[1024,1280]{1,0:T(8,128)} %get-tuple-element.183, bf16[1,16,64,1280]{3,2,1,0:T(8,128)(2,1)S(1)} %copy-done.31, bf16[1,16,64,1280]{3,2,1,0:T(8,128)(2,1)} %param.17, ...), kind=kLoop, calls=%fused_computation.64 | loop fusion | flops 22279680 | bytes 28867588 | tf_op jit(solution)/shard_map/reduce_sum | solution.py:832
  419.4 3.4 copy-done.26
  426.3 3.8 convolution_convert_fusion.7
  431.8 6.6 add_convert_fusion.4
  439.6 6.5 add_convert_fusion.3
  446.1 10.1 %collective-permute-done.10 = bf16[1280,1280]{1,0:T(8,128)(2,1)} collective-permute-done((bf16[1280,1280]{1,0:T(8,128)(2,1)}, bf16[1280,1280]{1,0:T(8,128)(2,1)}, u32[]{:S(2)}, u32[]{:S(2)}) %collective-permute-start.10) | collective-permute-done | bytes 3276832 | tf_op jit(solution)/shard_map/ppermute | solution.py:699
  456.2 2.7 add_convert_fusion.2
  459.0 40.3 %attend_back.2 = (bf16[28,80,960]{2,1,0:T(8,128)(2,1)}, bf16[28,80,960]{2,1,0:T(8,128)(2,1)}, f32[256,384]{1,0:T(8,128)S(1)}) custom-call(s32[1]{0:T(128)} %bitcast.1.shard_ref, bf16[4,28,80,960]{3,2,1,0:T(8,128)(2,1)} %bitcast.251, bf16[16,80,1280]{2,1,0:T(8,128)(2,1)S(1)} %fusion.40.grad_ref, bf16[256,384]{1,0:T(8,128)(2,1)S(1)} %copy-done.6, ...), custom_call_target="tpu_custom_call" | custom-call | flops 60000002048 | bytes 20000000 | tf_op jit(solution)/shard_map/attend_back/pallas_call | solution.py:566
  499.3 11.2 %convolution_convert_fusion.9 = bf16[1280,960]{0,1:T(8,128)(2,1)} fusion(bf16[1280,2240]{1,0:T(8,128)(2,1)} %turn.1, bf16[2240,960]{1,0:T(8,128)(2,1)} %bitcast.226), kind=kOutput, calls=%fused_computation.90 | convolution fusion | flops 5506252800 | bytes 12492800 | tf_op jit(solution)/shard_map/dn,nc->dc/dot_general | solution.py:888
  511.1 6.1 collective-permute-done.12
  518.3 3.3 add_convert_fusion.10
  521.5 4.3 collective-permute-done.8
  527.3 8.7 %add_convert_fusion.9 = bf16[1280,960]{0,1:T(8,128)(2,1)S(1)} fusion(bf16[1280,960]{0,1:T(8,128)(2,1)} %copy-done.51, bf16[1280,2240]{1,0:T(8,128)(2,1)S(1)} %bitcast.222, bf16[2240,960]{1,0:T(8,128)(2,1)S(1)} %bitcast.225), kind=kOutput, calls=%fused_computation.76 | convolution fusion | flops 5508710400 | bytes 14950400 | tf_op jit(solution)/shard_map/dn,nc->dc/dot_general | solution.py:888
  539.1 2.9 add_convert_fusion.1
  542.0 3.2 pad_maximum_fusion
  548.2 40.3 %attend_back.3 = (bf16[28,80,960]{2,1,0:T(8,128)(2,1)}, bf16[28,80,960]{2,1,0:T(8,128)(2,1)}, f32[256,384]{1,0:T(8,128)S(1)}) custom-call(s32[1]{0:T(128)} %bitcast.1.shard_ref, bf16[4,28,80,960]{3,2,1,0:T(8,128)(2,1)} %bitcast.252, bf16[16,80,1280]{2,1,0:T(8,128)(2,1)S(1)} %fusion.40.grad_ref, bf16[256,384]{1,0:T(8,128)(2,1)S(1)} %copy-done.6, ...), custom_call_target="tpu_custom_call" | custom-call | flops 60000002048 | bytes 20000000 | tf_op jit(solution)/shard_map/attend_back/pallas_call | solution.py:566
  588.5 9.8 %convolution_convert_fusion.8 = bf16[1280,960]{0,1:T(8,128)(2,1)} fusion(bf16[1280,2240]{1,0:T(8,128)(2,1)S(1)} %copy-done.21, bf16[2240,960]{1,0:T(8,128)(2,1)} %bitcast.230), kind=kOutput, calls=%fused_computation.89 | convolution fusion | flops 5506252800 | bytes 12492800 | tf_op jit(solution)/shard_map/dn,nc->dc/dot_general | solution.py:888
  598.7 42.1 %frame_back.1 = (bf16[28,64,1280]{2,1,0:T(8,128)(2,1)}, f32[4,1,960]{2,1,0:T(1,128)}) custom-call(s32[1]{0:T(128)} %bitcast.1.shard_ref, bf16[2240,960]{1,0:T(8,128)(2,1)} %bitcast.228, bf16[2240,960]{1,0:T(8,128)(2,1)} %bitcast.231, bf16[2240,960]{1,0:T(8,128)(2,1)} %bitcast.224, bf16[2240,960]{1,0:T(8,128)(2,1)} %bitcast.227, ...), custom_call_target="tpu_custom_call" | custom-call | flops 1000000 | bytes 1000000 | tf_op jit(solution)/shard_map/frame_back/pallas_call | solution.py:665
  640.8 10.1 %add_convert_fusion.8 = bf16[1280,960]{0,1:T(8,128)(2,1)S(1)} fusion(bf16[1280,960]{0,1:T(8,128)(2,1)S(1)} %collective-permute-done.15, bf16[1280,2240]{1,0:T(8,128)(2,1)} %turn.1, bf16[2240,960]{1,0:T(8,128)(2,1)} %bitcast.229), kind=kOutput, calls=%fused_computation.75 | convolution fusion | flops 5508710400 | bytes 14950400 | tf_op jit(solution)/shard_map/dn,nc->dc/dot_general | solution.py:888
  650.9 4.6 add_convert_fusion
  655.5 9.9 %reduce-scatter.5.cloned.1.call-done = bf16[160,2560]{1,0:T(8,128)(2,1)} async-done(((bf16[1280,2560]{1,0:T(8,128)(2,1)}), bf16[160,2560]{1,0:T(8,128)(2,1)}) %reduce-scatter.5.cloned.1.call-update) | async-done | bytes 819216 | tf_op jit(solution)/shard_map/reduce_scatter | solution.py:723
  665.4 5.7 copy.64
  671.7 2.9 constant_dynamic-update-slice_fusion
  689.8 6.9 multiply_reduce_fusion.1
  697.5 14.2 %collective-permute-start.18 = (f32[19681]{0:T(1024)S(1)}, f32[19681]{0:T(1024)S(1)}, u32[]{:S(2)}, u32[]{:S(2)}) collective-permute-start(f32[19681]{0:T(1024)S(1)} %concatenate.51), channel_id=1, source_target_pairs={{0,1},{1,0},{2,3},{3,2},{4,5},{5,4},{6,7},{7,6},{8,9},{9,8},{10,11... | collective-permute-start | bytes 236180 | tf_op jit(solution)/shard_map/ppermute | solution.py:699
  712.6 2.8 collective-permute-start.19
  719.7 3.0 collective-permute-done.20
  723.5 3.6 collective-permute-done.21
  728.8 6.6 fusion.22
  743.4 4.1 reduce-scatter.7.cloned.1.call-done
  (303 shorter events, 81.4 us)
Async XLA Ops:
  7.2 167.0 %all-gather.3.cloned.1.call-start = ((), (), s32[]{:S(2)}) async-start(), calls=%async_computation.2 | async-start | bytes 27033600 | tf_op jit(solution)/shard_map/all_gather | solution.py:785
  11.0 279.8 %all-gather.5.cloned.1.call-start = ((), (), s32[]{:S(2)}) async-start(), calls=%async_computation.3 | async-start | bytes 13516800 | tf_op jit(solution)/shard_map/all_gather | solution.py:813
  12.5 7.9 %collective-permute-start.1 = (bf16[12,64,1280]{2,1,0:T(8,128)(2,1)}, bf16[12,64,1280]{2,1,0:T(8,128)(2,1)}, u32[]{:S(2)}, u32[]{:S(2)}) collective-permute-start(bf16[12,64,1280]{2,1,0:T(8,128)(2,1)} %slice_bitcast_fusion), channel_id=1, source_target_pairs={{1,0},{2,1},{3,2},{5,4},{6,5},{7,6},{9,8},{10,9},{11,10},{13,12},{... | collective-permute-start | bytes 5898248 | tf_op jit(solution)/shard_map/ppermute | solution.py:699
  14.8 5.5 collective-permute-start
  27.8 146.5 %copy-start.50 = (bf16[2,320]{1,0:T(2,128)(2,1)S(1)}, bf16[2,320]{1,0:T(2,128)(2,1)}, u32[]{:S(2)}) copy-start(bf16[2,320]{1,0:T(2,128)(2,1)} %param.23) | copy-start | bytes 3844
  27.8 148.0 %copy-start.49 = (bf16[1280]{0:T(1024)(128)(2,1)S(1)}, bf16[1280]{0:T(1024)(128)(2,1)}, u32[]{:S(2)}) copy-start(bf16[1280]{0:T(1024)(128)(2,1)} %param.24) | copy-start | bytes 7684
  27.8 152.1 %copy-start.38 = (bf16[2,27,80]{2,0,1:T(2,128)(2,1)S(1)}, bf16[2,27,80]{2,0,1:T(2,128)(2,1)}, u32[]{:S(2)}) copy-start(bf16[2,27,80]{2,0,1:T(2,128)(2,1)} %param.28) | copy-start | bytes 25924
  27.8 152.9 %copy-start.42 = (bf16[2,1280]{1,0:T(2,128)(2,1)S(1)}, bf16[2,1280]{1,0:T(2,128)(2,1)}, u32[]{:S(2)}) copy-start(bf16[2,1280]{1,0:T(2,128)(2,1)} %param.27) | copy-start | bytes 15364
  174.2 491.2 %reduce-scatter.5.cloned.1.call-start = ((), (), s32[]{:S(2)}) async-start(), calls=%async_computation.4 | async-start | bytes 7372800 | tf_op jit(solution)/shard_map/reduce_scatter | solution.py:723
  177.1 5.2 collective-permute-start.4
  178.5 4.6 collective-permute-start.3
  179.0 4.7 collective-permute-start.2
  181.5 34.8 %copy-start.5 = (bf16[256,384]{1,0:T(8,128)(2,1)}, bf16[256,384]{1,0:T(8,128)(2,1)S(1)}, u32[]{:S(2)}) copy-start(bf16[256,384]{1,0:T(8,128)(2,1)S(1)} %pad.34.table_ref) | copy-start | bytes 589828
  184.7 31.6 %copy-start.9 = (bf16[4,224,256]{2,1,0:T(8,128)(2,1)S(1)}, bf16[4,224,256]{2,1,0:T(8,128)(2,1)}, u32[]{:S(2)}) copy-start(bf16[4,224,256]{2,1,0:T(8,128)(2,1)} %constant.138.clone.select_ref) | copy-start | bytes 1376260
  216.3 45.8 %copy-start.14 = (bf16[1280,1280]{1,0:T(8,128)(2,1)}, bf16[1280,1280]{1,0:T(8,128)(2,1)S(1)}, u32[]{:S(2)}) copy-start(bf16[1280,1280]{1,0:T(8,128)(2,1)S(1)} %get-tuple-element.43) | copy-start | bytes 9830404
  268.3 108.3 %copy-start.27 = (bf16[1024,1280]{1,0:T(8,128)(2,1)}, bf16[1024,1280]{1,0:T(8,128)(2,1)S(1)}, u32[]{:S(2)}) copy-start(bf16[1024,1280]{1,0:T(8,128)(2,1)S(1)} %add_convert_fusion.7) | copy-start | bytes 7864324
  313.9 16.5 %slice-start.2 = ((s8[13107200]{0:T(1024)(128)(4,1)}), s8[4194304]{0:T(1024)(128)(4,1)S(1)}, s32[]{:S(2)}) async-start(s8[13107200]{0:T(1024)(128)(4,1)} %bitcast.247), calls=%async_computation.8 | async-start | bytes 8388608
  313.9 16.5 %slice-start.3 = ((s8[13107200]{0:T(1024)(128)(4,1)}), s8[4194304]{0:T(1024)(128)(4,1)S(1)}, s32[]{:S(2)}) async-start(s8[13107200]{0:T(1024)(128)(4,1)} %bitcast.247), calls=%async_computation.9 | async-start | bytes 8388608
  321.9 34.3 %collective-permute-start.5 = (bf16[1280,1280]{1,0:T(8,128)(2,1)}, bf16[1280,1280]{1,0:T(8,128)(2,1)S(1)}, u32[]{:S(2)}, u32[]{:S(2)}) collective-permute-start(bf16[1280,1280]{1,0:T(8,128)(2,1)} %convolution_convert_fusion.3), channel_id=1, source_target_pairs={{0,1},{1,0},{2,3},{3,2},{4,5},{5,4},{6,7},{7,6},{8,9},{9,8},{10,11... | collective-permute-start | bytes 9830408 | tf_op jit(solution)/shard_map/ppermute | solution.py:699
  330.2 34.1 %collective-permute-start.6 = (bf16[1280,1280]{1,0:T(8,128)(2,1)}, bf16[1280,1280]{1,0:T(8,128)(2,1)S(1)}, u32[]{:S(2)}, u32[]{:S(2)}) collective-permute-start(bf16[1280,1280]{1,0:T(8,128)(2,1)} %convolution_convert_fusion.2), channel_id=1, source_target_pairs={{0,1},{1,0},{2,3},{3,2},{4,5},{5,4},{6,7},{7,6},{8,9},{9,8},{10,11... | collective-permute-start | bytes 9830408 | tf_op jit(solution)/shard_map/ppermute | solution.py:699
  356.2 15.2 %slice-start.6 = ((s8[10485760]{0:T(1024)(128)(4,1)}), s8[4194304]{0:T(1024)(128)(4,1)S(1)}, s32[]{:S(2)}) async-start(s8[10485760]{0:T(1024)(128)(4,1)} %bitcast.253), calls=%async_computation.12 | async-start | bytes 8388608
  356.2 15.2 %slice-start.7 = ((s8[10485760]{0:T(1024)(128)(4,1)}), s8[4194304]{0:T(1024)(128)(4,1)S(1)}, s32[]{:S(2)}) async-start(s8[10485760]{0:T(1024)(128)(4,1)} %bitcast.253), calls=%async_computation.13 | async-start | bytes 8388608
  381.6 25.3 %copy-start.31 = (bf16[1,16,64,1280]{3,2,1,0:T(8,128)(2,1)S(1)}, bf16[1,16,64,1280]{3,2,1,0:T(8,128)(2,1)}, u32[]{:S(2)}) copy-start(bf16[1,16,64,1280]{3,2,1,0:T(8,128)(2,1)} %param.18) | copy-start | bytes 7864324
  381.6 49.5 %collective-permute-start.7 = (bf16[1280,1280]{1,0:T(8,128)(2,1)}, bf16[1280,1280]{1,0:T(8,128)(2,1)}, u32[]{:S(2)}, u32[]{:S(2)}) collective-permute-start(bf16[1280,1280]{1,0:T(8,128)(2,1)} %convolution_convert_fusion.1), channel_id=1, source_target_pairs={{0,1},{1,0},{2,3},{3,2},{4,5},{5,4},{6,7},{7,6},{8,9},{9,8},{10,11... | collective-permute-start | bytes 9830408 | tf_op jit(solution)/shard_map/ppermute | solution.py:699
  382.0 57.6 %collective-permute-start.9 = (bf16[1280,1280]{1,0:T(8,128)(2,1)}, bf16[1280,1280]{1,0:T(8,128)(2,1)}, u32[]{:S(2)}, u32[]{:S(2)}) collective-permute-start(bf16[1280,1280]{1,0:T(8,128)(2,1)} %convolution_convert_fusion), channel_id=1, source_target_pairs={{0,1},{1,0},{2,3},{3,2},{4,5},{5,4},{6,7},{7,6},{8,9},{9,8},{10,11... | collective-permute-start | bytes 9830408 | tf_op jit(solution)/shard_map/ppermute | solution.py:699
  382.2 74.0 %collective-permute-start.10 = (bf16[1280,1280]{1,0:T(8,128)(2,1)}, bf16[1280,1280]{1,0:T(8,128)(2,1)}, u32[]{:S(2)}, u32[]{:S(2)}) collective-permute-start(bf16[1280,1280]{1,0:T(8,128)(2,1)} %add_convert_fusion.6), channel_id=1, source_target_pairs={{0,2},{2,0},{1,3},{3,1},{4,6},{6,4},{5,7},{7,5},{8,10},{10,8},{9,1... | collective-permute-start | bytes 9830408 | tf_op jit(solution)/shard_map/ppermute | solution.py:699
  438.4 17.8 %copy-start.23 = (bf16[1280,1280]{1,0:T(8,128)(2,1)S(1)}, bf16[1280,1280]{1,0:T(8,128)(2,1)}, u32[]{:S(2)}) copy-start(bf16[1280,1280]{1,0:T(8,128)(2,1)} %add_convert_fusion.5) | copy-start | bytes 9830404
  438.4 87.4 %collective-permute-start.8 = (bf16[1280,1280]{1,0:T(8,128)(2,1)}, bf16[1280,1280]{1,0:T(8,128)(2,1)}, u32[]{:S(2)}, u32[]{:S(2)}) collective-permute-start(bf16[1280,1280]{1,0:T(8,128)(2,1)} %add_convert_fusion.4), channel_id=1, source_target_pairs={{0,2},{2,0},{1,3},{3,1},{4,6},{6,4},{5,7},{7,5},{8,10},{10,8},{9,1... | collective-permute-start | bytes 9830408 | tf_op jit(solution)/shard_map/ppermute | solution.py:699
  446.1 12.9 %copy-start.6 = (bf16[256,384]{1,0:T(8,128)(2,1)S(1)}, bf16[256,384]{1,0:T(8,128)(2,1)}, u32[]{:S(2)}) copy-start(bf16[256,384]{1,0:T(8,128)(2,1)} %copy-done.5) | copy-start | bytes 589828
  446.1 12.9 %copy-start.7 = (bf16[256,384]{1,0:T(8,128)(2,1)S(1)}, bf16[256,384]{1,0:T(8,128)(2,1)}, u32[]{:S(2)}) copy-start(bf16[256,384]{1,0:T(8,128)(2,1)} %pad.36.back_ref) | copy-start | bytes 589828
  446.1 12.9 %copy-start.10 = (bf16[4,224,256]{2,1,0:T(8,128)(2,1)S(1)}, bf16[4,224,256]{2,1,0:T(8,128)(2,1)}, u32[]{:S(2)}) copy-start(bf16[4,224,256]{2,1,0:T(8,128)(2,1)} %constant.138.clone.select_ref) | copy-start | bytes 1376260
  446.1 12.9 %copy-start.12 = (bf16[4,224,128]{2,1,0:T(8,128)(2,1)S(1)}, bf16[4,224,128]{2,1,0:T(8,128)(2,1)}, u32[]{:S(2)}) copy-start(bf16[4,224,128]{2,1,0:T(8,128)(2,1)} %constant.139.clone.spread_ref) | copy-start | bytes 688132
  499.3 17.8 %copy-start.30 = (bf16[1024,1280]{1,0:T(8,128)(2,1)S(1)}, bf16[1024,1280]{1,0:T(8,128)(2,1)}, u32[]{:S(2)}) copy-start(bf16[1024,1280]{1,0:T(8,128)(2,1)} %copy-done.29) | copy-start | bytes 7864324
  510.5 15.3 %collective-permute-start.11 = (bf16[1280,960]{0,1:T(8,128)(2,1)}, bf16[1280,960]{0,1:T(8,128)(2,1)S(1)}, u32[]{:S(2)}, u32[]{:S(2)}) collective-permute-start(bf16[1280,960]{0,1:T(8,128)(2,1)} %convolution_convert_fusion.9), channel_id=1, source_target_pairs={{0,1},{1,0},{2,3},{3,2},{4,5},{5,4},{6,7},{7,6},{8,9},{9,8},{10,11... | collective-permute-start | bytes 7372808 | tf_op jit(solution)/shard_map/ppermute | solution.py:699
  510.5 6.6 collective-permute-start.12
  511.0 7.2 collective-permute-start.14
  538.0 102.8 %collective-permute-start.13 = (bf16[1280,1280]{0,1:T(8,128)(2,1)}, bf16[1280,1280]{0,1:T(8,128)(2,1)}, u32[]{:S(2)}, u32[]{:S(2)}) collective-permute-start(bf16[1280,1280]{0,1:T(8,128)(2,1)} %pad_maximum_fusion.1), channel_id=1, source_target_pairs={{0,2},{2,0},{1,3},{3,1},{4,6},{6,4},{5,7},{7,5},{8,10},{10,8},{9,1... | collective-permute-start | bytes 9830408 | tf_op jit(solution)/shard_map/ppermute | solution.py:699
  545.2 202.2 %reduce-scatter.7.cloned.1.call-start = ((), (), s32[]{:S(2)}) async-start(), calls=%async_computation.5 | async-start | bytes 3686400
  548.2 40.3 %copy-start.21 = (bf16[1280,2240]{1,0:T(8,128)(2,1)S(1)}, bf16[1280,2240]{1,0:T(8,128)(2,1)}, u32[]{:S(2)}) copy-start(bf16[1280,2240]{1,0:T(8,128)(2,1)} %turn.1) | copy-start | bytes 17203204
  598.3 42.5 %collective-permute-start.15 = (bf16[1280,960]{0,1:T(8,128)(2,1)}, bf16[1280,960]{0,1:T(8,128)(2,1)S(1)}, u32[]{:S(2)}, u32[]{:S(2)}) collective-permute-start(bf16[1280,960]{0,1:T(8,128)(2,1)} %convolution_convert_fusion.8), channel_id=1, source_target_pairs={{0,1},{1,0},{2,3},{3,2},{4,5},{5,4},{6,7},{7,6},{8,9},{9,8},{10,11... | collective-permute-start | bytes 7372808 | tf_op jit(solution)/shard_map/ppermute | solution.py:699
  678.6 11.2 %collective-permute-start.17 = (bf16[12,64,1280]{2,1,0:T(8,128)(2,1)}, bf16[12,64,1280]{2,1,0:T(8,128)(2,1)}, u32[]{:S(2)}, u32[]{:S(2)}) collective-permute-start(bf16[12,64,1280]{2,1,0:T(8,128)(2,1)} %slice.183), channel_id=1, source_target_pairs={{0,1},{1,2},{2,3},{4,5},{5,6},{6,7},{8,9},{9,10},{10,11},{12,13},{... | collective-permute-start | bytes 5898248 | tf_op jit(solution)/shard_map/ppermute | solution.py:699
  684.5 5.3 collective-permute-start.16
  697.5 15.1 %collective-permute-start.18 = (f32[19681]{0:T(1024)S(1)}, f32[19681]{0:T(1024)S(1)}, u32[]{:S(2)}, u32[]{:S(2)}) collective-permute-start(f32[19681]{0:T(1024)S(1)} %concatenate.51), channel_id=1, source_target_pairs={{0,1},{1,0},{2,3},{3,2},{4,5},{5,4},{6,7},{7,6},{8,9},{9,8},{10,11... | collective-permute-start | bytes 236180 | tf_op jit(solution)/shard_map/ppermute | solution.py:699
  712.6 5.5 collective-permute-start.19
  718.1 4.5 collective-permute-start.20
  722.7 4.5 collective-permute-start.21
  727.2 9.7 %collective-permute-start.22 = (f32[19681]{0:T(1024)S(1)}, f32[19681]{0:T(1024)S(1)}, u32[]{:S(2)}, u32[]{:S(2)}) collective-permute-start(f32[19681]{0:T(1024)S(1)} %add.311), channel_id=1, source_target_pairs={{0,16},{4,20},{8,24},{12,28},{16,0},{20,4},{24,8},{28,12},{1,17},{... | collective-permute-start | bytes 236180 | tf_op jit(solution)/shard_map/ppermute | solution.py:736
  728.8 13.3 %copy-start.33 = (bf16[160,2560]{1,0:T(8,128)(2,1)S(1)}, bf16[160,2560]{1,0:T(8,128)(2,1)}, u32[]{:S(2)}) copy-start(bf16[160,2560]{1,0:T(8,128)(2,1)} %reduce-scatter.5.cloned.1.call-done) | copy-start | bytes 2457604
  (45 other events, 278.4 us)
Sparse Core Ops, SparseCore 0:
  11.5 162.6 all-gather.2
  177.0 96.6 all-gather.4
  545.3 120.0 reduce-scatter.4
  671.2 76.2 reduce-scatter.6

commit v3 on v2

--- a/solution.py
+++ b/solution.py
@@ -397,11 +397,14 @@
     return jnp.concatenate([upper, lower], axis=1)
 
 
-def softmax_rows(q_sides, keys, bias, select, head):
+def score_rows(q_sides, keys, bias, select, head):
     low, high = SLABS[head]
     left = jnp.concatenate([q_sides[0][:, low:high], q_sides[1][:, low:high], bias], axis=1)
     right = jnp.concatenate([keys[:KEYS], keys[KEYS:], select], axis=1)
-    scores = dot(left, right, NT)
+    return dot(left, right, NT)
+
+
+def softmax_rows(scores):
     top = jnp.max(scores, axis=1, keepdims=True)
     raised = jnp.exp2((scores - top) * (SCALE * LOG2E))
     total = jnp.sum(raised, axis=1, keepdims=True)
@@ -428,10 +431,15 @@
         q_sides = by_side(q, first)
         bias = bias_rows(q, table_ref[...], first)
         v = pad_lanes(v, 384)
+        scores = []
         for head in range(GROUP):
             low, high = SLABS[head]
             keys = head_mask(k[:, low:high], head, low)
-            probs = softmax_rows(q_sides, keys, bias, select_ref[head], head).astype(jnp.bfloat16)
+            scores.append(score_rows(q_sides, keys, bias, select_ref[head], head))
+        all_probs = [softmax_rows(rows).astype(jnp.bfloat16) for rows in scores]
+        for head in range(GROUP):
+            low, high = SLABS[head]
+            probs = all_probs[head]
             values = head_mask(v[:, low:high], head, low)
             piece = pick_side(dot(probs, beside(values[:KEYS], values[KEYS:]), NN), first)
             if head == 0:
@@ -492,14 +500,20 @@
         dk[...] = jnp.zeros_like(dk)
         dv[...] = jnp.zeros_like(dv)
         marks = jnp.zeros((queries, 128), jnp.float32)
+        all_keys, scores, grads = [], [], []
         for head in range(GROUP):
             low, high = SLABS[head]
             keys = head_mask(k[:, low:high], head, low)
             values = head_mask(v[:, low:high], head, low)
-            probs = softmax_rows(q_sides, keys, bias, select_ref[head], head)
+            all_keys.append(keys)
+            scores.append(score_rows(q_sides, keys, bias, select_ref[head], head))
+            go_both = beside(go_sides[0][:, low:high], go_sides[1][:, low:high])
+            grads.append(dot(go_both, beside(values[:KEYS], values[KEYS:]), NT))
+        for head in range(GROUP):
+            low, high = SLABS[head]
+            keys, probs_grad = all_keys[head], grads[head]
+            probs = softmax_rows(scores[head])
             probs_low = probs.astype(jnp.bfloat16)
-            go_both = beside(go_sides[0][:, low:high], go_sides[1][:, low:high])
-            probs_grad = dot(go_both, beside(values[:KEYS], values[KEYS:]), NT)
             weighted = probs * probs_grad
             scores_grad = weighted - probs * jnp.sum(weighted, axis=1, keepdims=True)
             scores_low = scores_grad.astype(jnp.bfloat16)
@@ -890,14 +904,18 @@
     far_own, far_other = flatten(far_own), flatten(far_other)
     qkv_send = qkv_block(flat_turned, far_other).astype(bf16)
     qkv_three = swap(qkv_send, CORES)
-    flat_far, up_side, _ = lax.optimization_barrier((flat_turned, up_side, qkv_send))
+    flat_far, up_side, down_grad, _ = lax.optimization_barrier(
+        (flat_turned, up_side, scatter_dp(down_quarter), qkv_send)
+    )
     up_quarter = add_low(up_near, up_side)
-    mlp_grad = scatter_dp(jnp.concatenate([up_quarter, down_quarter], axis=1))
     proj_far = (proj_block(2) + proj_three.astype(f32)).astype(bf16)
     proj_near = (proj_block(0) + proj_one.astype(f32)).astype(bf16)
     qkv_far = (qkv_block(flat_far, far_own) + qkv_three.astype(f32)).astype(bf16)
-    far_side = swap(jnp.concatenate([qkv_far, proj_far], axis=1), SIDES)
-    (grad_near,) = after((qkv_far, proj_far, proj_near, up_quarter), attended_grad)
+    joint_far = jnp.concatenate([qkv_far, proj_far], axis=1)
+    joint_far, proj_near, up_quarter, grad_near = lax.optimization_barrier(
+        (joint_far, proj_near, up_quarter, attended_grad)
+    )
+    far_side = swap(joint_far, SIDES)
     near_own, near_other, near_sums = window_attend_back(
         0, where, qkv, grad_near, tables, back_tables, select_keys, spread_keys
     )
@@ -906,22 +924,21 @@
     qkv_one = swap(qkv_send, CORES)
     backs = after(qkv_send, near_own, near_other, far_own, far_other)
     frame_grad, bias_sums = frame_back(where, backs, joint_all, select.T)
-    flat_near, far_side, _ = lax.optimization_barrier((flat_turned, far_side, frame_grad))
+    spread = jnp.zeros((EARLY + ROWS + LATE, GRID, D), bf16)
+    spread = lax.dynamic_update_slice_in_dim(spread, frame_grad, EARLY - 2 * shard, 0)
+    flat_near, far_side, spread = lax.optimization_barrier((flat_turned, far_side, spread))
     qkv_near = qkv_block(flat_near, near_own) + qkv_one.astype(f32)
     near = jnp.concatenate([qkv_near.astype(bf16), proj_near], axis=1)
     joint_quarter = add_low(near, far_side)
-    mlp_grad, joint_ready = lax.optimization_barrier((mlp_grad, joint_quarter))
-    joint_grad = scatter_dp(joint_ready)
+    up_grad, joint_quarter = lax.optimization_barrier((scatter_dp(up_quarter), joint_quarter))
+    joint_grad = scatter_dp(joint_quarter)
     table_sums = far_sums + near_sums
-    (frame_grad,) = after(joint_quarter, frame_grad)
     bias_sums = bias_sums[:, 0]
     qv_acc = jnp.stack([bias_sums[:, :320], bias_sums[:, 640:]], axis=1)
     qv_acc = jnp.stack([own(qv_acc, shard ^ t) for t in range(4)])
     table_sums = table_sums[:, :320].reshape(2, GROUP, 32, GROUP, HEAD_DIM)
     table_acc = jnp.einsum("phrhd->prd", table_sums)
     table_acc = jnp.stack([table_acc[0, :27][::-1], table_acc[1, :27]])
-    spread = jnp.zeros((EARLY + ROWS + LATE, GRID, D), bf16)
-    spread = lax.dynamic_update_slice_in_dim(spread, frame_grad, EARLY - 2 * shard, 0)
     from_next = swap(spread[:EARLY], [(i + 1, i) for i in range(3)])
     from_before = swap(spread[EARLY + ROWS:], [(i, i + 1) for i in range(3)])
     first_grad = spread[EARLY:EARLY + ROWS].astype(f32)
@@ -951,8 +968,8 @@
         loss,
         joint_grad[:, :960].reshape(inner, 3, 320).transpose(1, 0, 2).astype(f32),
         joint_grad[:, 960:].T.astype(f32),
-        mlp_grad[:, :1280].astype(f32),
-        mlp_grad[:, 1280:].T.astype(f32),
+        up_grad.astype(f32),
+        down_grad.T.astype(f32),
         own(qv_sum, shard),
         own(up_sum, shard),
         jnp.stack([gain_one, gain_two]),

time: 766 us -> 744 us (0.971)
  Pallas kernels: 203 us -> 164 us
    pallas_call x2, Pallas kernels: 80.7 us -> 57.3 us  [window_attend_back(): pl.pallas_call(backward_kernel, grid_spec=spec, out_shape=[jax.ShapeDtype...]
    pallas_call x1, Pallas kernels: 44.9 us -> 28.1 us  [window_attend(): pl.pallas_call(forward_kernel, grid_spec=spec, out_shape=jax.ShapeDtypeSt...]
    unnamed x139 -> x141, local copies, waits for them, and re-layouts: 23.2 us -> 21.7 us
  transfers between devices with their start and end apart: 27 -> 28, of which waited for: 13 -> 11; matrix products, arithmetic and copies ran while one was open for 30% -> 32% of each run, Pallas kernels for 27% -> 22%
where the time goes in v3:
time: 744 us; the launch traced here: 737 us
  matrix products  214 us (29%)
  waiting for transfers between devices  195 us (26%)
  Pallas kernels  164 us (22%)
  other arithmetic  55.5 us (7%)
  local copies, waits for them, and re-layouts  52.6 us (7%)
  starting transfers between devices  39.3 us (5%)
  between operations  16.9 us (2%)
    all_gather x1, waiting for transfers between devices, fast_shards(): lax.all_gather(joint, both, axis=0, tiled=True).reshape(4, D, 2560)  140 us
    pallas_call x2, Pallas kernels, window_attend_back(): pl.pallas_call(backward_kernel, grid_spec=spec, out_shape=[jax.ShapeDtype...  57.3 us
    dot_general x4, matrix products, qkv_block(): return jnp.einsum('dn,nc->dc', tokens_in, back, preferred_element_type=f32)  41.9 us
    pallas_call x1, Pallas kernels, frame_back(): pl.pallas_call(frame_kernel, grid_spec=spec, out_shape=[jax.ShapeDtypeStr...  41.9 us
    ppermute x20, starting transfers between devices, swap(): return lax.ppermute(values, 'tensor', shifts)  34.8 us
    pallas_call x1, Pallas kernels, project(): pl.pallas_call(project_kernel, grid_spec=spec, out_shape=[jax.ShapeDtypeS...  32.1 us
    dot_general x4, matrix products, down_block(): jnp.einsum('nc,nm->cm', result_low, own(active, shard ^ p), preferred_ele...  29.7 us
    ppermute x20, waiting for transfers between devices, swap(): return lax.ppermute(values, 'tensor', shifts)  29.2 us
  transfers between devices with their start and end apart: 28, of which 11 were waited for; matrix products, arithmetic and copies ran while one was open for 32% of the time, Pallas kernels for 22%

profile of v3, /device:TPU:0, one launch (start us, length us, event | category | flops | bytes accessed | tf_op | source)
XLA Modules:
  0.0 736.5 jit_solution(16096339158008137180)
XLA Ops:
  14.8 4.0 collective-permute-start
  20.3 3.2 convert_reduce_fusion
  27.8 4.0 turn.1
  34.4 139.8 %all-gather.3.cloned.1.call-done = bf16[5120,2560]{1,0:T(8,128)(2,1)} async-done(((bf16[160,2560]{1,0:T(8,128)(2,1)}), bf16[5120,2560]{1,0:T(8,128)(2,1)}) %all-gather.3.cloned.1.call-update) | async-done | bytes 26214416 | tf_op jit(solution)/shard_map/all_gather | solution.py:799
  184.5 32.1 %project.1 = (bf16[4,2240,960]{2,1,0:T(8,128)(2,1)}, bf16[1280,1280]{1,0:T(8,128)(2,1)S(1)}) custom-call(s32[1]{0:T(128)} %bitcast.1.shard_ref, bf16[2240,1280]{1,0:T(8,128)(2,1)} %bitcast.215, bf16[4,1280,2560]{2,1,0:T(8,128)(2,1)} %bitcast.217, f32[4,1,960]{2,1,0:T(1,128)S(1)} %maximum_convert_fusion.bias_ref), custom_call_target="tpu_custom_call" | custom-call | flops 24000000000 | bytes 35000000 | tf_op jit(solution)/shard_map/project/pallas_call | solution.py:629
  216.7 28.1 %attend.1 = bf16[16,80,1280]{2,1,0:T(8,128)(2,1)S(1)} custom-call(s32[1]{0:T(128)} %bitcast.1.shard_ref, bf16[4,28,80,960]{3,2,1,0:T(8,128)(2,1)} %bitcast.252, bf16[256,384]{1,0:T(8,128)(2,1)S(1)} %pad.34.table_ref, bf16[4,224,256]{2,1,0:T(8,128)(2,1)S(1)} %copy-done.9), custom_call_target="tpu_custom_call" | custom-call | flops 49999998976 | bytes 20000000 | tf_op jit(solution)/shard_map/attend/pallas_call | solution.py:468
  245.6 3.8 fusion.105
  251.8 22.4 %fusion.8 = (bf16[4,1024,1280]{2,1,0:T(8,128)(2,1)}, f32[4,1280,1024]{1,2,0:T(8,128)}) fusion(f32[4,1280]{1,0:T(4,128)S(1)} %fusion.81, bf16[4,1280,2560]{2,1,0:T(8,128)(2,1)} %bitcast.218, bf16[1024,1280]{1,0:T(8,128)(2,1)S(1)} %add_convert_fusion.7), kind=kOutput, calls=%fused_computation.12 | convolution fusion | flops 13453230080 | bytes 47206400 | tf_op jit(solution)/shard_map/nd,tdm->tnm/dot_general | solution.py:838
  274.1 22.9 %fusion.99 = (bf16[1024,1280]{1,0:T(8,128)(2,1)}, f32[1024,1280]{1,0:T(8,128)}) fusion(bf16[1,16,64,1280]{3,2,1,0:T(8,128)(2,1)} %param.18, bf16[1,16,64,1280]{3,2,1,0:T(8,128)(2,1)} %param.17, f32[1280]{0:T(1024)S(1)} %get-tuple-element.145, f32[1024,1280]{1,0:T(8,128)} %copy-done.19, bf16[4,1024,1280]{2,1,0:T(8,128)(2,1)} %get-tuple-element.186, ...), kind=kOutput, calls=%fused_computation.205 | convolution fusion | flops 13430947840 | bytes 41948160 | tf_op jit(solution)/shard_map/tnm,tcm->nc/dot_general | solution.py:843
  297.1 8.0 %convolution_convert_fusion.3 = bf16[1280,1280]{1,0:T(8,128)(2,1)} fusion(bf16[1024,1280]{1,0:T(8,128)(2,1)} %get-tuple-element.49, bf16[4,1024,1280]{2,1,0:T(8,128)(2,1)} %get-tuple-element.186, s32[]{:T(128)S(6)} %select_n.79), kind=kOutput, calls=%fused_computation.29 | convolution fusion | flops 3357081600 | bytes 8519684 | tf_op jit(solution)/shard_map/nc,nm->cm/dot_general | solution.py:852
  306.6 6.8 convolution_convert_fusion.2
  313.6 26.1 %fusion.102 = (f32[4,1280]{1,0:T(4,128)}, bf16[4,1024,1280]{2,1,0:T(8,128)(2,1)}) fusion(f32[4,1280,1024]{1,2,0:T(8,128)} %get-tuple-element.187, bf16[4,1280,1280]{2,1,0:T(8,128)(2,1)S(1)} %bitcast.251, bf16[1024,1280]{1,0:T(8,128)(2,1)} %get-tuple-element.49), kind=kOutput, calls=%fused_computation.207 | convolution fusion | flops 13489925120 | bytes 47206400 | tf_op jit(solution)/shard_map/nc,tcm->tnm/dot_general | solution.py:857
  339.6 8.1 %add_convert_fusion.6 = bf16[1280,1280]{1,0:T(8,128)(2,1)} fusion(bf16[1280,1280]{1,0:T(8,128)(2,1)S(1)} %collective-permute-done.5, bf16[1024,1280]{1,0:T(8,128)(2,1)} %get-tuple-element.49, bf16[4,1024,1280]{2,1,0:T(8,128)(2,1)} %get-tuple-element.186, s32[]{:T(128)S(6)} %select_n.78), kind=kOutput, calls=%fused_computation.36 | convolution fusion | flops 3360358400 | bytes 11796484 | tf_op jit(solution)/shard_map/nc,nm->cm/dot_general | solution.py:852
  347.7 6.9 add_convert_fusion.5
  354.7 5.1 convolution_convert_fusion.1
  359.7 5.1 convolution_convert_fusion
  366.2 24.4 %fusion.23 = (f32[1280]{0:T(1024)}, f32[1024]{0:T(1024)S(1)}, f32[1024]{0:T(1024)S(1)}, f32[1280]{0:T(1024)}, f32[1024,1280,1]{1,0,2:T(8,128)}) fusion(f32[1024,1280]{1,0:T(8,128)} %copy-done.19, f32[1024]{0:T(1024)S(1)} %add_rsqrt_fusion.2, f32[1024]{0:T(1024)S(1)} %broadcast_multiply_fusion.9, f32[1280]{0:T(1024)S(1)} %get-tuple-element.141, ...), kind=kOutput, calls=%fused_computation.51 | convolution fusion | flops 13433565184 | bytes 34110464 | tf_op jit(solution)/shard_map/tnm,tdm->nd/dot_general | solution.py:872
  390.5 11.7 %multiply_reduce_fusion = (f32[]{:T(128)}, f32[1280]{0:T(1024)}, f32[1280]{0:T(1024)}, f32[1024,1280]{1,0:T(8,128)S(1)}, bf16[1024,1280]{1,0:T(8,128)(2,1)}) fusion(f32[1024,1280]{1,0:T(8,128)} %get-tuple-element.189, bf16[1,16,64,1280]{3,2,1,0:T(8,128)(2,1)S(1)} %copy-done.29, bf16[1,16,64,1280]{3,2,1,0:T(8,128)(2,1)} %param.17, ...), kind=kLoop, calls=%fused_computation.63 | loop fusion | flops 22279680 | bytes 28867588 | tf_op jit(solution)/shard_map/reduce_sum | solution.py:846
  402.5 3.4 copy-done.23
  410.8 3.8 convolution_convert_fusion.7
  416.3 6.7 add_convert_fusion.4
  424.3 6.5 add_convert_fusion.3
  430.8 8.6 %collective-permute-done.10 = bf16[1280,1280]{1,0:T(8,128)(2,1)} collective-permute-done((bf16[1280,1280]{1,0:T(8,128)(2,1)}, bf16[1280,1280]{1,0:T(8,128)(2,1)}, u32[]{:S(2)}, u32[]{:S(2)}) %collective-permute-start.10) | collective-permute-done | bytes 3276832 | tf_op jit(solution)/shard_map/ppermute | solution.py:713
  439.4 4.6 add_convert_fusion.2
  447.0 28.7 %attend_back.2 = (bf16[28,80,960]{2,1,0:T(8,128)(2,1)}, bf16[28,80,960]{2,1,0:T(8,128)(2,1)}, f32[256,384]{1,0:T(8,128)S(1)}) custom-call(s32[1]{0:T(128)} %bitcast.1.shard_ref, bf16[4,28,80,960]{3,2,1,0:T(8,128)(2,1)} %bitcast.253, bf16[16,80,1280]{2,1,0:T(8,128)(2,1)S(1)} %fusion.40.grad_ref, bf16[256,384]{1,0:T(8,128)(2,1)S(1)} %copy-done.6, ...), custom_call_target="tpu_custom_call" | custom-call | flops 60000002048 | bytes 20000000 | tf_op jit(solution)/shard_map/attend_back/pallas_call | solution.py:580
  475.7 11.2 %convolution_convert_fusion.9 = bf16[1280,960]{0,1:T(8,128)(2,1)} fusion(bf16[1280,2240]{1,0:T(8,128)(2,1)} %turn.1, bf16[2240,960]{1,0:T(8,128)(2,1)} %bitcast.226), kind=kOutput, calls=%fused_computation.89 | convolution fusion | flops 5506252800 | bytes 12492800 | tf_op jit(solution)/shard_map/dn,nc->dc/dot_general | solution.py:902
  487.0 3.2 add_convert_fusion.11
  490.1 3.1 add_convert_fusion.10
  493.3 15.8 %collective-permute-done.8 = bf16[1280,1280]{1,0:T(8,128)(2,1)} collective-permute-done((bf16[1280,1280]{1,0:T(8,128)(2,1)}, bf16[1280,1280]{1,0:T(8,128)(2,1)}, u32[]{:S(2)}, u32[]{:S(2)}) %collective-permute-start.8) | collective-permute-done | bytes 3276832 | tf_op jit(solution)/shard_map/ppermute | solution.py:713
  509.0 9.4 %reduce-scatter.6.cloned.1.call-done = bf16[160,1280]{1,0:T(8,128)(2,1)} async-done(((bf16[1280,1280]{1,0:T(8,128)(2,1)}), bf16[160,1280]{1,0:T(8,128)(2,1)}) %reduce-scatter.6.cloned.1.call-update) | async-done | bytes 409616 | tf_op jit(solution)/shard_map/reduce_scatter | solution.py:737
  518.5 5.5 add_convert_fusion.1
  524.0 10.6 %add_convert_fusion.9 = bf16[1280,960]{0,1:T(8,128)(2,1)S(1)} fusion(bf16[1280,960]{0,1:T(8,128)(2,1)} %collective-permute-done.11, bf16[1280,2240]{1,0:T(8,128)(2,1)} %turn.1, bf16[2240,960]{1,0:T(8,128)(2,1)} %bitcast.224), kind=kOutput, calls=%fused_computation.75 | convolution fusion | flops 5508710400 | bytes 14950400 | tf_op jit(solution)/shard_map/dn,nc->dc/dot_general | solution.py:902
  538.0 28.7 %attend_back.3 = (bf16[28,80,960]{2,1,0:T(8,128)(2,1)}, bf16[28,80,960]{2,1,0:T(8,128)(2,1)}, f32[256,384]{1,0:T(8,128)S(1)}) custom-call(s32[1]{0:T(128)} %bitcast.1.shard_ref, bf16[4,28,80,960]{3,2,1,0:T(8,128)(2,1)} %bitcast.254, bf16[16,80,1280]{2,1,0:T(8,128)(2,1)S(1)} %fusion.40.grad_ref, bf16[256,384]{1,0:T(8,128)(2,1)S(1)} %copy-done.6, ...), custom_call_target="tpu_custom_call" | custom-call | flops 60000002048 | bytes 20000000 | tf_op jit(solution)/shard_map/attend_back/pallas_call | solution.py:580
  567.5 11.6 %convolution_convert_fusion.8 = bf16[1280,960]{0,1:T(8,128)(2,1)} fusion(bf16[1280,2240]{1,0:T(8,128)(2,1)} %turn.1, bf16[2240,960]{1,0:T(8,128)(2,1)} %bitcast.232), kind=kOutput, calls=%fused_computation.88 | convolution fusion | flops 5506252800 | bytes 12492800 | tf_op jit(solution)/shard_map/dn,nc->dc/dot_general | solution.py:902
  579.2 41.9 %frame_back.1 = (bf16[28,64,1280]{2,1,0:T(8,128)(2,1)}, f32[4,1,960]{2,1,0:T(1,128)}) custom-call(s32[1]{0:T(128)} %bitcast.1.shard_ref, bf16[2240,960]{1,0:T(8,128)(2,1)} %bitcast.228, bf16[2240,960]{1,0:T(8,128)(2,1)} %bitcast.233, bf16[2240,960]{1,0:T(8,128)(2,1)} %bitcast.225, bf16[2240,960]{1,0:T(8,128)(2,1)} %bitcast.227, ...), custom_call_target="tpu_custom_call" | custom-call | flops 1000000 | bytes 1000000 | tf_op jit(solution)/shard_map/frame_back/pallas_call | solution.py:679
  621.1 3.5 broadcast_in_dim.26
  628.8 8.4 %add_convert_fusion.8 = bf16[1280,960]{0,1:T(8,128)(2,1)S(1)} fusion(bf16[1280,960]{0,1:T(8,128)(2,1)} %collective-permute-done.22, bf16[1280,2240]{1,0:T(8,128)(2,1)S(1)} %bitcast.222, bf16[2240,960]{1,0:T(8,128)(2,1)S(1)} %bitcast.231), kind=kOutput, calls=%fused_computation.74 | convolution fusion | flops 5508710400 | bytes 14950400 | tf_op jit(solution)/shard_map/dn,nc->dc/dot_general | solution.py:902
  637.3 4.6 add_convert_fusion
  641.9 5.8 copy.59
  648.3 3.0 slice.146
  651.3 3.7 collective-permute-start.16
  662.9 6.9 multiply_reduce_fusion.1
  670.6 13.6 %collective-permute-start.17 = (f32[19681]{0:T(1024)S(1)}, f32[19681]{0:T(1024)S(1)}, u32[]{:S(2)}, u32[]{:S(2)}) collective-permute-start(f32[19681]{0:T(1024)S(1)} %concatenate.47), channel_id=1, source_target_pairs={{0,1},{1,0},{2,3},{3,2},{4,5},{5,4},{6,7},{7,6},{8,9},{9,8},{10,11... | collective-permute-start | bytes 236180 | tf_op jit(solution)/shard_map/ppermute | solution.py:713
  685.2 2.8 collective-permute-start.18
  692.1 4.5 collective-permute-done.19
  698.2 2.9 collective-permute-done.20
  702.7 6.5 fusion.22
  715.4 9.0 %reduce-scatter.10.cloned.1.call-done = bf16[160,1280]{1,0:T(8,128)(2,1)} async-done(((bf16[1280,1280]{1,0:T(8,128)(2,1)}), bf16[160,1280]{1,0:T(8,128)(2,1)}) %reduce-scatter.10.cloned.1.call-update) | async-done | bytes 409616
  (309 shorter events, 78.4 us)
Async XLA Ops:
  7.2 167.0 %all-gather.3.cloned.1.call-start = ((), (), s32[]{:S(2)}) async-start(), calls=%async_computation.3 | async-start | bytes 27033600 | tf_op jit(solution)/shard_map/all_gather | solution.py:799
  11.0 263.2 %all-gather.5.cloned.1.call-start = ((), (), s32[]{:S(2)}) async-start(), calls=%async_computation.4 | async-start | bytes 13516800 | tf_op jit(solution)/shard_map/all_gather | solution.py:827
  12.5 7.9 %collective-permute-start.1 = (bf16[12,64,1280]{2,1,0:T(8,128)(2,1)}, bf16[12,64,1280]{2,1,0:T(8,128)(2,1)}, u32[]{:S(2)}, u32[]{:S(2)}) collective-permute-start(bf16[12,64,1280]{2,1,0:T(8,128)(2,1)} %slice_bitcast_fusion), channel_id=1, source_target_pairs={{1,0},{2,1},{3,2},{5,4},{6,5},{7,6},{9,8},{10,9},{11,10},{13,12},{... | collective-permute-start | bytes 5898248 | tf_op jit(solution)/shard_map/ppermute | solution.py:713
  14.8 5.5 collective-permute-start
  27.8 146.5 %copy-start.50 = (bf16[2,320]{1,0:T(2,128)(2,1)S(1)}, bf16[2,320]{1,0:T(2,128)(2,1)}, u32[]{:S(2)}) copy-start(bf16[2,320]{1,0:T(2,128)(2,1)} %param.23) | copy-start | bytes 3844
  27.8 148.0 %copy-start.49 = (bf16[1280]{0:T(1024)(128)(2,1)S(1)}, bf16[1280]{0:T(1024)(128)(2,1)}, u32[]{:S(2)}) copy-start(bf16[1280]{0:T(1024)(128)(2,1)} %param.24) | copy-start | bytes 7684
  27.8 152.0 %copy-start.38 = (bf16[2,27,80]{2,0,1:T(2,128)(2,1)S(1)}, bf16[2,27,80]{2,0,1:T(2,128)(2,1)}, u32[]{:S(2)}) copy-start(bf16[2,27,80]{2,0,1:T(2,128)(2,1)} %param.28) | copy-start | bytes 25924
  27.8 152.7 %copy-start.42 = (bf16[2,1280]{1,0:T(2,128)(2,1)S(1)}, bf16[2,1280]{1,0:T(2,128)(2,1)}, u32[]{:S(2)}) copy-start(bf16[2,1280]{1,0:T(2,128)(2,1)} %param.27) | copy-start | bytes 15364
  174.2 344.3 %reduce-scatter.6.cloned.1.call-start = ((), (), s32[]{:S(2)}) async-start(), calls=%async_computation.5 | async-start | bytes 3686400 | tf_op jit(solution)/shard_map/reduce_scatter | solution.py:737
  177.1 5.0 collective-permute-start.4
  178.5 4.4 collective-permute-start.3
  179.0 4.5 collective-permute-start.2
  181.3 35.3 %copy-start.5 = (bf16[256,384]{1,0:T(8,128)(2,1)}, bf16[256,384]{1,0:T(8,128)(2,1)S(1)}, u32[]{:S(2)}) copy-start(bf16[256,384]{1,0:T(8,128)(2,1)S(1)} %pad.34.table_ref) | copy-start | bytes 589828
  184.5 32.1 %copy-start.9 = (bf16[4,224,256]{2,1,0:T(8,128)(2,1)S(1)}, bf16[4,224,256]{2,1,0:T(8,128)(2,1)}, u32[]{:S(2)}) copy-start(bf16[4,224,256]{2,1,0:T(8,128)(2,1)} %constant.138.clone.select_ref) | copy-start | bytes 1376260
  216.6 29.0 %copy-start.14 = (bf16[1280,1280]{1,0:T(8,128)(2,1)}, bf16[1280,1280]{1,0:T(8,128)(2,1)S(1)}, u32[]{:S(2)}) copy-start(bf16[1280,1280]{1,0:T(8,128)(2,1)S(1)} %get-tuple-element.47) | copy-start | bytes 9830404
  251.8 108.0 %copy-start.25 = (bf16[1024,1280]{1,0:T(8,128)(2,1)}, bf16[1024,1280]{1,0:T(8,128)(2,1)S(1)}, u32[]{:S(2)}) copy-start(bf16[1024,1280]{1,0:T(8,128)(2,1)S(1)} %add_convert_fusion.7) | copy-start | bytes 7864324
  297.1 16.5 %slice-start.4 = ((s8[13107200]{0:T(1024)(128)(4,1)}), s8[4194304]{0:T(1024)(128)(4,1)S(1)}, s32[]{:S(2)}) async-start(s8[13107200]{0:T(1024)(128)(4,1)} %bitcast.249), calls=%async_computation.12 | async-start | bytes 8388608
  297.1 16.5 %slice-start.5 = ((s8[13107200]{0:T(1024)(128)(4,1)}), s8[4194304]{0:T(1024)(128)(4,1)S(1)}, s32[]{:S(2)}) async-start(s8[13107200]{0:T(1024)(128)(4,1)} %bitcast.249), calls=%async_computation.13 | async-start | bytes 8388608
  305.1 34.6 %collective-permute-start.5 = (bf16[1280,1280]{1,0:T(8,128)(2,1)}, bf16[1280,1280]{1,0:T(8,128)(2,1)S(1)}, u32[]{:S(2)}, u32[]{:S(2)}) collective-permute-start(bf16[1280,1280]{1,0:T(8,128)(2,1)} %convolution_convert_fusion.3), channel_id=1, source_target_pairs={{0,1},{1,0},{2,3},{3,2},{4,5},{5,4},{6,7},{7,6},{8,9},{9,8},{10,11... | collective-permute-start | bytes 9830408 | tf_op jit(solution)/shard_map/ppermute | solution.py:713
  313.4 34.3 %collective-permute-start.6 = (bf16[1280,1280]{1,0:T(8,128)(2,1)}, bf16[1280,1280]{1,0:T(8,128)(2,1)S(1)}, u32[]{:S(2)}, u32[]{:S(2)}) collective-permute-start(bf16[1280,1280]{1,0:T(8,128)(2,1)} %convolution_convert_fusion.2), channel_id=1, source_target_pairs={{0,1},{1,0},{2,3},{3,2},{4,5},{5,4},{6,7},{7,6},{8,9},{9,8},{10,11... | collective-permute-start | bytes 9830408 | tf_op jit(solution)/shard_map/ppermute | solution.py:713
  339.6 15.0 %slice-start.8 = ((s8[10485760]{0:T(1024)(128)(4,1)}), s8[4194304]{0:T(1024)(128)(4,1)S(1)}, s32[]{:S(2)}) async-start(s8[10485760]{0:T(1024)(128)(4,1)} %bitcast.255), calls=%async_computation.16 | async-start | bytes 8388608
  339.6 15.0 %slice-start.9 = ((s8[10485760]{0:T(1024)(128)(4,1)}), s8[4194304]{0:T(1024)(128)(4,1)S(1)}, s32[]{:S(2)}) async-start(s8[10485760]{0:T(1024)(128)(4,1)} %bitcast.255), calls=%async_computation.17 | async-start | bytes 8388608
  364.9 25.7 %copy-start.29 = (bf16[1,16,64,1280]{3,2,1,0:T(8,128)(2,1)S(1)}, bf16[1,16,64,1280]{3,2,1,0:T(8,128)(2,1)}, u32[]{:S(2)}) copy-start(bf16[1,16,64,1280]{3,2,1,0:T(8,128)(2,1)} %param.18) | copy-start | bytes 7864324
  364.9 50.8 %collective-permute-start.7 = (bf16[1280,1280]{1,0:T(8,128)(2,1)}, bf16[1280,1280]{1,0:T(8,128)(2,1)}, u32[]{:S(2)}, u32[]{:S(2)}) collective-permute-start(bf16[1280,1280]{1,0:T(8,128)(2,1)} %convolution_convert_fusion.1), channel_id=1, source_target_pairs={{0,1},{1,0},{2,3},{3,2},{4,5},{5,4},{6,7},{7,6},{8,9},{9,8},{10,11... | collective-permute-start | bytes 9830408 | tf_op jit(solution)/shard_map/ppermute | solution.py:713
  365.2 59.1 %collective-permute-start.9 = (bf16[1280,1280]{1,0:T(8,128)(2,1)}, bf16[1280,1280]{1,0:T(8,128)(2,1)}, u32[]{:S(2)}, u32[]{:S(2)}) collective-permute-start(bf16[1280,1280]{1,0:T(8,128)(2,1)} %convolution_convert_fusion), channel_id=1, source_target_pairs={{0,1},{1,0},{2,3},{3,2},{4,5},{5,4},{6,7},{7,6},{8,9},{9,8},{10,11... | collective-permute-start | bytes 9830408 | tf_op jit(solution)/shard_map/ppermute | solution.py:713
  365.4 74.0 %collective-permute-start.10 = (bf16[1280,1280]{1,0:T(8,128)(2,1)}, bf16[1280,1280]{1,0:T(8,128)(2,1)}, u32[]{:S(2)}, u32[]{:S(2)}) collective-permute-start(bf16[1280,1280]{1,0:T(8,128)(2,1)} %add_convert_fusion.6), channel_id=1, source_target_pairs={{0,2},{2,0},{1,3},{3,1},{4,6},{6,4},{5,7},{7,5},{8,10},{10,8},{9,1... | collective-permute-start | bytes 9830408 | tf_op jit(solution)/shard_map/ppermute | solution.py:713
  408.1 78.8 %collective-permute-start.12 = (bf16[1280,320]{0,1:T(8,128)(2,1)}, bf16[1280,320]{0,1:T(8,128)(2,1)}, u32[]{:S(2)}, u32[]{:S(2)}) collective-permute-start(bf16[1280,320]{0,1:T(8,128)(2,1)} %convolution_convert_fusion.11), channel_id=1, source_target_pairs={{0,1},{1,0},{2,3},{3,2},{4,5},{5,4},{6,7},{7,6},{8,9},{9,8},{10,11... | collective-permute-start | bytes 2457608 | tf_op jit(solution)/shard_map/ppermute | solution.py:713
  410.5 79.6 %collective-permute-start.13 = (bf16[1280,320]{0,1:T(8,128)(2,1)}, bf16[1280,320]{0,1:T(8,128)(2,1)}, u32[]{:S(2)}, u32[]{:S(2)}) collective-permute-start(bf16[1280,320]{0,1:T(8,128)(2,1)} %convolution_convert_fusion.10), channel_id=1, source_target_pairs={{0,1},{1,0},{2,3},{3,2},{4,5},{5,4},{6,7},{7,6},{8,9},{9,8},{10,11... | collective-permute-start | bytes 2457608 | tf_op jit(solution)/shard_map/ppermute | solution.py:713
  423.1 16.4 %copy-start.21 = (bf16[1280,1280]{1,0:T(8,128)(2,1)S(1)}, bf16[1280,1280]{1,0:T(8,128)(2,1)}, u32[]{:S(2)}) copy-start(bf16[1280,1280]{1,0:T(8,128)(2,1)} %add_convert_fusion.5) | copy-start | bytes 9830404
  423.1 86.0 %collective-permute-start.8 = (bf16[1280,1280]{1,0:T(8,128)(2,1)}, bf16[1280,1280]{1,0:T(8,128)(2,1)}, u32[]{:S(2)}, u32[]{:S(2)}) collective-permute-start(bf16[1280,1280]{1,0:T(8,128)(2,1)} %add_convert_fusion.4), channel_id=1, source_target_pairs={{0,2},{2,0},{1,3},{3,1},{4,6},{6,4},{5,7},{7,5},{8,10},{10,8},{9,1... | collective-permute-start | bytes 9830408 | tf_op jit(solution)/shard_map/ppermute | solution.py:713
  430.8 13.3 %copy-start.6 = (bf16[256,384]{1,0:T(8,128)(2,1)S(1)}, bf16[256,384]{1,0:T(8,128)(2,1)}, u32[]{:S(2)}) copy-start(bf16[256,384]{1,0:T(8,128)(2,1)} %copy-done.5) | copy-start | bytes 589828
  444.1 197.9 %reduce-scatter.8.cloned.1.call-start = ((), (), s32[]{:S(2)}) async-start(), calls=%async_computation.6 | async-start | bytes 3686400 | tf_op jit(solution)/shard_map/reduce_scatter | solution.py:737
  486.9 37.0 %collective-permute-start.11 = (bf16[1280,960]{0,1:T(8,128)(2,1)}, bf16[1280,960]{0,1:T(8,128)(2,1)}, u32[]{:S(2)}, u32[]{:S(2)}) collective-permute-start(bf16[1280,960]{0,1:T(8,128)(2,1)} %convolution_convert_fusion.9), channel_id=1, source_target_pairs={{0,1},{1,0},{2,3},{3,2},{4,5},{5,4},{6,7},{7,6},{8,9},{9,8},{10,11... | collective-permute-start | bytes 7372808 | tf_op jit(solution)/shard_map/ppermute | solution.py:713
  536.5 91.4 %collective-permute-start.14 = (bf16[1280,1280]{0,1:T(8,128)(2,1)}, bf16[1280,1280]{0,1:T(8,128)(2,1)}, u32[]{:S(2)}, u32[]{:S(2)}) collective-permute-start(bf16[1280,1280]{0,1:T(8,128)(2,1)} %pad_maximum_fusion), channel_id=1, source_target_pairs={{0,2},{2,0},{1,3},{3,1},{4,6},{6,4},{5,7},{7,5},{8,10},{10,8},{9,1... | collective-permute-start | bytes 9830408 | tf_op jit(solution)/shard_map/ppermute | solution.py:713
  567.5 156.9 %reduce-scatter.10.cloned.1.call-start = ((), (), s32[]{:S(2)}) async-start(), calls=%async_computation.7 | async-start | bytes 3686400
  567.5 60.4 %slice-start.2 = ((s8[4587520]{0:T(1024)(128)(4,1)}), s8[4194304]{0:T(1024)(128)(4,1)S(1)}, s32[]{:S(2)}) async-start(s8[4587520]{0:T(1024)(128)(4,1)} %bitcast.229), calls=%async_computation.10 | async-start | bytes 8388608
  579.2 48.8 %collective-permute-start.22 = (bf16[1280,960]{0,1:T(8,128)(2,1)}, bf16[1280,960]{0,1:T(8,128)(2,1)}, u32[]{:S(2)}, u32[]{:S(2)}) collective-permute-start(bf16[1280,960]{0,1:T(8,128)(2,1)} %convolution_convert_fusion.8), channel_id=1, source_target_pairs={{0,1},{1,0},{2,3},{3,2},{4,5},{5,4},{6,7},{7,6},{8,9},{9,8},{10,11... | collective-permute-start | bytes 7372808 | tf_op jit(solution)/shard_map/ppermute | solution.py:713
  579.2 48.8 %slice-start.3 = ((s8[4587520]{0:T(1024)(128)(4,1)}), s8[393216]{0:T(1024)(128)(4,1)S(1)}, s32[]{:S(2)}) async-start(s8[4587520]{0:T(1024)(128)(4,1)} %bitcast.229), calls=%async_computation.11 | async-start | bytes 786432
  647.8 11.8 %copy-start.2 = (f32[256,384]{1,0:T(8,128)S(1)}, f32[256,384]{1,0:T(8,128)}, u32[]{:S(2)}) copy-start(f32[256,384]{1,0:T(8,128)} %copy-done.1) | copy-start | bytes 1179652
  648.3 14.7 %copy-start.35 = (f32[1280]{0:T(1024)S(1)}, f32[1280]{0:T(1024)}, u32[]{:S(2)}) copy-start(f32[1280]{0:T(1024)} %copy-done.34) | copy-start | bytes 15364
  651.3 11.6 %collective-permute-start.16 = (bf16[12,64,1280]{2,1,0:T(8,128)(2,1)}, bf16[12,64,1280]{2,1,0:T(8,128)(2,1)}, u32[]{:S(2)}, u32[]{:S(2)}) collective-permute-start(bf16[12,64,1280]{2,1,0:T(8,128)(2,1)} %slice.146), channel_id=1, source_target_pairs={{0,1},{1,2},{2,3},{4,5},{5,6},{6,7},{8,9},{9,10},{10,11},{12,13},{... | collective-permute-start | bytes 5898248 | tf_op jit(solution)/shard_map/ppermute | solution.py:713
  658.1 4.8 collective-permute-start.15
  662.1 25.8 %copy-start.33 = (bf16[160,1280]{1,0:T(8,128)(2,1)S(1)}, bf16[160,1280]{1,0:T(8,128)(2,1)}, u32[]{:S(2)}) copy-start(bf16[160,1280]{1,0:T(8,128)(2,1)} %reduce-scatter.6.cloned.1.call-done) | copy-start | bytes 1228804
  670.6 14.5 %collective-permute-start.17 = (f32[19681]{0:T(1024)S(1)}, f32[19681]{0:T(1024)S(1)}, u32[]{:S(2)}, u32[]{:S(2)}) collective-permute-start(f32[19681]{0:T(1024)S(1)} %concatenate.47), channel_id=1, source_target_pairs={{0,1},{1,0},{2,3},{3,2},{4,5},{5,4},{6,7},{7,6},{8,9},{9,8},{10,11... | collective-permute-start | bytes 236180 | tf_op jit(solution)/shard_map/ppermute | solution.py:713
  685.2 5.6 collective-permute-start.18
  690.8 5.8 collective-permute-start.19
  696.6 4.5 collective-permute-start.20
  701.1 8.1 %collective-permute-start.21 = (f32[19681]{0:T(1024)S(1)}, f32[19681]{0:T(1024)S(1)}, u32[]{:S(2)}, u32[]{:S(2)}) collective-permute-start(f32[19681]{0:T(1024)S(1)} %add.311), channel_id=1, source_target_pairs={{0,16},{4,20},{8,24},{12,28},{16,0},{20,4},{24,8},{28,12},{1,17},{... | collective-permute-start | bytes 236180 | tf_op jit(solution)/shard_map/ppermute | solution.py:750
  (47 other events, 288.0 us)
Sparse Core Ops, SparseCore 0:
  11.5 162.6 all-gather.2
  177.0 96.6 all-gather.4
  444.2 74.2 reduce-scatter.5
  567.6 74.1 reduce-scatter.7
  647.9 76.4 reduce-scatter.9

commit v4 on v3

--- a/solution.py
+++ b/solution.py
@@ -640,20 +640,16 @@
 
 
 def frame_kernel(shard_ref, near_own, near_other, far_own, far_other, w_ref, fold_ref, out_ref, sums_ref):
+    @pl.when(pl.program_id(0) == 0)
+    def _():
+        sums_ref[...] = jnp.zeros_like(sums_ref)
+
     total = None
     for p, back_ref in enumerate((near_own, near_other, far_own, far_other)):
         back = back_ref[...]
         piece = dot(back, w_ref[p ^ shard_ref[0]][:, :960], NT)
         total = piece if total is None else total + piece
-        column = jnp.sum(back.astype(jnp.float32), axis=0, keepdims=True)
-
-        @pl.when(pl.program_id(0) == 0)
-        def _():
-            sums_ref[p] = column
-
-        @pl.when(pl.program_id(0) > 0)
-        def _():
-            sums_ref[p] += column
+        sums_ref[p] += jnp.sum(back.astype(jnp.float32), axis=0, keepdims=True)
     total = total.astype(jnp.bfloat16)
     for row in range(out_ref.shape[0]):
         piece = total[row * 80:(row + 1) * 80, :]

time: 744 us -> 744 us (level)
  transfers between devices with their start and end apart: 28 -> 28, of which waited for: 11 -> 12; matrix products, arithmetic and copies ran while one was open for 32% -> 32% of each run, Pallas kernels for 22% -> 21%
where the time goes in v4:
time: 744 us; the launch traced here: 737 us
  matrix products  214 us (29%)
  waiting for transfers between devices  202 us (27%)
  Pallas kernels  157 us (21%)
  other arithmetic  55.5 us (7%)
  local copies, waits for them, and re-layouts  52.3 us (7%)
  starting transfers between devices  38.9 us (5%)
  between operations  16.9 us (2%)
    all_gather x1, waiting for transfers between devices, fast_shards(): lax.all_gather(joint, both, axis=0, tiled=True).reshape(4, D, 2560)  140 us
    pallas_call x2, Pallas kernels, window_attend_back(): pl.pallas_call(backward_kernel, grid_spec=spec, out_shape=[jax.ShapeDtype...  57.3 us
    dot_general x4, matrix products, qkv_block(): return jnp.einsum('dn,nc->dc', tokens_in, back, preferred_element_type=f32)  41.9 us
    pallas_call x1, Pallas kernels, frame_back(): pl.pallas_call(frame_kernel, grid_spec=spec, out_shape=[jax.ShapeDtypeStr...  35.7 us
    ppermute x20, starting transfers between devices, swap(): return lax.ppermute(values, 'tensor', shifts)  34.4 us
    pallas_call x1, Pallas kernels, project(): pl.pallas_call(project_kernel, grid_spec=spec, out_shape=[jax.ShapeDtypeS...  32.1 us
    dot_general x4, matrix products, down_block(): jnp.einsum('nc,nm->cm', result_low, own(active, shard ^ p), preferred_ele...  29.8 us
    ppermute x20, waiting for transfers between devices, swap(): return lax.ppermute(values, 'tensor', shifts)  29.6 us
  transfers between devices with their start and end apart: 28, of which 12 were waited for; matrix products, arithmetic and copies ran while one was open for 32% of the time, Pallas kernels for 21%

profile of v4, /device:TPU:0, one launch (start us, length us, event | category | flops | bytes accessed | tf_op | source)
XLA Modules:
  0.0 736.5 jit_solution(9314356940248605073)
XLA Ops:
  14.8 4.0 collective-permute-start
  20.3 3.2 convert_reduce_fusion
  27.8 4.0 turn.1
  34.4 139.8 %all-gather.3.cloned.1.call-done = bf16[5120,2560]{1,0:T(8,128)(2,1)} async-done(((bf16[160,2560]{1,0:T(8,128)(2,1)}), bf16[5120,2560]{1,0:T(8,128)(2,1)}) %all-gather.3.cloned.1.call-update) | async-done | bytes 26214416 | tf_op jit(solution)/shard_map/all_gather | solution.py:795
  184.5 32.1 %project.1 = (bf16[4,2240,960]{2,1,0:T(8,128)(2,1)}, bf16[1280,1280]{1,0:T(8,128)(2,1)S(1)}) custom-call(s32[1]{0:T(128)} %bitcast.1.shard_ref, bf16[2240,1280]{1,0:T(8,128)(2,1)} %bitcast.215, bf16[4,1280,2560]{2,1,0:T(8,128)(2,1)} %bitcast.217, f32[4,1,960]{2,1,0:T(1,128)S(1)} %maximum_convert_fusion.bias_ref), custom_call_target="tpu_custom_call" | custom-call | flops 24000000000 | bytes 35000000 | tf_op jit(solution)/shard_map/project/pallas_call | solution.py:629
  216.7 28.1 %attend.1 = bf16[16,80,1280]{2,1,0:T(8,128)(2,1)S(1)} custom-call(s32[1]{0:T(128)} %bitcast.1.shard_ref, bf16[4,28,80,960]{3,2,1,0:T(8,128)(2,1)} %bitcast.252, bf16[256,384]{1,0:T(8,128)(2,1)S(1)} %pad.34.table_ref, bf16[4,224,256]{2,1,0:T(8,128)(2,1)S(1)} %copy-done.9), custom_call_target="tpu_custom_call" | custom-call | flops 49999998976 | bytes 20000000 | tf_op jit(solution)/shard_map/attend/pallas_call | solution.py:468
  245.6 3.8 fusion.105
  251.8 22.4 %fusion.8 = (bf16[4,1024,1280]{2,1,0:T(8,128)(2,1)}, f32[4,1280,1024]{1,2,0:T(8,128)}) fusion(f32[4,1280]{1,0:T(4,128)S(1)} %fusion.81, bf16[4,1280,2560]{2,1,0:T(8,128)(2,1)} %bitcast.218, bf16[1024,1280]{1,0:T(8,128)(2,1)S(1)} %add_convert_fusion.7), kind=kOutput, calls=%fused_computation.12 | convolution fusion | flops 13453230080 | bytes 47206400 | tf_op jit(solution)/shard_map/nd,tdm->tnm/dot_general | solution.py:834
  274.1 22.9 %fusion.99 = (bf16[1024,1280]{1,0:T(8,128)(2,1)}, f32[1024,1280]{1,0:T(8,128)}) fusion(bf16[1,16,64,1280]{3,2,1,0:T(8,128)(2,1)} %param.18, bf16[1,16,64,1280]{3,2,1,0:T(8,128)(2,1)} %param.17, f32[1280]{0:T(1024)S(1)} %get-tuple-element.145, f32[1024,1280]{1,0:T(8,128)} %copy-done.19, bf16[4,1024,1280]{2,1,0:T(8,128)(2,1)} %get-tuple-element.186, ...), kind=kOutput, calls=%fused_computation.205 | convolution fusion | flops 13430947840 | bytes 41948160 | tf_op jit(solution)/shard_map/tnm,tcm->nc/dot_general | solution.py:839
  297.1 8.0 %convolution_convert_fusion.3 = bf16[1280,1280]{1,0:T(8,128)(2,1)} fusion(bf16[1024,1280]{1,0:T(8,128)(2,1)} %get-tuple-element.49, bf16[4,1024,1280]{2,1,0:T(8,128)(2,1)} %get-tuple-element.186, s32[]{:T(128)S(6)} %select_n.79), kind=kOutput, calls=%fused_computation.29 | convolution fusion | flops 3357081600 | bytes 8519684 | tf_op jit(solution)/shard_map/nc,nm->cm/dot_general | solution.py:848
  306.6 6.8 convolution_convert_fusion.2
  313.6 26.1 %fusion.102 = (f32[4,1280]{1,0:T(4,128)}, bf16[4,1024,1280]{2,1,0:T(8,128)(2,1)}) fusion(f32[4,1280,1024]{1,2,0:T(8,128)} %get-tuple-element.187, bf16[4,1280,1280]{2,1,0:T(8,128)(2,1)S(1)} %bitcast.251, bf16[1024,1280]{1,0:T(8,128)(2,1)} %get-tuple-element.49), kind=kOutput, calls=%fused_computation.207 | convolution fusion | flops 13489925120 | bytes 47206400 | tf_op jit(solution)/shard_map/nc,tcm->tnm/dot_general | solution.py:853
  339.6 8.1 %add_convert_fusion.6 = bf16[1280,1280]{1,0:T(8,128)(2,1)} fusion(bf16[1280,1280]{1,0:T(8,128)(2,1)S(1)} %collective-permute-done.5, bf16[1024,1280]{1,0:T(8,128)(2,1)} %get-tuple-element.49, bf16[4,1024,1280]{2,1,0:T(8,128)(2,1)} %get-tuple-element.186, s32[]{:T(128)S(6)} %select_n.78), kind=kOutput, calls=%fused_computation.36 | convolution fusion | flops 3360358400 | bytes 11796484 | tf_op jit(solution)/shard_map/nc,nm->cm/dot_general | solution.py:848
  347.7 6.9 add_convert_fusion.5
  354.7 5.1 convolution_convert_fusion.1
  359.7 5.1 convolution_convert_fusion
  366.2 24.4 %fusion.23 = (f32[1280]{0:T(1024)}, f32[1024]{0:T(1024)S(1)}, f32[1024]{0:T(1024)S(1)}, f32[1280]{0:T(1024)}, f32[1024,1280,1]{1,0,2:T(8,128)}) fusion(f32[1024,1280]{1,0:T(8,128)} %copy-done.19, f32[1024]{0:T(1024)S(1)} %add_rsqrt_fusion.2, f32[1024]{0:T(1024)S(1)} %broadcast_multiply_fusion.9, f32[1280]{0:T(1024)S(1)} %get-tuple-element.141, ...), kind=kOutput, calls=%fused_computation.51 | convolution fusion | flops 13433565184 | bytes 34110464 | tf_op jit(solution)/shard_map/tnm,tdm->nd/dot_general | solution.py:868
  390.5 11.7 %multiply_reduce_fusion = (f32[]{:T(128)}, f32[1280]{0:T(1024)}, f32[1280]{0:T(1024)}, f32[1024,1280]{1,0:T(8,128)S(1)}, bf16[1024,1280]{1,0:T(8,128)(2,1)}) fusion(f32[1024,1280]{1,0:T(8,128)} %get-tuple-element.189, bf16[1,16,64,1280]{3,2,1,0:T(8,128)(2,1)S(1)} %copy-done.29, bf16[1,16,64,1280]{3,2,1,0:T(8,128)(2,1)} %param.17, ...), kind=kLoop, calls=%fused_computation.63 | loop fusion | flops 22279680 | bytes 28867588 | tf_op jit(solution)/shard_map/reduce_sum | solution.py:842
  402.5 3.4 copy-done.23
  410.8 3.8 convolution_convert_fusion.7
  416.3 6.7 add_convert_fusion.4
  424.3 6.5 add_convert_fusion.3
  430.8 8.6 %collective-permute-done.10 = bf16[1280,1280]{1,0:T(8,128)(2,1)} collective-permute-done((bf16[1280,1280]{1,0:T(8,128)(2,1)}, bf16[1280,1280]{1,0:T(8,128)(2,1)}, u32[]{:S(2)}, u32[]{:S(2)}) %collective-permute-start.10) | collective-permute-done | bytes 3276832 | tf_op jit(solution)/shard_map/ppermute | solution.py:709
  439.4 4.6 add_convert_fusion.2
  447.0 28.7 %attend_back.2 = (bf16[28,80,960]{2,1,0:T(8,128)(2,1)}, bf16[28,80,960]{2,1,0:T(8,128)(2,1)}, f32[256,384]{1,0:T(8,128)S(1)}) custom-call(s32[1]{0:T(128)} %bitcast.1.shard_ref, bf16[4,28,80,960]{3,2,1,0:T(8,128)(2,1)} %bitcast.253, bf16[16,80,1280]{2,1,0:T(8,128)(2,1)S(1)} %fusion.40.grad_ref, bf16[256,384]{1,0:T(8,128)(2,1)S(1)} %copy-done.6, ...), custom_call_target="tpu_custom_call" | custom-call | flops 60000002048 | bytes 20000000 | tf_op jit(solution)/shard_map/attend_back/pallas_call | solution.py:580
  475.7 11.2 %convolution_convert_fusion.9 = bf16[1280,960]{0,1:T(8,128)(2,1)} fusion(bf16[1280,2240]{1,0:T(8,128)(2,1)} %turn.1, bf16[2240,960]{1,0:T(8,128)(2,1)} %bitcast.226), kind=kOutput, calls=%fused_computation.89 | convolution fusion | flops 5506252800 | bytes 12492800 | tf_op jit(solution)/shard_map/dn,nc->dc/dot_general | solution.py:898
  487.0 3.2 add_convert_fusion.11
  490.1 3.1 add_convert_fusion.10
  493.3 15.8 %collective-permute-done.8 = bf16[1280,1280]{1,0:T(8,128)(2,1)} collective-permute-done((bf16[1280,1280]{1,0:T(8,128)(2,1)}, bf16[1280,1280]{1,0:T(8,128)(2,1)}, u32[]{:S(2)}, u32[]{:S(2)}) %collective-permute-start.8) | collective-permute-done | bytes 3276832 | tf_op jit(solution)/shard_map/ppermute | solution.py:709
  509.0 9.4 %reduce-scatter.6.cloned.1.call-done = bf16[160,1280]{1,0:T(8,128)(2,1)} async-done(((bf16[1280,1280]{1,0:T(8,128)(2,1)}), bf16[160,1280]{1,0:T(8,128)(2,1)}) %reduce-scatter.6.cloned.1.call-update) | async-done | bytes 409616 | tf_op jit(solution)/shard_map/reduce_scatter | solution.py:733
  518.5 5.5 add_convert_fusion.1
  524.0 10.6 %add_convert_fusion.9 = bf16[1280,960]{0,1:T(8,128)(2,1)S(1)} fusion(bf16[1280,960]{0,1:T(8,128)(2,1)} %collective-permute-done.11, bf16[1280,2240]{1,0:T(8,128)(2,1)} %turn.1, bf16[2240,960]{1,0:T(8,128)(2,1)} %bitcast.224), kind=kOutput, calls=%fused_computation.75 | convolution fusion | flops 5508710400 | bytes 14950400 | tf_op jit(solution)/shard_map/dn,nc->dc/dot_general | solution.py:898
  538.0 28.7 %attend_back.3 = (bf16[28,80,960]{2,1,0:T(8,128)(2,1)}, bf16[28,80,960]{2,1,0:T(8,128)(2,1)}, f32[256,384]{1,0:T(8,128)S(1)}) custom-call(s32[1]{0:T(128)} %bitcast.1.shard_ref, bf16[4,28,80,960]{3,2,1,0:T(8,128)(2,1)} %bitcast.254, bf16[16,80,1280]{2,1,0:T(8,128)(2,1)S(1)} %fusion.40.grad_ref, bf16[256,384]{1,0:T(8,128)(2,1)S(1)} %copy-done.6, ...), custom_call_target="tpu_custom_call" | custom-call | flops 60000002048 | bytes 20000000 | tf_op jit(solution)/shard_map/attend_back/pallas_call | solution.py:580
  567.5 11.6 %convolution_convert_fusion.8 = bf16[1280,960]{0,1:T(8,128)(2,1)} fusion(bf16[1280,2240]{1,0:T(8,128)(2,1)} %turn.1, bf16[2240,960]{1,0:T(8,128)(2,1)} %bitcast.232), kind=kOutput, calls=%fused_computation.88 | convolution fusion | flops 5506252800 | bytes 12492800 | tf_op jit(solution)/shard_map/dn,nc->dc/dot_general | solution.py:898
  579.2 35.7 %frame_back.1 = (bf16[28,64,1280]{2,1,0:T(8,128)(2,1)}, f32[4,1,960]{2,1,0:T(1,128)}) custom-call(s32[1]{0:T(128)} %bitcast.1.shard_ref, bf16[2240,960]{1,0:T(8,128)(2,1)} %bitcast.228, bf16[2240,960]{1,0:T(8,128)(2,1)} %bitcast.233, bf16[2240,960]{1,0:T(8,128)(2,1)} %bitcast.225, bf16[2240,960]{1,0:T(8,128)(2,1)} %bitcast.227, ...), custom_call_target="tpu_custom_call" | custom-call | flops 1000000 | bytes 1000000 | tf_op jit(solution)/shard_map/frame_back/pallas_call | solution.py:675
  614.9 3.5 broadcast_in_dim.26
  622.4 8.4 %add_convert_fusion.8 = bf16[1280,960]{0,1:T(8,128)(2,1)S(1)} fusion(bf16[1280,960]{0,1:T(8,128)(2,1)} %collective-permute-done.22, bf16[1280,2240]{1,0:T(8,128)(2,1)S(1)} %bitcast.222, bf16[2240,960]{1,0:T(8,128)(2,1)S(1)} %bitcast.231), kind=kOutput, calls=%fused_computation.74 | convolution fusion | flops 5508710400 | bytes 14950400 | tf_op jit(solution)/shard_map/dn,nc->dc/dot_general | solution.py:898
  630.9 4.7 add_convert_fusion
  635.5 6.2 reduce-scatter.8.cloned.1.call-done
  641.8 5.7 copy.59
  648.0 3.0 slice.146
  662.0 6.9 multiply_reduce_fusion.1
  669.7 14.4 %collective-permute-start.17 = (f32[19681]{0:T(1024)S(1)}, f32[19681]{0:T(1024)S(1)}, u32[]{:S(2)}, u32[]{:S(2)}) collective-permute-start(f32[19681]{0:T(1024)S(1)} %concatenate.47), channel_id=1, source_target_pairs={{0,1},{1,0},{2,3},{3,2},{4,5},{5,4},{6,7},{7,6},{8,9},{9,8},{10,11... | collective-permute-start | bytes 236180 | tf_op jit(solution)/shard_map/ppermute | solution.py:709
  685.0 2.8 collective-permute-start.18
  691.9 4.5 collective-permute-done.19
  697.7 3.2 collective-permute-done.20
  702.8 6.5 fusion.22
  715.4 9.0 %reduce-scatter.10.cloned.1.call-done = bf16[160,1280]{1,0:T(8,128)(2,1)} async-done(((bf16[1280,1280]{1,0:T(8,128)(2,1)}), bf16[160,1280]{1,0:T(8,128)(2,1)}) %reduce-scatter.10.cloned.1.call-update) | async-done | bytes 409616
  (309 shorter events, 81.3 us)
Async XLA Ops:
  7.2 167.0 %all-gather.3.cloned.1.call-start = ((), (), s32[]{:S(2)}) async-start(), calls=%async_computation.3 | async-start | bytes 27033600 | tf_op jit(solution)/shard_map/all_gather | solution.py:795
  11.0 263.2 %all-gather.5.cloned.1.call-start = ((), (), s32[]{:S(2)}) async-start(), calls=%async_computation.4 | async-start | bytes 13516800 | tf_op jit(solution)/shard_map/all_gather | solution.py:823
  12.5 7.9 %collective-permute-start.1 = (bf16[12,64,1280]{2,1,0:T(8,128)(2,1)}, bf16[12,64,1280]{2,1,0:T(8,128)(2,1)}, u32[]{:S(2)}, u32[]{:S(2)}) collective-permute-start(bf16[12,64,1280]{2,1,0:T(8,128)(2,1)} %slice_bitcast_fusion), channel_id=1, source_target_pairs={{1,0},{2,1},{3,2},{5,4},{6,5},{7,6},{9,8},{10,9},{11,10},{13,12},{... | collective-permute-start | bytes 5898248 | tf_op jit(solution)/shard_map/ppermute | solution.py:709
  14.8 5.5 collective-permute-start
  27.8 146.5 %copy-start.50 = (bf16[2,320]{1,0:T(2,128)(2,1)S(1)}, bf16[2,320]{1,0:T(2,128)(2,1)}, u32[]{:S(2)}) copy-start(bf16[2,320]{1,0:T(2,128)(2,1)} %param.23) | copy-start | bytes 3844
  27.8 148.0 %copy-start.49 = (bf16[1280]{0:T(1024)(128)(2,1)S(1)}, bf16[1280]{0:T(1024)(128)(2,1)}, u32[]{:S(2)}) copy-start(bf16[1280]{0:T(1024)(128)(2,1)} %param.24) | copy-start | bytes 7684
  27.8 152.0 %copy-start.38 = (bf16[2,27,80]{2,0,1:T(2,128)(2,1)S(1)}, bf16[2,27,80]{2,0,1:T(2,128)(2,1)}, u32[]{:S(2)}) copy-start(bf16[2,27,80]{2,0,1:T(2,128)(2,1)} %param.28) | copy-start | bytes 25924
  27.8 152.7 %copy-start.42 = (bf16[2,1280]{1,0:T(2,128)(2,1)S(1)}, bf16[2,1280]{1,0:T(2,128)(2,1)}, u32[]{:S(2)}) copy-start(bf16[2,1280]{1,0:T(2,128)(2,1)} %param.27) | copy-start | bytes 15364
  174.2 344.3 %reduce-scatter.6.cloned.1.call-start = ((), (), s32[]{:S(2)}) async-start(), calls=%async_computation.5 | async-start | bytes 3686400 | tf_op jit(solution)/shard_map/reduce_scatter | solution.py:733
  177.1 5.0 collective-permute-start.4
  178.5 4.4 collective-permute-start.3
  179.0 4.5 collective-permute-start.2
  181.3 35.3 %copy-start.5 = (bf16[256,384]{1,0:T(8,128)(2,1)}, bf16[256,384]{1,0:T(8,128)(2,1)S(1)}, u32[]{:S(2)}) copy-start(bf16[256,384]{1,0:T(8,128)(2,1)S(1)} %pad.34.table_ref) | copy-start | bytes 589828
  184.5 32.1 %copy-start.9 = (bf16[4,224,256]{2,1,0:T(8,128)(2,1)S(1)}, bf16[4,224,256]{2,1,0:T(8,128)(2,1)}, u32[]{:S(2)}) copy-start(bf16[4,224,256]{2,1,0:T(8,128)(2,1)} %constant.138.clone.select_ref) | copy-start | bytes 1376260
  216.6 29.0 %copy-start.14 = (bf16[1280,1280]{1,0:T(8,128)(2,1)}, bf16[1280,1280]{1,0:T(8,128)(2,1)S(1)}, u32[]{:S(2)}) copy-start(bf16[1280,1280]{1,0:T(8,128)(2,1)S(1)} %get-tuple-element.47) | copy-start | bytes 9830404
  251.8 108.0 %copy-start.25 = (bf16[1024,1280]{1,0:T(8,128)(2,1)}, bf16[1024,1280]{1,0:T(8,128)(2,1)S(1)}, u32[]{:S(2)}) copy-start(bf16[1024,1280]{1,0:T(8,128)(2,1)S(1)} %add_convert_fusion.7) | copy-start | bytes 7864324
  297.1 16.5 %slice-start.4 = ((s8[13107200]{0:T(1024)(128)(4,1)}), s8[4194304]{0:T(1024)(128)(4,1)S(1)}, s32[]{:S(2)}) async-start(s8[13107200]{0:T(1024)(128)(4,1)} %bitcast.249), calls=%async_computation.12 | async-start | bytes 8388608
  297.1 16.5 %slice-start.5 = ((s8[13107200]{0:T(1024)(128)(4,1)}), s8[4194304]{0:T(1024)(128)(4,1)S(1)}, s32[]{:S(2)}) async-start(s8[13107200]{0:T(1024)(128)(4,1)} %bitcast.249), calls=%async_computation.13 | async-start | bytes 8388608
  305.1 34.6 %collective-permute-start.5 = (bf16[1280,1280]{1,0:T(8,128)(2,1)}, bf16[1280,1280]{1,0:T(8,128)(2,1)S(1)}, u32[]{:S(2)}, u32[]{:S(2)}) collective-permute-start(bf16[1280,1280]{1,0:T(8,128)(2,1)} %convolution_convert_fusion.3), channel_id=1, source_target_pairs={{0,1},{1,0},{2,3},{3,2},{4,5},{5,4},{6,7},{7,6},{8,9},{9,8},{10,11... | collective-permute-start | bytes 9830408 | tf_op jit(solution)/shard_map/ppermute | solution.py:709
  313.4 34.3 %collective-permute-start.6 = (bf16[1280,1280]{1,0:T(8,128)(2,1)}, bf16[1280,1280]{1,0:T(8,128)(2,1)S(1)}, u32[]{:S(2)}, u32[]{:S(2)}) collective-permute-start(bf16[1280,1280]{1,0:T(8,128)(2,1)} %convolution_convert_fusion.2), channel_id=1, source_target_pairs={{0,1},{1,0},{2,3},{3,2},{4,5},{5,4},{6,7},{7,6},{8,9},{9,8},{10,11... | collective-permute-start | bytes 9830408 | tf_op jit(solution)/shard_map/ppermute | solution.py:709
  339.6 15.0 %slice-start.8 = ((s8[10485760]{0:T(1024)(128)(4,1)}), s8[4194304]{0:T(1024)(128)(4,1)S(1)}, s32[]{:S(2)}) async-start(s8[10485760]{0:T(1024)(128)(4,1)} %bitcast.255), calls=%async_computation.16 | async-start | bytes 8388608
  339.6 15.0 %slice-start.9 = ((s8[10485760]{0:T(1024)(128)(4,1)}), s8[4194304]{0:T(1024)(128)(4,1)S(1)}, s32[]{:S(2)}) async-start(s8[10485760]{0:T(1024)(128)(4,1)} %bitcast.255), calls=%async_computation.17 | async-start | bytes 8388608
  364.9 25.7 %copy-start.29 = (bf16[1,16,64,1280]{3,2,1,0:T(8,128)(2,1)S(1)}, bf16[1,16,64,1280]{3,2,1,0:T(8,128)(2,1)}, u32[]{:S(2)}) copy-start(bf16[1,16,64,1280]{3,2,1,0:T(8,128)(2,1)} %param.18) | copy-start | bytes 7864324
  364.9 50.8 %collective-permute-start.7 = (bf16[1280,1280]{1,0:T(8,128)(2,1)}, bf16[1280,1280]{1,0:T(8,128)(2,1)}, u32[]{:S(2)}, u32[]{:S(2)}) collective-permute-start(bf16[1280,1280]{1,0:T(8,128)(2,1)} %convolution_convert_fusion.1), channel_id=1, source_target_pairs={{0,1},{1,0},{2,3},{3,2},{4,5},{5,4},{6,7},{7,6},{8,9},{9,8},{10,11... | collective-permute-start | bytes 9830408 | tf_op jit(solution)/shard_map/ppermute | solution.py:709
  365.2 59.1 %collective-permute-start.9 = (bf16[1280,1280]{1,0:T(8,128)(2,1)}, bf16[1280,1280]{1,0:T(8,128)(2,1)}, u32[]{:S(2)}, u32[]{:S(2)}) collective-permute-start(bf16[1280,1280]{1,0:T(8,128)(2,1)} %convolution_convert_fusion), channel_id=1, source_target_pairs={{0,1},{1,0},{2,3},{3,2},{4,5},{5,4},{6,7},{7,6},{8,9},{9,8},{10,11... | collective-permute-start | bytes 9830408 | tf_op jit(solution)/shard_map/ppermute | solution.py:709
  365.4 74.0 %collective-permute-start.10 = (bf16[1280,1280]{1,0:T(8,128)(2,1)}, bf16[1280,1280]{1,0:T(8,128)(2,1)}, u32[]{:S(2)}, u32[]{:S(2)}) collective-permute-start(bf16[1280,1280]{1,0:T(8,128)(2,1)} %add_convert_fusion.6), channel_id=1, source_target_pairs={{0,2},{2,0},{1,3},{3,1},{4,6},{6,4},{5,7},{7,5},{8,10},{10,8},{9,1... | collective-permute-start | bytes 9830408 | tf_op jit(solution)/shard_map/ppermute | solution.py:709
  408.1 78.8 %collective-permute-start.12 = (bf16[1280,320]{0,1:T(8,128)(2,1)}, bf16[1280,320]{0,1:T(8,128)(2,1)}, u32[]{:S(2)}, u32[]{:S(2)}) collective-permute-start(bf16[1280,320]{0,1:T(8,128)(2,1)} %convolution_convert_fusion.11), channel_id=1, source_target_pairs={{0,1},{1,0},{2,3},{3,2},{4,5},{5,4},{6,7},{7,6},{8,9},{9,8},{10,11... | collective-permute-start | bytes 2457608 | tf_op jit(solution)/shard_map/ppermute | solution.py:709
  410.5 79.6 %collective-permute-start.13 = (bf16[1280,320]{0,1:T(8,128)(2,1)}, bf16[1280,320]{0,1:T(8,128)(2,1)}, u32[]{:S(2)}, u32[]{:S(2)}) collective-permute-start(bf16[1280,320]{0,1:T(8,128)(2,1)} %convolution_convert_fusion.10), channel_id=1, source_target_pairs={{0,1},{1,0},{2,3},{3,2},{4,5},{5,4},{6,7},{7,6},{8,9},{9,8},{10,11... | collective-permute-start | bytes 2457608 | tf_op jit(solution)/shard_map/ppermute | solution.py:709
  423.1 16.4 %copy-start.21 = (bf16[1280,1280]{1,0:T(8,128)(2,1)S(1)}, bf16[1280,1280]{1,0:T(8,128)(2,1)}, u32[]{:S(2)}) copy-start(bf16[1280,1280]{1,0:T(8,128)(2,1)} %add_convert_fusion.5) | copy-start | bytes 9830404
  423.1 86.0 %collective-permute-start.8 = (bf16[1280,1280]{1,0:T(8,128)(2,1)}, bf16[1280,1280]{1,0:T(8,128)(2,1)}, u32[]{:S(2)}, u32[]{:S(2)}) collective-permute-start(bf16[1280,1280]{1,0:T(8,128)(2,1)} %add_convert_fusion.4), channel_id=1, source_target_pairs={{0,2},{2,0},{1,3},{3,1},{4,6},{6,4},{5,7},{7,5},{8,10},{10,8},{9,1... | collective-permute-start | bytes 9830408 | tf_op jit(solution)/shard_map/ppermute | solution.py:709
  430.8 13.3 %copy-start.6 = (bf16[256,384]{1,0:T(8,128)(2,1)S(1)}, bf16[256,384]{1,0:T(8,128)(2,1)}, u32[]{:S(2)}) copy-start(bf16[256,384]{1,0:T(8,128)(2,1)} %copy-done.5) | copy-start | bytes 589828
  444.1 197.7 %reduce-scatter.8.cloned.1.call-start = ((), (), s32[]{:S(2)}) async-start(), calls=%async_computation.6 | async-start | bytes 3686400 | tf_op jit(solution)/shard_map/reduce_scatter | solution.py:733
  486.9 37.0 %collective-permute-start.11 = (bf16[1280,960]{0,1:T(8,128)(2,1)}, bf16[1280,960]{0,1:T(8,128)(2,1)}, u32[]{:S(2)}, u32[]{:S(2)}) collective-permute-start(bf16[1280,960]{0,1:T(8,128)(2,1)} %convolution_convert_fusion.9), channel_id=1, source_target_pairs={{0,1},{1,0},{2,3},{3,2},{4,5},{5,4},{6,7},{7,6},{8,9},{9,8},{10,11... | collective-permute-start | bytes 7372808 | tf_op jit(solution)/shard_map/ppermute | solution.py:709
  536.5 85.1 %collective-permute-start.14 = (bf16[1280,1280]{0,1:T(8,128)(2,1)}, bf16[1280,1280]{0,1:T(8,128)(2,1)}, u32[]{:S(2)}, u32[]{:S(2)}) collective-permute-start(bf16[1280,1280]{0,1:T(8,128)(2,1)} %pad_maximum_fusion), channel_id=1, source_target_pairs={{0,2},{2,0},{1,3},{3,1},{4,6},{6,4},{5,7},{7,5},{8,10},{10,8},{9,1... | collective-permute-start | bytes 9830408 | tf_op jit(solution)/shard_map/ppermute | solution.py:709
  567.5 156.9 %reduce-scatter.10.cloned.1.call-start = ((), (), s32[]{:S(2)}) async-start(), calls=%async_computation.7 | async-start | bytes 3686400
  567.5 54.1 %slice-start.2 = ((s8[4587520]{0:T(1024)(128)(4,1)}), s8[4194304]{0:T(1024)(128)(4,1)S(1)}, s32[]{:S(2)}) async-start(s8[4587520]{0:T(1024)(128)(4,1)} %bitcast.229), calls=%async_computation.10 | async-start | bytes 8388608
  579.2 42.5 %collective-permute-start.22 = (bf16[1280,960]{0,1:T(8,128)(2,1)}, bf16[1280,960]{0,1:T(8,128)(2,1)}, u32[]{:S(2)}, u32[]{:S(2)}) collective-permute-start(bf16[1280,960]{0,1:T(8,128)(2,1)} %convolution_convert_fusion.8), channel_id=1, source_target_pairs={{0,1},{1,0},{2,3},{3,2},{4,5},{5,4},{6,7},{7,6},{8,9},{9,8},{10,11... | collective-permute-start | bytes 7372808 | tf_op jit(solution)/shard_map/ppermute | solution.py:709
  579.2 42.5 %slice-start.3 = ((s8[4587520]{0:T(1024)(128)(4,1)}), s8[393216]{0:T(1024)(128)(4,1)S(1)}, s32[]{:S(2)}) async-start(s8[4587520]{0:T(1024)(128)(4,1)} %bitcast.229), calls=%async_computation.11 | async-start | bytes 786432
  635.5 12.0 %copy-start.17 = (bf16[1,16,64,1280]{3,2,1,0:T(8,128)(2,1)S(1)}, bf16[1,16,64,1280]{3,2,1,0:T(8,128)(2,1)}, u32[]{:S(2)}) copy-start(bf16[1,16,64,1280]{3,2,1,0:T(8,128)(2,1)} %param.16) | copy-start | bytes 7864324
  648.0 14.0 %copy-start.35 = (f32[1280]{0:T(1024)S(1)}, f32[1280]{0:T(1024)}, u32[]{:S(2)}) copy-start(f32[1280]{0:T(1024)} %copy-done.34) | copy-start | bytes 15364
  651.0 11.0 %collective-permute-start.16 = (bf16[12,64,1280]{2,1,0:T(8,128)(2,1)}, bf16[12,64,1280]{2,1,0:T(8,128)(2,1)}, u32[]{:S(2)}, u32[]{:S(2)}) collective-permute-start(bf16[12,64,1280]{2,1,0:T(8,128)(2,1)} %slice.146), channel_id=1, source_target_pairs={{0,1},{1,2},{2,3},{4,5},{5,6},{6,7},{8,9},{9,10},{10,11},{12,13},{... | collective-permute-start | bytes 5898248 | tf_op jit(solution)/shard_map/ppermute | solution.py:709
  656.7 5.3 collective-permute-start.15
  660.7 27.0 %copy-start.33 = (bf16[160,1280]{1,0:T(8,128)(2,1)S(1)}, bf16[160,1280]{1,0:T(8,128)(2,1)}, u32[]{:S(2)}) copy-start(bf16[160,1280]{1,0:T(8,128)(2,1)} %reduce-scatter.6.cloned.1.call-done) | copy-start | bytes 1228804
  669.7 15.3 %collective-permute-start.17 = (f32[19681]{0:T(1024)S(1)}, f32[19681]{0:T(1024)S(1)}, u32[]{:S(2)}, u32[]{:S(2)}) collective-permute-start(f32[19681]{0:T(1024)S(1)} %concatenate.47), channel_id=1, source_target_pairs={{0,1},{1,0},{2,3},{3,2},{4,5},{5,4},{6,7},{7,6},{8,9},{9,8},{10,11... | collective-permute-start | bytes 236180 | tf_op jit(solution)/shard_map/ppermute | solution.py:709
  685.0 5.6 collective-permute-start.18
  690.6 5.9 collective-permute-start.19
  696.4 4.5 collective-permute-start.20
  701.0 8.3 %collective-permute-start.21 = (f32[19681]{0:T(1024)S(1)}, f32[19681]{0:T(1024)S(1)}, u32[]{:S(2)}, u32[]{:S(2)}) collective-permute-start(f32[19681]{0:T(1024)S(1)} %add.311), channel_id=1, source_target_pairs={{0,16},{4,20},{8,24},{12,28},{16,0},{20,4},{24,8},{28,12},{1,17},{... | collective-permute-start | bytes 236180 | tf_op jit(solution)/shard_map/ppermute | solution.py:746
  (47 other events, 290.9 us)
Sparse Core Ops, SparseCore 0:
  11.5 162.6 all-gather.2
  177.0 96.6 all-gather.4
  444.2 74.2 reduce-scatter.5
  567.6 74.1 reduce-scatter.7
  647.6 76.7 reduce-scatter.9
